TPU v7x, 256 devices: a whole 4x4x8 slice. The times are simulated.
256 devices in a mesh: wide: 64 (over z, x, core), narrow: 4 (over y).
Axes of the slice: x: 4, y: 4, z: 8, core: 2. Of those that a mesh axis runs over, the one named last changes fastest.
Arguments:
- snapshots: float32 [128, 4096, 1024], P('wide', None, 'narrow'), may hold values from -384 to 384
- snap_factor: float32 [128, 256], replicated, may hold values from 0 to 1
- row_factor: float32 [1024, 256], P('wide'), may hold values from 0 to 3
- col_factor: float32 [1024, 256], P('narrow'), may hold values from 0 to 3
- row_dual: float32 [1024, 256], P('wide'), may hold values from -0.5 to 0.5
- col_dual: float32 [1024, 256], P('narrow'), may hold values from -0.5 to 0.5
Outputs:
- row_new: float32 [1024, 256], P('wide')
- col_new: float32 [1024, 256], P('narrow')
- row_dual_new: float32 [1024, 256], P('wide')
- col_dual_new: float32 [1024, 256], P('narrow')
All inputs are finite; a program needn't handle non-finite values.
Results may differ from a plain program's by a relative error of at most 0.00018.
Values sent between devices are 32-bit elements; how exact they have to be, the bound alone decides.
No kernel may reach another device: no remote copies, remote signals or barrier semaphores. Data moves between devices by JAX's collectives and lax.ppermute only.
A program may use at most 64 MiB of HBM per device.

v0:
```python
import functools
import math

import jax
import jax.numpy as jnp
import numpy as np
from jax import lax
from jax.experimental import pallas as pl
from jax.experimental.pallas import tpu as pltpu
from jax.sharding import Mesh
from jax.sharding import PartitionSpec as P

ROWS = 4096
KEEP = 1024
RANK = 256
COLS = 256
ADMM_STEPS = 3
PART = ROWS // 4
BAND = KEEP // 4
STEP = 256
NZ, NX, NC, NY = 8, 4, 2, 4
WIDE = ("z", "x", "c")
F32 = jnp.float32
BF16 = jnp.bfloat16
VMEM = pl.BlockSpec(memory_space=pltpu.VMEM)
SMEM = pl.BlockSpec(memory_space=pltpu.SMEM)


def halves(table):
    high = table.astype(np.float32).astype(jnp.bfloat16)
    low = (table - high.astype(np.float64)).astype(np.float32).astype(jnp.bfloat16)
    return high, low


def twiddles():
    odd = 2 * np.arange(PART)[None, :] + 1
    degree = np.arange(BAND)[:, None]
    scale = math.sqrt(2.0 / ROWS)
    plain = scale * np.cos(np.pi * (odd * degree % 4096) / 2048)
    plain[0] = math.sqrt(1.0 / ROWS)
    angle = np.pi * (odd * (2 * degree + 1) % 8192) / 4096
    tables = []
    for table in (plain, scale * np.cos(angle), scale * np.sin(angle)):
        tables.extend(halves(table))
    turn = np.pi * odd.T / 8192
    lanes = np.ones((1, 128))
    return tables, (np.cos(turn) * lanes).astype(np.float32), (np.sin(turn) * lanes).astype(np.float32)


def split(value):
    high = value.astype(BF16)
    return high, (value - high.astype(F32)).astype(BF16)


def dot(a, b):
    return jnp.dot(a, b, preferred_element_type=F32)


def dot3(a, b):
    return dot(a[0], b[0]) + (dot(a[1], b[0]) + dot(a[0], b[1]))


def exact(a, b):
    return jnp.dot(a, b, precision=lax.Precision.HIGHEST, preferred_element_type=F32)


def turned(ref, s):
    index = 7 - lax.broadcasted_iota(jnp.int32, (8, COLS), 0)
    tiles = []
    for t in range(STEP // 8):
        tile = ref[s, STEP - 8 * (t + 1) : STEP - 8 * t, :]
        tiles.append(jnp.take_along_axis(tile, index, axis=0, mode="promise_in_bounds"))
    return jnp.concatenate(tiles, axis=0)


def dct_kernel(x0, x1, x2, x3, cos_ref, sin_ref, ah, al, bh, bl, ch, cl, out):
    @pl.when(pl.program_id(0) == 0)
    def _():
        out[...] = jnp.zeros_like(out)

    plain, even, odd = (ah[...], al[...]), (bh[...], bl[...]), (ch[...], cl[...])
    cos = jnp.concatenate([cos_ref[...]] * 2, axis=1)
    sin = jnp.concatenate([sin_ref[...]] * 2, axis=1)
    for s in range(2):
        first, third = x0[s], x2[s]
        second, fourth = turned(x1, s), turned(x3, s)
        outer, inner = first + fourth, second + third
        v, w = first - fourth, second - third
        out[s, 0] += dot3(plain, split(outer + inner))
        out[s, 2] += dot3(even, split(outer - inner))
        p = dot3(even, split(v * cos - w * sin))
        q = dot3(odd, split(v * sin + w * cos))
        out[s, 1] += p + q
        out[s, 3] += p - q


def dct(snapshots):
    tables, cos, sin = twiddles()
    steps = PART // STEP
    block = (2, STEP, COLS)
    table = pl.BlockSpec((BAND, STEP), lambda i: (0, i))
    turn = pl.BlockSpec((STEP, 128), lambda i: (i, 0))
    return pl.pallas_call(
        dct_kernel,
        grid=(steps,),
        in_specs=[
            pl.BlockSpec(block, lambda i: (0, i, 0)),
            pl.BlockSpec(block, lambda i: (0, 2 * steps - 1 - i, 0)),
            pl.BlockSpec(block, lambda i: (0, 2 * steps + i, 0)),
            pl.BlockSpec(block, lambda i: (0, 4 * steps - 1 - i, 0)),
            turn,
            turn,
        ]
        + [table] * 6,
        out_specs=pl.BlockSpec((2, 4, BAND, COLS), lambda i: (0, 0, 0, 0)),
        out_shape=jax.ShapeDtypeStruct((2, 4, BAND, COLS), F32),
        cost_estimate=pl.CostEstimate(flops=7_000_000_000, bytes_accessed=13_000_000, transcendentals=0),
        name="dct",
    )(*([snapshots] * 4), jnp.asarray(cos), jnp.asarray(sin), *map(jnp.asarray, tables))


def place_rows(where, pieces, rows):
    x, core = where[1], where[2]
    for side in range(NC):
        for shift in range(NX):
            source = lax.rem(x - shift + NX, NX)
            owner = core if side == 0 else 1 - core
            for z in range(NZ):
                start = pl.multiple_of(z * 128 + source * 32 + owner * 16, 16)
                block = pieces[side * NX + shift][z]
                for half in range(2):
                    rows[half, pl.ds(start, 16), :] = block[:, 128 * half : 128 * half + 128]


def totals_kernel(where, comp, snap, *refs):
    pieces, (keep, send), (rows, total) = refs[:8], refs[8:10], refs[10:]
    place_rows(where, pieces, rows)
    z, x, core = where[0], where[1], where[2]
    wide = (z * NX + x) * NC + core
    sums = [None, None]
    for k in range(4):
        line = [rows[half, pl.ds(k, BAND, stride=4), :] for half in range(2)]
        lines = split(jnp.concatenate(line, axis=1).T)
        for s in range(2):
            term = dot3(lines, split(comp[s, k]))
            sums[s] = term if sums[s] is None else sums[s] + term
    total[...] = sum(sums[s].T * snap[pl.ds(2 * wide + s, 1), :] for s in range(2))
    for shift in range(NX):
        target = lax.rem(x + shift, NX)
        for ref, owner in ((keep, core), (send, 1 - core)):
            start = pl.multiple_of(owner * 128 + target * 32, 32)
            ref[shift] = total[pl.ds(start, 32), :]


def totals(where, comp, snap, pieces):
    part = jax.ShapeDtypeStruct((NX, 32, RANK), F32)
    return pl.pallas_call(
        totals_kernel,
        in_specs=[SMEM] + [VMEM] * 10,
        out_specs=[VMEM] * 2,
        out_shape=[part] * 2,
        scratch_shapes=[pltpu.VMEM((2, KEEP, 128), F32), pltpu.VMEM((COLS, RANK), F32)],
        cost_estimate=pl.CostEstimate(flops=800_000_000, bytes_accessed=4_000_000, transcendentals=0),
        name="totals",
    )(where, comp, snap, *pieces)


def inverse(gram):
    eye = (
        lax.broadcasted_iota(jnp.int32, (RANK, RANK), 0)
        == lax.broadcasted_iota(jnp.int32, (RANK, RANK), 1)
    ).astype(F32)
    penalty = jnp.sum(gram * eye) / RANK
    system = gram / penalty + eye
    middle = 2.0 / (1.0 + 257.0)
    rest = eye - middle * system
    reach = 258.0 / 256.0
    found = middle * eye
    for step in range(6):
        doubled = 2.0 * reach * reach - 1.0
        gain = 2.0 * reach * reach / doubled
        if step == 0:
            found = (gain * middle) * (eye + rest)
        else:
            found = gain * (found + exact(found, rest))
        if step < 5:
            rest = gain * exact(rest, rest) - (1.0 / doubled) * eye
        reach = doubled
    found = found + exact(found, eye - exact(system, found))
    return found / penalty, penalty


def col_system_kernel(where, snap, *refs):
    pieces, (inv, pen), (rows,) = refs[:8], refs[8:10], refs[10:]
    place_rows(where, pieces, rows)
    snaps, lines = snap[...], jnp.concatenate([rows[0], rows[1]], axis=1)
    gram = exact(snaps.T, snaps) * exact(lines.T, lines)
    found, penalty = inverse(gram)
    inv[...] = found
    pen[...] = jnp.full((8, 128), penalty, F32)


def row_system_kernel(where, snap, mine, other, inv, pen, gram):
    core = where[2]
    gram[pl.ds(pl.multiple_of(core * 128, 128), 128), :] = mine[...]
    gram[pl.ds(pl.multiple_of((1 - core) * 128, 128), 128), :] = other[...]
    snaps = snap[...]
    found, penalty = inverse(exact(snaps.T, snaps) * gram[...])
    inv[...] = found
    pen[...] = jnp.full((8, 128), penalty, F32)


def system(kernel, where, snap, parts, scratch, name):
    return pl.pallas_call(
        kernel,
        in_specs=[SMEM] + [VMEM] * (1 + len(parts)),
        out_specs=[VMEM] * 2,
        out_shape=[
            jax.ShapeDtypeStruct((RANK, RANK), F32),
            jax.ShapeDtypeStruct((8, 128), F32),
        ],
        scratch_shapes=[scratch],
        cost_estimate=pl.CostEstimate(flops=3_000_000_000, bytes_accessed=1_000_000, transcendentals=0),
        name=name,
    )(where, snap, *parts)


def admm_update(sums, inv, penalty, primal, multiplier):
    for _ in range(ADMM_STEPS):
        solved = exact(sums + penalty * (primal + multiplier), inv)
        primal = jnp.maximum(solved - multiplier, 0.0)
        multiplier = multiplier + primal - solved
    return primal, multiplier


def col_kernel(where, comp, snap, inv, pen, factor, dual, *refs):
    pieces = refs[:8]
    new, dual_new, keep, send, gram_half = refs[8:13]
    total, mapped, gram = refs[13:]
    z, x, core = where[0], where[1], where[2]
    wide = (z * NX + x) * NC + core
    for side in range(NC):
        for shift in range(NX):
            source = lax.rem(x - shift + NX, NX)
            owner = core if side == 0 else 1 - core
            start = pl.multiple_of(owner * 128 + source * 32, 32)
            total[pl.ds(start, 32), :] = pieces[side * NX + shift][...]
    primal, multiplier = admm_update(total[...], inv[...], pen[0, 0], factor[...], dual[...])
    new[...] = primal
    dual_new[...] = multiplier
    gram[...] = exact(primal.T, primal)
    gram_half[...] = gram[pl.ds(pl.multiple_of(core * 128, 128), 128), :]
    weights = split(primal)
    for k in range(4):
        line = sum(
            dot3(split(comp[s, k]), weights) * snap[pl.ds(2 * wide + s, 1), :] for s in range(2)
        )
        for half in range(2):
            mapped[half, pl.ds(k, BAND, stride=4), :] = line[:, 128 * half : 128 * half + 128]
    for shift in range(NX):
        target = lax.rem(x + shift, NX)
        for ref, owner in ((keep, core), (send, 1 - core)):
            for line in range(NZ):
                start = pl.multiple_of(line * 128 + target * 32 + owner * 16, 16)
                for half in range(2):
                    ref[shift, line, :, 128 * half : 128 * half + 128] = mapped[half, pl.ds(start, 16), :]


def col_update(where, comp, snap, inv, pen, factor, dual, pieces):
    square = jax.ShapeDtypeStruct((COLS, RANK), F32)
    part = jax.ShapeDtypeStruct((NX, NZ, 16, RANK), F32)
    return pl.pallas_call(
        col_kernel,
        in_specs=[SMEM] + [VMEM] * 3 + [VMEM] * 11,
        out_specs=[VMEM] * 5,
        out_shape=[square, square, part, part, jax.ShapeDtypeStruct((128, RANK), F32)],
        scratch_shapes=[
            pltpu.VMEM((COLS, RANK), F32),
            pltpu.VMEM((2, KEEP, 128), F32),
            pltpu.VMEM((RANK, RANK), F32),
        ],
        cost_estimate=pl.CostEstimate(flops=1_500_000_000, bytes_accessed=5_000_000, transcendentals=0),
        name="col_update",
    )(where, comp, snap, inv, pen, factor, dual, *pieces)


def in_order(where, parts, held):
    y = where[3]
    for shift in range(NY):
        held[lax.rem(y - shift + NY, NY)] = parts[shift][...]
    return (held[0] + held[1]) + (held[2] + held[3])


def sum_kernel(where, *refs):
    parts, out, held = refs[:4], refs[4], refs[5]
    out[...] = in_order(where, parts, held)


def ordered_sum(where, parts):
    shape = parts[0].shape
    return pl.pallas_call(
        sum_kernel,
        in_specs=[SMEM] + [VMEM] * 4,
        out_specs=VMEM,
        out_shape=jax.ShapeDtypeStruct(shape, F32),
        scratch_shapes=[pltpu.VMEM((NY, *shape), F32)],
        name="ordered_sum",
    )(where, *parts)


def row_kernel(where, inv, pen, factor, dual, *refs):
    parts, (new, dual_new), held = refs[:4], refs[4:6], refs[6]
    sums = in_order(where, parts, held)
    primal, multiplier = admm_update(sums, inv[...], pen[0, 0], factor[...], dual[...])
    new[...] = primal
    dual_new[...] = multiplier


def row_update(where, inv, pen, factor, dual, parts):
    own = jax.ShapeDtypeStruct((16, RANK), F32)
    return pl.pallas_call(
        row_kernel,
        in_specs=[SMEM] + [VMEM] * 8,
        out_specs=[VMEM] * 2,
        out_shape=[own] * 2,
        scratch_shapes=[pltpu.VMEM((NY, 16, RANK), F32)],
        name="row_update",
    )(where, inv, pen, factor, dual, *parts)


def shifted(array, axis, size, by):
    return lax.ppermute(array, axis, [(i, (i + by) % size) for i in range(size)])


def from_all(array, axis, size):
    return [array] + [shifted(array, axis, size, by) for by in range(1, size)]


def copied_along_z(array):
    whole = jnp.broadcast_to(array[None], (NZ, *array.shape))
    return lax.all_to_all(whole, "z", 0, 0, tiled=True)


def body(snapshots, snap_factor, row_factor, col_factor, row_dual, col_dual):
    where = jnp.stack([lax.axis_index(name) for name in ("z", "x", "c", "y")]).astype(jnp.int32)
    lines = from_all(copied_along_z(row_factor), "x", NX)
    lines = lines + [shifted(line, "c", NC, 1) for line in lines]
    comp = dct(snapshots)
    keep, send = totals(where, comp, snap_factor, lines)
    inv, pen = system(
        col_system_kernel, where, snap_factor, lines, pltpu.VMEM((2, KEEP, 128), F32), "col_system"
    )
    half = keep + shifted(send, "c", NC, 1)
    chunk = half[0] + sum(shifted(half[by], "x", NX, by) for by in range(1, NX))
    chunk = copied_along_z(chunk).sum(axis=0)
    pieces = from_all(chunk, "x", NX)
    pieces = pieces + [shifted(piece, "c", NC, 1) for piece in pieces]
    col_new, col_dual_new, keep, send, gram_half = col_update(
        where, comp, snap_factor, inv, pen, col_factor, col_dual, pieces
    )
    gram_mine = ordered_sum(where, from_all(gram_half, "y", NY))
    gram_other = shifted(gram_mine, "c", NC, 1)
    inv, pen = system(
        row_system_kernel, where, snap_factor, [gram_mine, gram_other], pltpu.VMEM((RANK, RANK), F32), "row_system"
    )
    half = keep + shifted(send, "c", NC, 1)
    block = half[0] + sum(shifted(half[by], "x", NX, by) for by in range(1, NX))
    mine = lax.all_to_all(block, "z", 0, 0, tiled=True).sum(axis=0)
    row_new, row_dual_new = row_update(
        where, inv, pen, row_factor, row_dual, from_all(mine, "y", NY)
    )
    return row_new, col_new, row_dual_new, col_dual_new


def solution(mesh):
    fine = Mesh(mesh.devices.reshape(NZ, NX, NC, NY), ("z", "x", "c", "y"))
    return jax.shard_map(
        body,
        mesh=fine,
        in_specs=(
            P(WIDE, None, "y"),
            P(),
            P(WIDE, None),
            P("y", None),
            P(WIDE, None),
            P("y", None),
        ),
        out_specs=(P(WIDE, None), P("y", None), P(WIDE, None), P("y", None)),
        check_vma=False,
    )
```

profile of v0, /device:TPU:8, one launch (start us, length us, event | category | flops | bytes accessed | tf_op | source)
XLA Modules:
  0.0 132.8 jit_solution(17040392404500393470)
XLA Ops:
  1.4 17.4 %all_to_all.15.refs_0_ = f32[8,16,256]{2,1,0:T(8,128)S(1)} all-to-all(f32[8,16,256]{2,1,0:T(8,128)S(1)} %broadcast_in_dim.4), channel_id=1, replica_groups=mesh['z'=8,'x'=4,'c'=2,'y'=4] {'z'}, dimensions={0} | all-to-all | bytes 262144 | tf_op jit(solution)/shard_map/all_to_all | solution.py:341
  18.7 2.8 %collective-permute-start.2 = (f32[8,16,256]{2,1,0:T(8,128)S(1)}, f32[8,16,256]{2,1,0:T(8,128)S(1)}, u32[]{:S(2)}, u32[]{:S(2)}) collective-permute-start(f32[8,16,256]{2,1,0:T(8,128)S(1)} %all_to_all.15.refs_0_), channel_id=1, source_target_pairs={{0,24},{8,0},{16,8},{24,16},{1,25},{9,1},{17,9},{25,17},{2,26},{10... | collective-permute-start | bytes 393224 | tf_op jit(solution)/shard_map/ppermute | solution.py:332
  23.2 2.4 %collective-permute-done.2.refs_3_ = f32[8,16,256]{2,1,0:T(8,128)S(1)} collective-permute-done((f32[8,16,256]{2,1,0:T(8,128)S(1)}, f32[8,16,256]{2,1,0:T(8,128)S(1)}, u32[]{:S(2)}, u32[]{:S(2)}) %collective-permute-start.2) | collective-permute-done | bytes 131104 | tf_op jit(solution)/shard_map/ppermute | solution.py:332
  25.5 2.5 %collective-permute-done.1.refs_2_ = f32[8,16,256]{2,1,0:T(8,128)S(1)} collective-permute-done((f32[8,16,256]{2,1,0:T(8,128)S(1)}, f32[8,16,256]{2,1,0:T(8,128)S(1)}, u32[]{:S(2)}, u32[]{:S(2)}) %collective-permute-start.1) | collective-permute-done | bytes 131104 | tf_op jit(solution)/shard_map/ppermute | solution.py:332
  29.4 8.8 %dct.1.comp = f32[2,4,256,256]{3,2,1,0:T(8,128)} custom-call(f32[2,4096,256]{2,1,0:T(8,128)} %x3.1, f32[2,4096,256]{2,1,0:T(8,128)} %x3.1, f32[2,4096,256]{2,1,0:T(8,128)} %x3.1, f32[2,4096,256]{2,1,0:T(8,128)} %x3.1, f32[1024,128]{1,0:T(8,128)} %constant.35.clone.cos_ref, f32[1024,128]{1,0:T(8,128)} %constant.36.clone.sin_ref, ...), custom_call_target="tpu_custom_call" | custom-call | flops 7000000000 | bytes 13000000 | tf_op jit(solution)/shard_map/dct/pallas_call | solution.py:103
  40.3 3.9 %totals.1 = (f32[4,32,256]{2,1,0:T(8,128)}, f32[4,32,256]{2,1,0:T(8,128)}) custom-call(s32[4]{0:T(128)} %pad_add_fusion.where, f32[2,4,256,256]{3,2,1,0:T(8,128)} %dct.1.comp, f32[128,256]{1,0:T(8,128)} %snap.7, f32[8,16,256]{2,1,0:T(8,128)} %copy-done, f32[8,16,256]{2,1,0:T(8,128)} %copy-done.3, f32[8,16,256]{2,1,0:T(8,128)} %copy-done.2, ...), custom_call_target="tpu_custom_call" | custom-call | flops 800000000 | bytes 4000000 | tf_op jit(solution)/shard_map/totals/pallas_call | solution.py:157
  49.8 2.6 %collective-permute-done.9 = f32[32,256]{1,0:T(8,128)S(1)} collective-permute-done((f32[32,256]{1,0:T(8,128)S(1)}, f32[32,256]{1,0:T(8,128)S(1)}, u32[]{:S(2)}, u32[]{:S(2)}) %collective-permute-start.9) | collective-permute-done | bytes 32800 | tf_op jit(solution)/shard_map/ppermute | solution.py:332
  52.4 1.7 %collective-permute-done.8 = f32[32,256]{1,0:T(8,128)S(1)} collective-permute-done((f32[32,256]{1,0:T(8,128)S(1)}, f32[32,256]{1,0:T(8,128)S(1)}, u32[]{:S(2)}, u32[]{:S(2)}) %collective-permute-start.8) | collective-permute-done | bytes 32800 | tf_op jit(solution)/shard_map/ppermute | solution.py:332
  54.1 13.4 %all_to_all.16 = f32[8,32,256]{2,1,0:T(8,128)S(1)} all-to-all(f32[8,32,256]{2,1,0:T(8,128)S(1)} %broadcast_in_dim.5), channel_id=1, replica_groups=mesh['z'=8,'x'=4,'c'=2,'y'=4] {'z'}, dimensions={0} | all-to-all | bytes 524288 | tf_op jit(solution)/shard_map/all_to_all | solution.py:341
  69.8 1.7 %collective-permute-done.13.refs_3_ = f32[32,256]{1,0:T(8,128)S(1)} collective-permute-done((f32[32,256]{1,0:T(8,128)S(1)}, f32[32,256]{1,0:T(8,128)S(1)}, u32[]{:S(2)}, u32[]{:S(2)}) %collective-permute-start.13) | collective-permute-done | bytes 32800 | tf_op jit(solution)/shard_map/ppermute | solution.py:332
  71.5 2.7 %collective-permute-done.12.refs_2_ = f32[32,256]{1,0:T(8,128)S(1)} collective-permute-done((f32[32,256]{1,0:T(8,128)S(1)}, f32[32,256]{1,0:T(8,128)S(1)}, u32[]{:S(2)}, u32[]{:S(2)}) %collective-permute-start.12) | collective-permute-done | bytes 32800 | tf_op jit(solution)/shard_map/ppermute | solution.py:332
  74.7 9.2 %col_system.1 = (f32[256,256]{1,0:T(8,128)}, f32[8,128]{1,0:T(8,128)}) custom-call(s32[4]{0:T(128)} %pad_add_fusion.where, f32[128,256]{1,0:T(8,128)} %snap.7, f32[8,16,256]{2,1,0:T(8,128)} %copy-done, f32[8,16,256]{2,1,0:T(8,128)} %copy-done.3, f32[8,16,256]{2,1,0:T(8,128)} %copy-done.2, f32[8,16,256]{2,1,0:T(8,128)} %copy-done.1, f32[8,16,256]{2,1,0:T(8,128)} %copy-done.4, ...), custom_call_target="tpu_custom_call" | custom-call | flops 3000000000 | bytes 1000000 | tf_op jit(solution)/shard_map/col_system/pallas_call | solution.py:214
  84.6 6.0 %col_update.1 = (f32[256,256]{1,0:T(8,128)}, f32[256,256]{1,0:T(8,128)}, f32[4,8,16,256]{3,2,1,0:T(8,128)}, f32[4,8,16,256]{3,2,1,0:T(8,128)}, f32[128,256]{1,0:T(8,128)}) custom-call(s32[4]{0:T(128)} %pad_add_fusion.where, f32[2,4,256,256]{3,2,1,0:T(8,128)} %dct.1.comp, f32[128,256]{1,0:T(8,128)} %snap.7, f32[256,256]{1,0:T(8,128)} %get-tuple-element.17.inv, ...), custom_call_target="tpu_custom_call" | custom-call | flops 1500000000 | bytes 5000000 | tf_op jit(solution)/shard_map/col_update/pallas_call | solution.py:272
  90.9 1.8 %collective-permute-done.22 = f32[4,8,16,256]{3,2,1,0:T(8,128)S(1)} collective-permute-done((f32[4,8,16,256]{3,2,1,0:T(8,128)}, f32[4,8,16,256]{3,2,1,0:T(8,128)S(1)}, u32[]{:S(2)}, u32[]{:S(2)}) %collective-permute-start.22) | collective-permute-done | bytes 524320 | tf_op jit(solution)/shard_map/ppermute | solution.py:332
  93.9 1.7 %collective-permute-start.24 = (f32[8,16,256]{2,1,0:T(8,128)S(1)}, f32[8,16,256]{2,1,0:T(8,128)S(1)}, u32[]{:S(2)}, u32[]{:S(2)}) collective-permute-start(f32[8,16,256]{2,1,0:T(8,128)S(1)} %get-tuple-element.30), channel_id=1, source_target_pairs={{0,16},{8,24},{16,0},{24,8},{1,17},{9,25},{17,1},{25,9},{2,18},{10... | collective-permute-start | bytes 393224 | tf_op jit(solution)/shard_map/ppermute | solution.py:332
  95.6 1.8 %collective-permute-start.25 = (f32[8,16,256]{2,1,0:T(8,128)S(1)}, f32[8,16,256]{2,1,0:T(8,128)S(1)}, u32[]{:S(2)}, u32[]{:S(2)}) collective-permute-start(f32[8,16,256]{2,1,0:T(8,128)S(1)} %get-tuple-element.31), channel_id=1, source_target_pairs={{0,24},{8,0},{16,8},{24,16},{1,25},{9,1},{17,9},{25,17},{2,26},{10... | collective-permute-start | bytes 393224 | tf_op jit(solution)/shard_map/ppermute | solution.py:332
  98.1 2.6 %collective-permute-start.19 = (f32[128,256]{1,0:T(8,128)}, f32[128,256]{1,0:T(8,128)S(1)}, u32[]{:S(2)}, u32[]{:S(2)}) collective-permute-start(f32[128,256]{1,0:T(8,128)} %get-tuple-element.21.refs_0_), channel_id=1, source_target_pairs={{0,2},{1,3},{2,0},{3,1},{4,6},{5,7},{6,4},{7,5},{8,10},{9,11},{10,... | collective-permute-start | bytes 393224 | tf_op jit(solution)/shard_map/ppermute | solution.py:332
  104.8 3.4 %all-to-all-start.2 = ((f32[8,16,256]{2,1,0:T(8,128)}), f32[8,16,256]{2,1,0:T(8,128)S(1)}, u32[]{:S(2)}, u32[]{:S(2)}) async-start(f32[8,16,256]{2,1,0:T(8,128)} %fusion), calls=%async_computation.2 | async-start | bytes 262144 | tf_op jit(solution)/shard_map/all_to_all | solution.py:368
  109.6 1.8 %ordered_sum.1.mine = f32[128,256]{1,0:T(8,128)} custom-call(s32[4]{0:T(128)} %pad_add_fusion.where, f32[128,256]{1,0:T(8,128)} %get-tuple-element.21.refs_0_, f32[128,256]{1,0:T(8,128)} %copy-done.10, f32[128,256]{1,0:T(8,128)} %copy-done.9, f32[128,256]{1,0:T(8,128)} %copy-done.8), custom_call_target="tpu_custom_call" | custom-call | tf_op jit(solution)/shard_map/ordered_sum/pallas_call | solution.py:301
  111.4 5.8 %all-to-all-done.2 = f32[8,16,256]{2,1,0:T(8,128)S(1)} async-done(((f32[8,16,256]{2,1,0:T(8,128)}), f32[8,16,256]{2,1,0:T(8,128)S(1)}, u32[]{:S(2)}, u32[]{:S(2)}) %all-to-all-start.2) | async-done | bytes 131104 | tf_op jit(solution)/shard_map/all_to_all | solution.py:368
  117.8 2.6 %collective-permute-start.27 = (f32[16,256]{1,0:T(8,128)S(1)}, f32[16,256]{1,0:T(8,128)S(1)}, u32[]{:S(2)}, u32[]{:S(2)}) collective-permute-start(f32[16,256]{1,0:T(8,128)S(1)} %reduce_sum.19.refs_0_), channel_id=1, source_target_pairs={{0,2},{1,3},{2,0},{3,1},{4,6},{5,7},{6,4},{7,5},{8,10},{9,11},{10,... | collective-permute-start | bytes 49160 | tf_op jit(solution)/shard_map/ppermute | solution.py:332
  120.4 1.9 %collective-permute-start.26 = (f32[16,256]{1,0:T(8,128)S(1)}, f32[16,256]{1,0:T(8,128)S(1)}, u32[]{:S(2)}, u32[]{:S(2)}) collective-permute-start(f32[16,256]{1,0:T(8,128)S(1)} %reduce_sum.19.refs_0_), channel_id=1, source_target_pairs={{0,1},{1,2},{2,3},{3,0},{4,5},{5,6},{6,7},{7,4},{8,9},{9,10},{10,1... | collective-permute-start | bytes 49160 | tf_op jit(solution)/shard_map/ppermute | solution.py:332
  122.9 6.8 %row_system.1 = (f32[256,256]{1,0:T(8,128)}, f32[8,128]{1,0:T(8,128)}) custom-call(s32[4]{0:T(128)} %pad_add_fusion.where, f32[128,256]{1,0:T(8,128)} %snap.7, f32[128,256]{1,0:T(8,128)} %ordered_sum.1.mine, f32[128,256]{1,0:T(8,128)} %copy-done.16), custom_call_target="tpu_custom_call" | custom-call | flops 3000000000 | bytes 1000000 | tf_op jit(solution)/shard_map/row_system/pallas_call | solution.py:214
  130.4 2.5 %row_update.1 = (f32[16,256]{1,0:T(8,128)}, f32[16,256]{1,0:T(8,128)}) custom-call(s32[4]{0:T(128)} %pad_add_fusion.where, f32[256,256]{1,0:T(8,128)} %get-tuple-element.22.inv, f32[8,128]{1,0:T(8,128)} %get-tuple-element.23.pen, f32[16,256]{1,0:T(8,128)} %factor.3, f32[16,256]{1,0:T(8,128)} %dual.3, f32[16,256]{1,0:T(8,128)} %copy-done.11, ...), custom_call_target="tpu_custom_call" | custom-call | tf_op jit(solution)/shard_map/row_update/pallas_call | solution.py:321
  (104 shorter events, 24.2 us)
Async XLA Ops:
  18.7 6.8 %collective-permute-start.2 = (f32[8,16,256]{2,1,0:T(8,128)S(1)}, f32[8,16,256]{2,1,0:T(8,128)S(1)}, u32[]{:S(2)}, u32[]{:S(2)}) collective-permute-start(f32[8,16,256]{2,1,0:T(8,128)S(1)} %all_to_all.15.refs_0_), channel_id=1, source_target_pairs={{0,24},{8,0},{16,8},{24,16},{1,25},{9,1},{17,9},{25,17},{2,26},{10... | collective-permute-start | bytes 393224 | tf_op jit(solution)/shard_map/ppermute | solution.py:332
  21.5 6.6 %collective-permute-start.1 = (f32[8,16,256]{2,1,0:T(8,128)S(1)}, f32[8,16,256]{2,1,0:T(8,128)S(1)}, u32[]{:S(2)}, u32[]{:S(2)}) collective-permute-start(f32[8,16,256]{2,1,0:T(8,128)S(1)} %all_to_all.15.refs_0_), channel_id=1, source_target_pairs={{0,16},{8,24},{16,0},{24,8},{1,17},{9,25},{17,1},{25,9},{2,18},{10... | collective-permute-start | bytes 393224 | tf_op jit(solution)/shard_map/ppermute | solution.py:332
  22.3 7.1 %collective-permute-start = (f32[8,16,256]{2,1,0:T(8,128)S(1)}, f32[8,16,256]{2,1,0:T(8,128)S(1)}, u32[]{:S(2)}, u32[]{:S(2)}) collective-permute-start(f32[8,16,256]{2,1,0:T(8,128)S(1)} %all_to_all.15.refs_0_), channel_id=1, source_target_pairs={{0,8},{8,16},{16,24},{24,0},{1,9},{9,17},{17,25},{25,1},{2,10},{10... | collective-permute-start | bytes 393224 | tf_op jit(solution)/shard_map/ppermute | solution.py:332
  23.2 15.7 %collective-permute-start.3 = (f32[8,16,256]{2,1,0:T(8,128)S(1)}, f32[8,16,256]{2,1,0:T(8,128)S(1)}, u32[]{:S(2)}, u32[]{:S(2)}) collective-permute-start(f32[8,16,256]{2,1,0:T(8,128)S(1)} %all_to_all.15.refs_0_), channel_id=1, source_target_pairs={{0,4},{4,0},{1,5},{5,1},{2,6},{6,2},{3,7},{7,3},{8,12},{12,8},{9,1... | collective-permute-start | bytes 393224 | tf_op jit(solution)/shard_map/ppermute | solution.py:332
  25.5 13.3 %collective-permute-start.6 = (f32[8,16,256]{2,1,0:T(8,128)S(1)}, f32[8,16,256]{2,1,0:T(8,128)S(1)}, u32[]{:S(2)}, u32[]{:S(2)}) collective-permute-start(f32[8,16,256]{2,1,0:T(8,128)S(1)} %collective-permute-done.2.refs_3_), channel_id=1, source_target_pairs={{0,4},{4,0},{1,5},{5,1},{2,6},{6,2},{3,7},{7,3},{8,12},{12,8},{9,1... | collective-permute-start | bytes 393224 | tf_op jit(solution)/shard_map/ppermute | solution.py:332
  28.0 10.9 %collective-permute-start.5 = (f32[8,16,256]{2,1,0:T(8,128)S(1)}, f32[8,16,256]{2,1,0:T(8,128)S(1)}, u32[]{:S(2)}, u32[]{:S(2)}) collective-permute-start(f32[8,16,256]{2,1,0:T(8,128)S(1)} %collective-permute-done.1.refs_2_), channel_id=1, source_target_pairs={{0,4},{4,0},{1,5},{5,1},{2,6},{6,2},{3,7},{7,3},{8,12},{12,8},{9,1... | collective-permute-start | bytes 393224 | tf_op jit(solution)/shard_map/ppermute | solution.py:332
  29.4 9.6 %collective-permute-start.4 = (f32[8,16,256]{2,1,0:T(8,128)S(1)}, f32[8,16,256]{2,1,0:T(8,128)S(1)}, u32[]{:S(2)}, u32[]{:S(2)}) collective-permute-start(f32[8,16,256]{2,1,0:T(8,128)S(1)} %collective-permute-done.refs_1_), channel_id=1, source_target_pairs={{0,4},{4,0},{1,5},{5,1},{2,6},{6,2},{3,7},{7,3},{8,12},{12,8},{9,1... | collective-permute-start | bytes 393224 | tf_op jit(solution)/shard_map/ppermute | solution.py:332
  46.9 5.5 %collective-permute-start.9 = (f32[32,256]{1,0:T(8,128)S(1)}, f32[32,256]{1,0:T(8,128)S(1)}, u32[]{:S(2)}, u32[]{:S(2)}) collective-permute-start(f32[32,256]{1,0:T(8,128)S(1)} %get-tuple-element.33), channel_id=1, source_target_pairs={{0,16},{8,24},{16,0},{24,8},{1,17},{9,25},{17,1},{25,9},{2,18},{10... | collective-permute-start | bytes 98312 | tf_op jit(solution)/shard_map/ppermute | solution.py:332
  68.8 5.4 %collective-permute-start.12 = (f32[32,256]{1,0:T(8,128)S(1)}, f32[32,256]{1,0:T(8,128)S(1)}, u32[]{:S(2)}, u32[]{:S(2)}) collective-permute-start(f32[32,256]{1,0:T(8,128)S(1)} %reduce_sum.18.refs_0_), channel_id=1, source_target_pairs={{0,16},{8,24},{16,0},{24,8},{1,17},{9,25},{17,1},{25,9},{2,18},{10... | collective-permute-start | bytes 98312 | tf_op jit(solution)/shard_map/ppermute | solution.py:332
  69.8 14.2 %collective-permute-start.14 = (f32[32,256]{1,0:T(8,128)S(1)}, f32[32,256]{1,0:T(8,128)S(1)}, u32[]{:S(2)}, u32[]{:S(2)}) collective-permute-start(f32[32,256]{1,0:T(8,128)S(1)} %reduce_sum.18.refs_0_), channel_id=1, source_target_pairs={{0,4},{4,0},{1,5},{5,1},{2,6},{6,2},{3,7},{7,3},{8,12},{12,8},{9,1... | collective-permute-start | bytes 98312 | tf_op jit(solution)/shard_map/ppermute | solution.py:332
  71.5 12.4 %collective-permute-start.17 = (f32[32,256]{1,0:T(8,128)S(1)}, f32[32,256]{1,0:T(8,128)S(1)}, u32[]{:S(2)}, u32[]{:S(2)}) collective-permute-start(f32[32,256]{1,0:T(8,128)S(1)} %collective-permute-done.13.refs_3_), channel_id=1, source_target_pairs={{0,4},{4,0},{1,5},{5,1},{2,6},{6,2},{3,7},{7,3},{8,12},{12,8},{9,1... | collective-permute-start | bytes 98312 | tf_op jit(solution)/shard_map/ppermute | solution.py:332
  74.2 9.7 %collective-permute-start.16 = (f32[32,256]{1,0:T(8,128)S(1)}, f32[32,256]{1,0:T(8,128)S(1)}, u32[]{:S(2)}, u32[]{:S(2)}) collective-permute-start(f32[32,256]{1,0:T(8,128)S(1)} %collective-permute-done.12.refs_2_), channel_id=1, source_target_pairs={{0,4},{4,0},{1,5},{5,1},{2,6},{6,2},{3,7},{7,3},{8,12},{12,8},{9,1... | collective-permute-start | bytes 98312 | tf_op jit(solution)/shard_map/ppermute | solution.py:332
  74.6 9.4 %collective-permute-start.15 = (f32[32,256]{1,0:T(8,128)S(1)}, f32[32,256]{1,0:T(8,128)S(1)}, u32[]{:S(2)}, u32[]{:S(2)}) collective-permute-start(f32[32,256]{1,0:T(8,128)S(1)} %collective-permute-done.11.refs_1_), channel_id=1, source_target_pairs={{0,4},{4,0},{1,5},{5,1},{2,6},{6,2},{3,7},{7,3},{8,12},{12,8},{9,1... | collective-permute-start | bytes 98312 | tf_op jit(solution)/shard_map/ppermute | solution.py:332
  93.9 8.0 %collective-permute-start.24 = (f32[8,16,256]{2,1,0:T(8,128)S(1)}, f32[8,16,256]{2,1,0:T(8,128)S(1)}, u32[]{:S(2)}, u32[]{:S(2)}) collective-permute-start(f32[8,16,256]{2,1,0:T(8,128)S(1)} %get-tuple-element.30), channel_id=1, source_target_pairs={{0,16},{8,24},{16,0},{24,8},{1,17},{9,25},{17,1},{25,9},{2,18},{10... | collective-permute-start | bytes 393224 | tf_op jit(solution)/shard_map/ppermute | solution.py:332
  95.6 7.8 %collective-permute-start.25 = (f32[8,16,256]{2,1,0:T(8,128)S(1)}, f32[8,16,256]{2,1,0:T(8,128)S(1)}, u32[]{:S(2)}, u32[]{:S(2)}) collective-permute-start(f32[8,16,256]{2,1,0:T(8,128)S(1)} %get-tuple-element.31), channel_id=1, source_target_pairs={{0,24},{8,0},{16,8},{24,16},{1,25},{9,1},{17,9},{25,17},{2,26},{10... | collective-permute-start | bytes 393224 | tf_op jit(solution)/shard_map/ppermute | solution.py:332
  97.5 6.7 %collective-permute-start.23 = (f32[8,16,256]{2,1,0:T(8,128)S(1)}, f32[8,16,256]{2,1,0:T(8,128)S(1)}, u32[]{:S(2)}, u32[]{:S(2)}) collective-permute-start(f32[8,16,256]{2,1,0:T(8,128)S(1)} %get-tuple-element.32), channel_id=1, source_target_pairs={{0,8},{8,16},{16,24},{24,0},{1,9},{9,17},{17,25},{25,1},{2,10},{10... | collective-permute-start | bytes 393224 | tf_op jit(solution)/shard_map/ppermute | solution.py:332
  97.6 10.6 %collective-permute-start.20 = (f32[128,256]{1,0:T(8,128)}, f32[128,256]{1,0:T(8,128)S(1)}, u32[]{:S(2)}, u32[]{:S(2)}) collective-permute-start(f32[128,256]{1,0:T(8,128)} %get-tuple-element.21.refs_0_), channel_id=1, source_target_pairs={{0,3},{1,0},{2,1},{3,2},{4,7},{5,4},{6,5},{7,6},{8,11},{9,8},{10,9... | collective-permute-start | bytes 393224 | tf_op jit(solution)/shard_map/ppermute | solution.py:332
  98.1 10.2 %collective-permute-start.19 = (f32[128,256]{1,0:T(8,128)}, f32[128,256]{1,0:T(8,128)S(1)}, u32[]{:S(2)}, u32[]{:S(2)}) collective-permute-start(f32[128,256]{1,0:T(8,128)} %get-tuple-element.21.refs_0_), channel_id=1, source_target_pairs={{0,2},{1,3},{2,0},{3,1},{4,6},{5,7},{6,4},{7,5},{8,10},{9,11},{10,... | collective-permute-start | bytes 393224 | tf_op jit(solution)/shard_map/ppermute | solution.py:332
  101.8 6.4 %collective-permute-start.18 = (f32[128,256]{1,0:T(8,128)}, f32[128,256]{1,0:T(8,128)S(1)}, u32[]{:S(2)}, u32[]{:S(2)}) collective-permute-start(f32[128,256]{1,0:T(8,128)} %get-tuple-element.21.refs_0_), channel_id=1, source_target_pairs={{0,1},{1,2},{2,3},{3,0},{4,5},{5,6},{6,7},{7,4},{8,9},{9,10},{10,1... | collective-permute-start | bytes 393224 | tf_op jit(solution)/shard_map/ppermute | solution.py:332
  104.8 12.4 %all-to-all-start.2 = ((f32[8,16,256]{2,1,0:T(8,128)}), f32[8,16,256]{2,1,0:T(8,128)S(1)}, u32[]{:S(2)}, u32[]{:S(2)}) async-start(f32[8,16,256]{2,1,0:T(8,128)} %fusion), calls=%async_computation.2 | async-start | bytes 262144 | tf_op jit(solution)/shard_map/all_to_all | solution.py:368
  111.4 10.8 %collective-permute-start.21 = (f32[128,256]{1,0:T(8,128)}, f32[128,256]{1,0:T(8,128)S(1)}, u32[]{:S(2)}, u32[]{:S(2)}) collective-permute-start(f32[128,256]{1,0:T(8,128)} %ordered_sum.1.mine), channel_id=1, source_target_pairs={{0,4},{4,0},{1,5},{5,1},{2,6},{6,2},{3,7},{7,3},{8,12},{12,8},{9,1... | collective-permute-start | bytes 393224 | tf_op jit(solution)/shard_map/ppermute | solution.py:332
  117.2 12.5 %collective-permute-start.28 = (f32[16,256]{1,0:T(8,128)S(1)}, f32[16,256]{1,0:T(8,128)S(1)}, u32[]{:S(2)}, u32[]{:S(2)}) collective-permute-start(f32[16,256]{1,0:T(8,128)S(1)} %reduce_sum.19.refs_0_), channel_id=1, source_target_pairs={{0,3},{1,0},{2,1},{3,2},{4,7},{5,4},{6,5},{7,6},{8,11},{9,8},{10,9... | collective-permute-start | bytes 49160 | tf_op jit(solution)/shard_map/ppermute | solution.py:332
  117.8 12.0 %collective-permute-start.27 = (f32[16,256]{1,0:T(8,128)S(1)}, f32[16,256]{1,0:T(8,128)S(1)}, u32[]{:S(2)}, u32[]{:S(2)}) collective-permute-start(f32[16,256]{1,0:T(8,128)S(1)} %reduce_sum.19.refs_0_), channel_id=1, source_target_pairs={{0,2},{1,3},{2,0},{3,1},{4,6},{5,7},{6,4},{7,5},{8,10},{9,11},{10,... | collective-permute-start | bytes 49160 | tf_op jit(solution)/shard_map/ppermute | solution.py:332
  120.4 9.4 %collective-permute-start.26 = (f32[16,256]{1,0:T(8,128)S(1)}, f32[16,256]{1,0:T(8,128)S(1)}, u32[]{:S(2)}, u32[]{:S(2)}) collective-permute-start(f32[16,256]{1,0:T(8,128)S(1)} %reduce_sum.19.refs_0_), channel_id=1, source_target_pairs={{0,1},{1,2},{2,3},{3,0},{4,5},{5,6},{6,7},{7,4},{8,9},{9,10},{10,1... | collective-permute-start | bytes 49160 | tf_op jit(solution)/shard_map/ppermute | solution.py:332
  (30 other events, 144.2 us)
where the time goes:
time: 133 us
  Pallas kernels  39 us (29%)
  blocking collectives  30.7 us (23%)
  starting transfers between devices  27.4 us (21%)
  waiting for transfers between devices  25.9 us (19%)
  local copies, waits for them, and re-layouts  5.36 us (4%)
  other arithmetic  3.44 us (3%)
    all_to_all x2, blocking collectives, copied_along_z(): return lax.all_to_all(whole, 'z', 0, 0, tiled=True)  30.7 us
    ppermute x29, starting transfers between devices, shifted(): lax.ppermute(array, axis, [(i, (i + by) % size) for i in range(size)])  24 us
    ppermute x29, waiting for transfers between devices, shifted(): lax.ppermute(array, axis, [(i, (i + by) % size) for i in range(size)])  20.1 us
    pallas_call x2, Pallas kernels, system(): pl.pallas_call(kernel, in_specs=[SMEM] + [VMEM] * (1 + len(parts)), out_s...  16 us
    pallas_call x1, Pallas kernels, dct(): pl.pallas_call(dct_kernel, grid=(steps,), in_specs=[pl.BlockSpec(block, l...  8.82 us
    pallas_call x1, Pallas kernels, col_update(): pl.pallas_call(col_kernel, in_specs=[SMEM] + [VMEM] * 3 + [VMEM] * 11, ou...  6.01 us
    all_to_all x1, waiting for transfers between devices, body(): mine = lax.all_to_all(block, 'z', 0, 0, tiled=True).sum(axis=0)  5.78 us
    unnamed x48, local copies, waits for them, and re-layouts  4.58 us
  transfers between devices with their start and end apart: 30, of which 13 were waited for; matrix products, arithmetic and copies ran while one was open for 1% of the time, Pallas kernels for 20%

commit v1 on v0

v1 whole, which is shorter than its diff:
```python
import math

import jax
import jax.numpy as jnp
import numpy as np
from jax import lax
from jax.experimental import pallas as pl
from jax.experimental.pallas import tpu as pltpu
from jax.sharding import Mesh
from jax.sharding import PartitionSpec as P

ROWS = 4096
KEEP = 1024
RANK = 256
COLS = 256
ADMM_STEPS = 3
PART = ROWS // 4
BAND = KEEP // 4
STEP = 256
NZ, NX, NC, NY = 8, 4, 2, 4
WIDE = ("z", "x", "c")
F32 = jnp.float32
BF16 = jnp.bfloat16
VMEM = pl.BlockSpec(memory_space=pltpu.VMEM)


def twiddles():
    odd = 2 * np.arange(STEP)[None, :] + 1
    degree = np.arange(BAND)[:, None]
    scale = math.sqrt(2.0 / ROWS)
    angles = np.pi * odd * degree / 2048, np.pi * odd * (2 * degree + 1) / 4096
    weight = np.where(degree == 0, math.sqrt(1.0 / ROWS), scale), scale
    base = [w * f(a) for w, a in zip(weight, angles) for f in (np.cos, np.sin)]
    lanes = np.ones((1, 128))
    eight = np.arange(8)[:, None] * lanes
    ahead = [f(a) for a in (np.pi * eight / 4, np.pi * (2 * eight + 1) / 8) for f in (np.cos, np.sin)]
    turn = np.pi * (2 * eight + 1) / 8192
    tables = base + [np.stack(ahead + [np.cos(turn), np.sin(turn)])]
    return [jnp.asarray(table.astype(np.float32)) for table in tables]


def room(mebibytes):
    return pltpu.CompilerParams(vmem_limit_bytes=mebibytes * 2**20)


def split(value):
    high = value.astype(BF16)
    return high, (value - high.astype(F32)).astype(BF16)


def dot(a, b):
    return jnp.dot(a, b, preferred_element_type=F32)


def dot3(a, b):
    return dot(a[0], b[0]) + (dot(a[1], b[0]) + dot(a[0], b[1]))


def exact(a, b):
    return jnp.dot(a, b, precision=lax.Precision.HIGHEST, preferred_element_type=F32)


def twice(value):
    return jnp.concatenate([value, value], axis=1)


def turned(ref, s):
    index = 7 - lax.broadcasted_iota(jnp.int32, (8, COLS), 0)
    tiles = []
    for t in range(STEP // 8):
        tile = ref[s, STEP - 8 * (t + 1) : STEP - 8 * t, :]
        tiles.append(jnp.take_along_axis(tile, index, axis=0, mode="promise_in_bounds"))
    return jnp.concatenate(tiles, axis=0)


def dct_kernel(x0, x1, x2, x3, *refs):
    base, ahead, outs = refs[:4], refs[4], refs[5:9]
    held, rotated, total = refs[9:13], refs[13:15], refs[15]
    high, low, high_t, low_t = outs
    step = pl.program_id(0)

    @pl.when(step == 0)
    def _():
        total[...] = jnp.zeros_like(total)
        for ref, first in zip(held, base):
            ref[...] = first[...]
        cos, sin = ahead[4], ahead[5]
        for t in range(STEP // 8):
            by_cos, by_sin = math.cos(math.pi * t / 512), math.sin(math.pi * t / 512)
            rotated[0][8 * t : 8 * t + 8, :] = cos * by_cos - sin * by_sin
            rotated[1][8 * t : 8 * t + 8, :] = sin * by_cos + cos * by_sin

    @pl.when(step > 0)
    def _():
        for pair in range(2):
            cos, sin = held[2 * pair][...], held[2 * pair + 1][...]
            by_cos = jnp.concatenate([twice(ahead[2 * pair])] * 32, axis=0)
            by_sin = jnp.concatenate([twice(ahead[2 * pair + 1])] * 32, axis=0)
            held[2 * pair][...] = cos * by_cos - sin * by_sin
            held[2 * pair + 1][...] = sin * by_cos + cos * by_sin
        cos, sin = rotated[0][...], rotated[1][...]
        by_cos, by_sin = math.cos(math.pi / 16), math.sin(math.pi / 16)
        rotated[0][...] = cos * by_cos - sin * by_sin
        rotated[1][...] = sin * by_cos + cos * by_sin

    plain, even, odd = split(held[0][...]), split(held[2][...]), split(held[3][...])
    cos, sin = twice(rotated[0][...]), twice(rotated[1][...])
    for s in range(2):
        first, third = x0[s], x2[s]
        second, fourth = turned(x1, s), turned(x3, s)
        outer, inner = first + fourth, second + third
        v, w = first - fourth, second - third
        total[s, 0] += dot3(plain, split(outer + inner))
        total[s, 2] += dot3(even, split(outer - inner))
        p = dot3(even, split(v * cos - w * sin))
        q = dot3(odd, split(v * sin + w * cos))
        total[s, 1] += p + q
        total[s, 3] += p - q

    @pl.when(step == pl.num_programs(0) - 1)
    def _():
        for s in range(2):
            for k in range(4):
                high[s, k], low[s, k] = split(total[s, k])
                place = slice(BAND * k, BAND * (k + 1))
                high_t[s, :, place], low_t[s, :, place] = split(total[s, k].T)


def dct(snapshots):
    tables = twiddles()
    steps = PART // STEP
    block = (2, STEP, COLS)
    square = pltpu.VMEM((BAND, STEP), F32)
    turn = pltpu.VMEM((STEP, 128), F32)
    straight = jax.ShapeDtypeStruct((2, 4, BAND, COLS), BF16)
    crossed = jax.ShapeDtypeStruct((2, COLS, KEEP), BF16)

    def whole(shape):
        return pl.BlockSpec(shape, lambda i: (0,) * len(shape))

    return pl.pallas_call(
        dct_kernel,
        grid=(steps,),
        in_specs=[
            pl.BlockSpec(block, lambda i: (0, i, 0)),
            pl.BlockSpec(block, lambda i: (0, 2 * steps - 1 - i, 0)),
            pl.BlockSpec(block, lambda i: (0, 2 * steps + i, 0)),
            pl.BlockSpec(block, lambda i: (0, 4 * steps - 1 - i, 0)),
        ]
        + [whole(table.shape) for table in tables],
        out_specs=[whole(a.shape) for a in (straight, straight, crossed, crossed)],
        out_shape=[straight, straight, crossed, crossed],
        scratch_shapes=[square] * 4 + [turn] * 2 + [pltpu.VMEM((2, 4, BAND, COLS), F32)],
        cost_estimate=pl.CostEstimate(flops=7_000_000_000, bytes_accessed=13_000_000, transcendentals=0),
        compiler_params=room(24),
        name="dct",
    )(*([snapshots] * 4), *tables)


def place_of_own():
    return tuple(lax.axis_index(name) for name in ("z", "x", "c", "y"))


def own_weights(snap, z, x, core):
    wide = (z * NX + x) * NC + core
    return [snap[pl.ds(2 * wide + s, 1), :] for s in range(2)]


def place_rows(core, mine, other, rows):
    for ref, owner in ((mine, core), (other, 1 - core)):
        for group in range(NZ * NX):
            start = pl.multiple_of(group * 32 + owner * 16, 16)
            for half in range(2):
                rows[half, pl.ds(start, 16), :] = ref[group, :, 128 * half : 128 * half + 128]


def totals_kernel(high_t, low_t, snap, mine, other, keep, send, rows, total):
    z, x, core, _ = place_of_own()
    place_rows(core, mine, other, rows)
    sums = [0.0, 0.0]
    for k in range(4):
        line = [rows[half, pl.ds(k, BAND, stride=4), :] for half in range(2)]
        lines = split(jnp.concatenate(line, axis=1))
        place = slice(BAND * k, BAND * (k + 1))
        for s in range(2):
            sums[s] += dot3((high_t[s, :, place], low_t[s, :, place]), lines)
    weights = own_weights(snap, z, x, core)
    total[...] = sums[0] * weights[0] + sums[1] * weights[1]
    for shift in range(NX):
        target = lax.rem(x + shift, NX)
        for ref, owner in ((keep, core), (send, 1 - core)):
            start = pl.multiple_of(owner * 128 + target * 32, 32)
            ref[shift] = total[pl.ds(start, 32), :]


def totals(high_t, low_t, snap, mine, other):
    part = jax.ShapeDtypeStruct((NX, 32, RANK), F32)
    return pl.pallas_call(
        totals_kernel,
        in_specs=[VMEM] * 5,
        out_specs=[VMEM] * 2,
        out_shape=[part] * 2,
        scratch_shapes=[pltpu.VMEM((2, KEEP, 128), F32), pltpu.VMEM((COLS, RANK), F32)],
        cost_estimate=pl.CostEstimate(flops=800_000_000, bytes_accessed=4_000_000, transcendentals=0),
        compiler_params=room(12),
        name="totals",
    )(high_t, low_t, snap, mine, other)


def inverse(gram, state):
    eye = (
        lax.broadcasted_iota(jnp.int32, (RANK, RANK), 0)
        == lax.broadcasted_iota(jnp.int32, (RANK, RANK), 1)
    ).astype(F32)
    penalty = jnp.sum(gram * eye) / RANK
    system = gram / penalty + eye
    middle = 2.0 / (1.0 + 257.0)
    state[:RANK] = middle * eye
    state[RANK:] = eye - middle * system

    def double(step, reach):
        doubled = 2.0 * reach * reach - 1.0
        gain = 2.0 * reach * reach / doubled
        both = state[...]
        product = gain * dot3(split(both), split(both[RANK:]))
        state[:RANK] = gain * both[:RANK] + product[:RANK]
        state[RANK:] = product[RANK:] - (1.0 / doubled) * eye
        return doubled

    lax.fori_loop(0, 6, double, jnp.float32(258.0 / 256.0))
    found = state[:RANK]
    found = found + dot3(split(found), split(eye - exact(system, found)))
    return found / penalty, penalty


def col_system_kernel(snap, mine, other, inv, pen, rows, state):
    _, _, core, _ = place_of_own()
    place_rows(core, mine, other, rows)
    snaps, lines = snap[...], jnp.concatenate([rows[0], rows[1]], axis=1)
    found, penalty = inverse(exact(snaps.T, snaps) * exact(lines.T, lines), state)
    inv[...] = found
    pen[...] = jnp.full((8, 128), penalty, F32)


def row_system_kernel(snap, mine, other, inv, pen, gram, state):
    _, _, core, _ = place_of_own()
    gram[pl.ds(pl.multiple_of(core * 128, 128), 128), :] = mine[...]
    gram[pl.ds(pl.multiple_of((1 - core) * 128, 128), 128), :] = other[...]
    snaps = snap[...]
    found, penalty = inverse(exact(snaps.T, snaps) * gram[...], state)
    inv[...] = found
    pen[...] = jnp.full((8, 128), penalty, F32)


def system(kernel, snap, mine, other, scratch, name):
    return pl.pallas_call(
        kernel,
        in_specs=[VMEM] * 3,
        out_specs=[VMEM] * 2,
        out_shape=[
            jax.ShapeDtypeStruct((RANK, RANK), F32),
            jax.ShapeDtypeStruct((8, 128), F32),
        ],
        scratch_shapes=[pltpu.VMEM(scratch, F32), pltpu.VMEM((2 * RANK, RANK), F32)],
        cost_estimate=pl.CostEstimate(flops=3_000_000_000, bytes_accessed=1_000_000, transcendentals=0),
        compiler_params=room(8),
        name=name,
    )(snap, mine, other)


def admm_update(sums, inv, penalty, factor, dual, new, dual_new):
    new[...] = factor[...]
    dual_new[...] = dual[...]

    def update(step, carry):
        primal, multiplier = new[...], dual_new[...]
        solved = exact(sums[...] + penalty * (primal + multiplier), inv[...])
        primal = jnp.maximum(solved - multiplier, 0.0)
        new[...] = primal
        dual_new[...] = multiplier + primal - solved
        return carry

    lax.fori_loop(0, ADMM_STEPS, update, 0)


def col_kernel(high, low, snap, inv, pen, factor, dual, *refs):
    pieces = refs[:8]
    new, dual_new, keep, send, gram_half = refs[8:13]
    total, mapped, gram = refs[13:]
    z, x, core, _ = place_of_own()
    for side in range(NC):
        for shift in range(NX):
            source = lax.rem(x - shift + NX, NX)
            owner = core if side == 0 else 1 - core
            start = pl.multiple_of(owner * 128 + source * 32, 32)
            total[pl.ds(start, 32), :] = pieces[side * NX + shift][...]
    admm_update(total, inv, pen[0, 0], factor, dual, new, dual_new)
    primal = new[...]
    gram[...] = exact(primal.T, primal)
    gram_half[...] = gram[pl.ds(pl.multiple_of(core * 128, 128), 128), :]
    lines, weights = split(primal), own_weights(snap, z, x, core)
    for k in range(4):
        line = sum(dot3((high[s, k], low[s, k]), lines) * weights[s] for s in range(2))
        for half in range(2):
            mapped[half, pl.ds(k, BAND, stride=4), :] = line[:, 128 * half : 128 * half + 128]
    for shift in range(NX):
        target = lax.rem(x + shift, NX)
        for ref, owner in ((keep, core), (send, 1 - core)):
            for line in range(NZ):
                start = pl.multiple_of(line * 128 + target * 32 + owner * 16, 16)
                for half in range(2):
                    ref[shift, line, :, 128 * half : 128 * half + 128] = mapped[half, pl.ds(start, 16), :]


def col_update(high, low, snap, inv, pen, factor, dual, pieces):
    square = jax.ShapeDtypeStruct((COLS, RANK), F32)
    part = jax.ShapeDtypeStruct((NX, NZ, 16, RANK), F32)
    return pl.pallas_call(
        col_kernel,
        in_specs=[VMEM] * 15,
        out_specs=[VMEM] * 5,
        out_shape=[square, square, part, part, jax.ShapeDtypeStruct((128, RANK), F32)],
        scratch_shapes=[
            pltpu.VMEM((COLS, RANK), F32),
            pltpu.VMEM((2, KEEP, 128), F32),
            pltpu.VMEM((RANK, RANK), F32),
        ],
        cost_estimate=pl.CostEstimate(flops=1_500_000_000, bytes_accessed=5_000_000, transcendentals=0),
        compiler_params=room(14),
        name="col_update",
    )(high, low, snap, inv, pen, factor, dual, *pieces)


def in_order(parts, held):
    y = lax.axis_index("y")
    for shift in range(NY):
        held[lax.rem(y - shift + NY, NY)] = parts[shift][...]
    return (held[0] + held[1]) + (held[2] + held[3])


def sum_kernel(*refs):
    parts, out, held = refs[:4], refs[4], refs[5]
    out[...] = in_order(parts, held)


def ordered_sum(parts):
    shape = parts[0].shape
    return pl.pallas_call(
        sum_kernel,
        in_specs=[VMEM] * 4,
        out_specs=VMEM,
        out_shape=jax.ShapeDtypeStruct(shape, F32),
        scratch_shapes=[pltpu.VMEM((NY, *shape), F32)],
        compiler_params=room(4),
        name="ordered_sum",
    )(*parts)


def row_kernel(inv, pen, factor, dual, *refs):
    parts, (new, dual_new), held = refs[:4], refs[4:6], refs[6]
    held[0] = in_order(parts, held)
    admm_update(held.at[0], inv, pen[0, 0], factor, dual, new, dual_new)


def row_update(inv, pen, factor, dual, parts):
    own = jax.ShapeDtypeStruct((16, RANK), F32)
    return pl.pallas_call(
        row_kernel,
        in_specs=[VMEM] * 8,
        out_specs=[VMEM] * 2,
        out_shape=[own] * 2,
        scratch_shapes=[pltpu.VMEM((NY, 16, RANK), F32)],
        compiler_params=room(4),
        name="row_update",
    )(inv, pen, factor, dual, *parts)


def shifted(array, axis, size, by):
    return lax.ppermute(array, axis, [(i, (i + by) % size) for i in range(size)])


def from_all(array, axis, size):
    return [array] + [shifted(array, axis, size, by) for by in range(1, size)]


def copied_along(array, axes, size):
    whole = jnp.broadcast_to(array[None], (size, *array.shape))
    return lax.all_to_all(whole, axes, 0, 0, tiled=True)


def body(snapshots, snap_factor, row_factor, col_factor, row_dual, col_dual):
    mine = copied_along(row_factor, ("z", "x"), NZ * NX)
    high, low, high_t, low_t = dct(snapshots)
    mine, high_t = lax.optimization_barrier((mine, high_t))
    other = shifted(mine, "c", NC, 1)
    keep, send = totals(high_t, low_t, snap_factor, mine, other)
    inv, pen = system(
        col_system_kernel, snap_factor, mine, other, (2, KEEP, 128), "col_system"
    )
    half = keep + shifted(send, "c", NC, 1)
    chunk = half[0] + sum(shifted(half[by], "x", NX, by) for by in range(1, NX))
    chunk = copied_along(chunk, "z", NZ)
    chunk, inv = lax.optimization_barrier((chunk, inv))
    pieces = from_all(chunk.sum(axis=0), "x", NX)
    pieces = pieces + [shifted(piece, "c", NC, 1) for piece in pieces]
    col_new, col_dual_new, keep, send, gram_half = col_update(
        high, low, snap_factor, inv, pen, col_factor, col_dual, pieces
    )
    gram_mine = ordered_sum(from_all(gram_half, "y", NY))
    gram_other = shifted(gram_mine, "c", NC, 1)
    inv, pen = system(
        row_system_kernel, snap_factor, gram_mine, gram_other, (RANK, RANK), "row_system"
    )
    half = keep + shifted(send, "c", NC, 1)
    block = half[0] + sum(shifted(half[by], "x", NX, by) for by in range(1, NX))
    block = lax.all_to_all(block, "z", 0, 0, tiled=True)
    block, inv = lax.optimization_barrier((block, inv))
    row_new, row_dual_new = row_update(
        inv, pen, row_factor, row_dual, from_all(block.sum(axis=0), "y", NY)
    )
    return row_new, col_new, row_dual_new, col_dual_new


def solution(mesh):
    fine = Mesh(mesh.devices.reshape(NZ, NX, NC, NY), ("z", "x", "c", "y"))
    return jax.shard_map(
        body,
        mesh=fine,
        in_specs=(
            P(WIDE, None, "y"),
            P(),
            P(WIDE, None),
            P("y", None),
            P(WIDE, None),
            P("y", None),
        ),
        out_specs=(P(WIDE, None), P("y", None), P(WIDE, None), P("y", None)),
        check_vma=False,
    )
```

time: 133 us -> 116 us (0.87); the launches traced: 133 us -> 114 us
  blocking collectives: 30.7 us -> 0 us
  Pallas kernels: 39 us -> 21.3 us
  starting transfers between devices: 27.4 us -> 43.1 us
  local copies, waits for them, and re-layouts: 5.36 us -> 14.9 us
  waiting for transfers between devices: 25.9 us -> 32.3 us
  other arithmetic: 3.44 us -> 1.79 us
    all_to_all x2 -> x0, blocking collectives: 30.7 us -> none  [copied_along_z(): return lax.all_to_all(whole, 'z', 0, 0, tiled=True)]
    all_to_all x1 -> x3, starting transfers between devices: 3.37 us -> 21.3 us  [the longest x2 18 us: copied_along(): return lax.all_to_all(whole, axes, 0, 0, tiled=True)]
    pallas_call x6, Pallas kernels: 30.2 us -> 14.2 us  [the longest x2 8.5 us: system(): pl.pallas_call(kernel, in_specs=[VMEM] * 3, out_specs=[VMEM] * 2, out_sha...]
    unnamed x48 -> x34, local copies, waits for them, and re-layouts: 4.58 us -> 12.5 us
    all_to_all x1 -> x3, waiting for transfers between devices: 5.78 us -> 11.1 us  [the longest x2 5.82 us: copied_along(): return lax.all_to_all(whole, axes, 0, 0, tiled=True)]
    ppermute x29 -> x23, starting transfers between devices: 24 us -> 21.8 us  [shifted(): lax.ppermute(array, axis, [(i, (i + by) % size) for i in range(size)])]
    add x2, other arithmetic: 2.05 us -> 0.1 us  [body(): half = keep + shifted(send, 'c', NC, 1)]
    pallas_call x1, Pallas kernels: 8.82 us -> 7.07 us  [dct(): pl.pallas_call(dct_kernel, grid=(steps,), in_specs=[pl.BlockSpec(block, l...]
  transfers between devices with their start and end apart: 30 -> 26, of which waited for: 13 -> 20; matrix products, arithmetic and copies ran while one was open for 1% -> 1% of each run, Pallas kernels for 20% -> 14%
where the time goes in v1:
time: 116 us; the launch traced here: 114 us
  starting transfers between devices  43.1 us (37%)
  waiting for transfers between devices  32.3 us (28%)
  Pallas kernels  21.3 us (18%)
  local copies, waits for them, and re-layouts  14.9 us (13%)
  other arithmetic  1.79 us (2%)
    ppermute x23, starting transfers between devices, shifted(): lax.ppermute(array, axis, [(i, (i + by) % size) for i in range(size)])  21.8 us
    ppermute x23, waiting for transfers between devices, shifted(): lax.ppermute(array, axis, [(i, (i + by) % size) for i in range(size)])  21.2 us
    all_to_all x2, starting transfers between devices, copied_along(): return lax.all_to_all(whole, axes, 0, 0, tiled=True)  18 us
    unnamed x34, local copies, waits for them, and re-layouts  12.5 us
    pallas_call x2, Pallas kernels, system(): pl.pallas_call(kernel, in_specs=[VMEM] * 3, out_specs=[VMEM] * 2, out_sha...  8.5 us
    pallas_call x1, Pallas kernels, dct(): pl.pallas_call(dct_kernel, grid=(steps,), in_specs=[pl.BlockSpec(block, l...  7.07 us
    all_to_all x2, waiting for transfers between devices, copied_along(): return lax.all_to_all(whole, axes, 0, 0, tiled=True)  5.82 us
    all_to_all x1, waiting for transfers between devices, body(): block = lax.all_to_all(block, 'z', 0, 0, tiled=True)  5.27 us
  transfers between devices with their start and end apart: 26, of which 20 were waited for; matrix products, arithmetic and copies ran while one was open for 1% of the time, Pallas kernels for 14%

profile of v1, /device:TPU:8, one launch (start us, length us, event | category | flops | bytes accessed | tf_op | source)
XLA Modules:
  0.0 114.2 jit_solution(173164302981876026)
XLA Ops:
  0.6 1.6 %broadcast_in_dim.4 = f32[32,16,256]{2,1,0:T(8,128)} broadcast(f32[16,256]{1,0:T(8,128)} %factor.3), dimensions={1,2} | broadcast | bytes 540672 | tf_op jit(solution)/shard_map/broadcast_in_dim | solution.py:387
  2.2 11.3 %all-to-all-start = ((f32[32,16,256]{2,1,0:T(8,128)}), f32[32,16,256]{2,1,0:T(8,128)S(1)}, u32[]{:S(2)}, u32[]{:S(2)}) async-start(f32[32,16,256]{2,1,0:T(8,128)} %broadcast_in_dim.4), calls=%async_computation | async-start | bytes 1048576 | tf_op jit(solution)/shard_map/all_to_all | solution.py:388
  13.6 3.4 %copy-done = f32[2,4096,256]{2,1,0:T(8,128)S(1)} copy-done((f32[2,4096,256]{2,1,0:T(8,128)S(1)}, f32[2,4096,256]{2,1,0:T(8,128)}, u32[]{:S(2)}) %copy-start) | copy-done | bytes 8388632
  21.5 7.1 %dct.1 = (bf16[2,4,256,256]{3,2,1,0:T(8,128)(2,1)S(1)}, bf16[2,4,256,256]{3,2,1,0:T(8,128)(2,1)S(1)}, bf16[2,256,1024]{2,1,0:T(8,128)(2,1)S(1)}, bf16[2,256,1024]{2,1,0:T(8,128)(2,1)S(1)}) custom-call(f32[2,4096,256]{2,1,0:T(8,128)S(1)} %copy-done, f32[2,4096,256]{2,1,0:T(8,128)S(1)} %copy-done, f32[2,4096,256]{2,1,0:T(8,128)S(1)} %copy-done, ...), custom_call_target="tpu_custom_call" | custom-call | flops 7000000000 | bytes 13000000 | tf_op jit(solution)/shard_map/dct/pallas_call | solution.py:141
  31.3 1.9 %collective-permute-done.other = f32[32,16,256]{2,1,0:T(8,128)S(1)} collective-permute-done((f32[32,16,256]{2,1,0:T(8,128)S(1)}, f32[32,16,256]{2,1,0:T(8,128)S(1)}, u32[]{:S(2)}, u32[]{:S(2)}) %collective-permute-start) | collective-permute-done | bytes 524320 | tf_op jit(solution)/shard_map/ppermute | solution.py:379
  35.9 2.6 %collective-permute-start.3 = (f32[32,256]{1,0:T(8,128)S(1)}, f32[32,256]{1,0:T(8,128)S(1)}, u32[]{:S(2)}, u32[]{:S(2)}) collective-permute-start(f32[32,256]{1,0:T(8,128)S(1)} %get-tuple-element.53), channel_id=1, source_target_pairs={{0,16},{8,24},{16,0},{24,8},{1,17},{9,25},{17,1},{25,9},{2,18},{10... | collective-permute-start | bytes 98312 | tf_op jit(solution)/shard_map/ppermute | solution.py:379
  42.4 2.4 %collective-permute-done.2 = f32[32,256]{1,0:T(8,128)S(1)} collective-permute-done((f32[32,256]{1,0:T(8,128)S(1)}, f32[32,256]{1,0:T(8,128)S(1)}, u32[]{:S(2)}, u32[]{:S(2)}) %collective-permute-start.2) | collective-permute-done | bytes 32800 | tf_op jit(solution)/shard_map/ppermute | solution.py:379
  45.5 6.6 %all-to-all-start.1 = ((f32[8,32,256]{2,1,0:T(8,128)}), f32[8,32,256]{2,1,0:T(8,128)}, u32[]{:S(2)}, u32[]{:S(2)}) async-start(f32[8,32,256]{2,1,0:T(8,128)} %broadcast_in_dim.5), calls=%async_computation.1 | async-start | bytes 524288 | tf_op jit(solution)/shard_map/all_to_all | solution.py:388
  52.2 4.8 %col_system.1 = (f32[256,256]{1,0:T(8,128)S(1)}, f32[8,128]{1,0:T(8,128)S(1)}) custom-call(f32[128,256]{1,0:T(8,128)S(1)} %copy-done.5, f32[32,16,256]{2,1,0:T(8,128)S(1)} %all-to-all-done.mine, f32[32,16,256]{2,1,0:T(8,128)S(1)} %collective-permute-done.other), custom_call_target="tpu_custom_call" | custom-call | flops 3000000000 | bytes 1000000 | tf_op jit(solution)/shard_map/col_system/pallas_call | solution.py:256
  57.7 5.1 %all-to-all-done.1 = f32[8,32,256]{2,1,0:T(8,128)} async-done(((f32[8,32,256]{2,1,0:T(8,128)}), f32[8,32,256]{2,1,0:T(8,128)}, u32[]{:S(2)}, u32[]{:S(2)}) %all-to-all-start.1) | async-done | bytes 262176 | tf_op jit(solution)/shard_map/all_to_all | solution.py:388
  65.8 1.9 %collective-permute-done.7.refs_3_ = f32[32,256]{1,0:T(8,128)S(1)} collective-permute-done((f32[32,256]{1,0:T(8,128)S(1)}, f32[32,256]{1,0:T(8,128)S(1)}, u32[]{:S(2)}, u32[]{:S(2)}) %collective-permute-start.7) | collective-permute-done | bytes 32800 | tf_op jit(solution)/shard_map/ppermute | solution.py:379
  67.7 2.1 %collective-permute-done.6.refs_2_ = f32[32,256]{1,0:T(8,128)S(1)} collective-permute-done((f32[32,256]{1,0:T(8,128)S(1)}, f32[32,256]{1,0:T(8,128)S(1)}, u32[]{:S(2)}, u32[]{:S(2)}) %collective-permute-start.6) | collective-permute-done | bytes 32800 | tf_op jit(solution)/shard_map/ppermute | solution.py:379
  74.0 3.2 %col_update.1 = (f32[256,256]{1,0:T(8,128)}, f32[256,256]{1,0:T(8,128)}, f32[4,8,16,256]{3,2,1,0:T(8,128)S(1)}, f32[4,8,16,256]{3,2,1,0:T(8,128)S(1)}, f32[128,256]{1,0:T(8,128)S(1)}) custom-call(bf16[2,4,256,256]{3,2,1,0:T(8,128)(2,1)S(1)} %copy-done.10, bf16[2,4,256,256]{3,2,1,0:T(8,128)(2,1)S(1)} %copy-done.12, f32[128,256]{1,0:T(8,128)S(1)} %copy-done.5, ...), custom_call_target="tpu_custom_call" | custom-call | flops 1500000000 | bytes 5000000 | tf_op jit(solution)/shard_map/col_update/pallas_call | solution.py:318
  77.8 2.6 %collective-permute-start.17 = (f32[128,256]{1,0:T(8,128)S(1)}, f32[128,256]{1,0:T(8,128)S(1)}, u32[]{:S(2)}, u32[]{:S(2)}) collective-permute-start(f32[128,256]{1,0:T(8,128)S(1)} %get-tuple-element.41.refs_0_), channel_id=1, source_target_pairs={{0,2},{1,3},{2,0},{3,1},{4,6},{5,7},{6,4},{7,5},{8,10},{9,11},{10,... | collective-permute-start | bytes 393224 | tf_op jit(solution)/shard_map/ppermute | solution.py:379
  80.4 1.9 %collective-permute-start.16 = (f32[128,256]{1,0:T(8,128)S(1)}, f32[128,256]{1,0:T(8,128)S(1)}, u32[]{:S(2)}, u32[]{:S(2)}) collective-permute-start(f32[128,256]{1,0:T(8,128)S(1)} %get-tuple-element.41.refs_0_), channel_id=1, source_target_pairs={{0,1},{1,2},{2,3},{3,0},{4,5},{5,6},{6,7},{7,4},{8,9},{9,10},{10,1... | collective-permute-start | bytes 393224 | tf_op jit(solution)/shard_map/ppermute | solution.py:379
  83.4 2.5 %collective-permute-start.15 = (f32[8,16,256]{2,1,0:T(8,128)S(1)}, f32[8,16,256]{2,1,0:T(8,128)S(1)}, u32[]{:S(2)}, u32[]{:S(2)}) collective-permute-start(f32[8,16,256]{2,1,0:T(8,128)S(1)} %get-tuple-element.51), channel_id=1, source_target_pairs={{0,24},{8,0},{16,8},{24,16},{1,25},{9,1},{17,9},{25,17},{2,26},{10... | collective-permute-start | bytes 393224 | tf_op jit(solution)/shard_map/ppermute | solution.py:379
  87.9 2.5 %collective-permute-done.14 = f32[8,16,256]{2,1,0:T(8,128)S(1)} collective-permute-done((f32[8,16,256]{2,1,0:T(8,128)S(1)}, f32[8,16,256]{2,1,0:T(8,128)S(1)}, u32[]{:S(2)}, u32[]{:S(2)}) %collective-permute-start.14) | collective-permute-done | bytes 131104 | tf_op jit(solution)/shard_map/ppermute | solution.py:379
  90.6 1.6 %collective-permute-done.13 = f32[8,16,256]{2,1,0:T(8,128)S(1)} collective-permute-done((f32[8,16,256]{2,1,0:T(8,128)S(1)}, f32[8,16,256]{2,1,0:T(8,128)S(1)}, u32[]{:S(2)}, u32[]{:S(2)}) %collective-permute-start.13) | collective-permute-done | bytes 131104 | tf_op jit(solution)/shard_map/ppermute | solution.py:379
  92.9 3.4 %all-to-all-start.2 = ((f32[8,16,256]{2,1,0:T(8,128)}), f32[8,16,256]{2,1,0:T(8,128)S(1)}, u32[]{:S(2)}, u32[]{:S(2)}) async-start(f32[8,16,256]{2,1,0:T(8,128)} %fusion), calls=%async_computation.2 | async-start | bytes 262144 | tf_op jit(solution)/shard_map/all_to_all | solution.py:416
  96.3 3.7 %row_system.1 = (f32[256,256]{1,0:T(8,128)S(1)}, f32[8,128]{1,0:T(8,128)S(1)}) custom-call(f32[128,256]{1,0:T(8,128)S(1)} %copy-done.5, f32[128,256]{1,0:T(8,128)S(1)} %ordered_sum.1.mine, f32[128,256]{1,0:T(8,128)S(1)} %collective-permute-done.19.other), custom_call_target="tpu_custom_call" | custom-call | flops 3000000000 | bytes 1000000 | tf_op jit(solution)/shard_map/row_system/pallas_call | solution.py:256
  100.0 5.3 %all-to-all-done.2 = f32[8,16,256]{2,1,0:T(8,128)S(1)} async-done(((f32[8,16,256]{2,1,0:T(8,128)}), f32[8,16,256]{2,1,0:T(8,128)S(1)}, u32[]{:S(2)}, u32[]{:S(2)}) %all-to-all-start.2) | async-done | bytes 131104 | tf_op jit(solution)/shard_map/all_to_all | solution.py:416
  106.2 2.6 %collective-permute-start.21 = (f32[16,256]{1,0:T(8,128)S(1)}, f32[16,256]{1,0:T(8,128)S(1)}, u32[]{:S(2)}, u32[]{:S(2)}) collective-permute-start(f32[16,256]{1,0:T(8,128)S(1)} %reduce_sum.19.refs_0_), channel_id=1, source_target_pairs={{0,2},{1,3},{2,0},{3,1},{4,6},{5,7},{6,4},{7,5},{8,10},{9,11},{10,... | collective-permute-start | bytes 49160 | tf_op jit(solution)/shard_map/ppermute | solution.py:379
  108.9 2.5 %collective-permute-start.20 = (f32[16,256]{1,0:T(8,128)S(1)}, f32[16,256]{1,0:T(8,128)S(1)}, u32[]{:S(2)}, u32[]{:S(2)}) collective-permute-start(f32[16,256]{1,0:T(8,128)S(1)} %reduce_sum.19.refs_0_), channel_id=1, source_target_pairs={{0,1},{1,2},{2,3},{3,0},{4,5},{5,6},{6,7},{7,4},{8,9},{9,10},{10,1... | collective-permute-start | bytes 49160 | tf_op jit(solution)/shard_map/ppermute | solution.py:379
  111.5 1.4 %collective-permute-done.20.refs_1_ = f32[16,256]{1,0:T(8,128)S(1)} collective-permute-done((f32[16,256]{1,0:T(8,128)S(1)}, f32[16,256]{1,0:T(8,128)S(1)}, u32[]{:S(2)}, u32[]{:S(2)}) %collective-permute-start.20) | collective-permute-done | bytes 16416 | tf_op jit(solution)/shard_map/ppermute | solution.py:379
  (79 shorter events, 29.5 us)
Async XLA Ops:
  2.2 29.1 %all-to-all-start = ((f32[32,16,256]{2,1,0:T(8,128)}), f32[32,16,256]{2,1,0:T(8,128)S(1)}, u32[]{:S(2)}, u32[]{:S(2)}) async-start(f32[32,16,256]{2,1,0:T(8,128)} %broadcast_in_dim.4), calls=%async_computation | async-start | bytes 1048576 | tf_op jit(solution)/shard_map/all_to_all | solution.py:388
  31.3 1.9 %collective-permute-start = (f32[32,16,256]{2,1,0:T(8,128)S(1)}, f32[32,16,256]{2,1,0:T(8,128)S(1)}, u32[]{:S(2)}, u32[]{:S(2)}) collective-permute-start(f32[32,16,256]{2,1,0:T(8,128)S(1)} %all-to-all-done.mine), channel_id=1, source_target_pairs={{0,4},{4,0},{1,5},{5,1},{2,6},{6,2},{3,7},{7,3},{8,12},{12,8},{9,1... | collective-permute-start | bytes 1572872 | tf_op jit(solution)/shard_map/ppermute | solution.py:379
  34.4 1.4 %collective-permute-start.1 = (f32[4,32,256]{2,1,0:T(8,128)S(1)}, f32[4,32,256]{2,1,0:T(8,128)S(1)}, u32[]{:S(2)}, u32[]{:S(2)}) collective-permute-start(f32[4,32,256]{2,1,0:T(8,128)S(1)} %get-tuple-element.34), channel_id=1, source_target_pairs={{0,4},{4,0},{1,5},{5,1},{2,6},{6,2},{3,7},{7,3},{8,12},{12,8},{9,1... | collective-permute-start | bytes 393224 | tf_op jit(solution)/shard_map/ppermute | solution.py:379
  35.9 5.5 %collective-permute-start.3 = (f32[32,256]{1,0:T(8,128)S(1)}, f32[32,256]{1,0:T(8,128)S(1)}, u32[]{:S(2)}, u32[]{:S(2)}) collective-permute-start(f32[32,256]{1,0:T(8,128)S(1)} %get-tuple-element.53), channel_id=1, source_target_pairs={{0,16},{8,24},{16,0},{24,8},{1,17},{9,25},{17,1},{25,9},{2,18},{10... | collective-permute-start | bytes 98312 | tf_op jit(solution)/shard_map/ppermute | solution.py:379
  38.5 3.9 %collective-permute-start.4 = (f32[32,256]{1,0:T(8,128)S(1)}, f32[32,256]{1,0:T(8,128)S(1)}, u32[]{:S(2)}, u32[]{:S(2)}) collective-permute-start(f32[32,256]{1,0:T(8,128)S(1)} %get-tuple-element.54), channel_id=1, source_target_pairs={{0,24},{8,0},{16,8},{24,16},{1,25},{9,1},{17,9},{25,17},{2,26},{10... | collective-permute-start | bytes 98312 | tf_op jit(solution)/shard_map/ppermute | solution.py:379
  39.7 5.1 %collective-permute-start.2 = (f32[32,256]{1,0:T(8,128)S(1)}, f32[32,256]{1,0:T(8,128)S(1)}, u32[]{:S(2)}, u32[]{:S(2)}) collective-permute-start(f32[32,256]{1,0:T(8,128)S(1)} %get-tuple-element.55), channel_id=1, source_target_pairs={{0,8},{8,16},{16,24},{24,0},{1,9},{9,17},{17,25},{25,1},{2,10},{10... | collective-permute-start | bytes 98312 | tf_op jit(solution)/shard_map/ppermute | solution.py:379
  45.5 17.2 %all-to-all-start.1 = ((f32[8,32,256]{2,1,0:T(8,128)}), f32[8,32,256]{2,1,0:T(8,128)}, u32[]{:S(2)}, u32[]{:S(2)}) async-start(f32[8,32,256]{2,1,0:T(8,128)} %broadcast_in_dim.5), calls=%async_computation.1 | async-start | bytes 524288 | tf_op jit(solution)/shard_map/all_to_all | solution.py:388
  63.7 4.0 %collective-permute-start.7 = (f32[32,256]{1,0:T(8,128)S(1)}, f32[32,256]{1,0:T(8,128)S(1)}, u32[]{:S(2)}, u32[]{:S(2)}) collective-permute-start(f32[32,256]{1,0:T(8,128)S(1)} %reduce_sum.18.refs_0_), channel_id=1, source_target_pairs={{0,24},{8,0},{16,8},{24,16},{1,25},{9,1},{17,9},{25,17},{2,26},{10... | collective-permute-start | bytes 98312 | tf_op jit(solution)/shard_map/ppermute | solution.py:379
  64.4 5.4 %collective-permute-start.6 = (f32[32,256]{1,0:T(8,128)S(1)}, f32[32,256]{1,0:T(8,128)S(1)}, u32[]{:S(2)}, u32[]{:S(2)}) collective-permute-start(f32[32,256]{1,0:T(8,128)S(1)} %reduce_sum.18.refs_0_), channel_id=1, source_target_pairs={{0,16},{8,24},{16,0},{24,8},{1,17},{9,25},{17,1},{25,9},{2,18},{10... | collective-permute-start | bytes 98312 | tf_op jit(solution)/shard_map/ppermute | solution.py:379
  65.7 5.1 %collective-permute-start.5 = (f32[32,256]{1,0:T(8,128)S(1)}, f32[32,256]{1,0:T(8,128)S(1)}, u32[]{:S(2)}, u32[]{:S(2)}) collective-permute-start(f32[32,256]{1,0:T(8,128)S(1)} %reduce_sum.18.refs_0_), channel_id=1, source_target_pairs={{0,8},{8,16},{16,24},{24,0},{1,9},{9,17},{17,25},{25,1},{2,10},{10... | collective-permute-start | bytes 98312 | tf_op jit(solution)/shard_map/ppermute | solution.py:379
  65.8 5.0 %collective-permute-start.8 = (f32[32,256]{1,0:T(8,128)S(1)}, f32[32,256]{1,0:T(8,128)S(1)}, u32[]{:S(2)}, u32[]{:S(2)}) collective-permute-start(f32[32,256]{1,0:T(8,128)S(1)} %reduce_sum.18.refs_0_), channel_id=1, source_target_pairs={{0,4},{4,0},{1,5},{5,1},{2,6},{6,2},{3,7},{7,3},{8,12},{12,8},{9,1... | collective-permute-start | bytes 98312 | tf_op jit(solution)/shard_map/ppermute | solution.py:379
  67.7 3.2 %collective-permute-start.11 = (f32[32,256]{1,0:T(8,128)S(1)}, f32[32,256]{1,0:T(8,128)S(1)}, u32[]{:S(2)}, u32[]{:S(2)}) collective-permute-start(f32[32,256]{1,0:T(8,128)S(1)} %collective-permute-done.7.refs_3_), channel_id=1, source_target_pairs={{0,4},{4,0},{1,5},{5,1},{2,6},{6,2},{3,7},{7,3},{8,12},{12,8},{9,1... | collective-permute-start | bytes 98312 | tf_op jit(solution)/shard_map/ppermute | solution.py:379
  77.2 5.1 %collective-permute-start.12 = (f32[4,8,16,256]{3,2,1,0:T(8,128)S(1)}, f32[4,8,16,256]{3,2,1,0:T(8,128)S(1)}, u32[]{:S(2)}, u32[]{:S(2)}) collective-permute-start(f32[4,8,16,256]{3,2,1,0:T(8,128)S(1)} %get-tuple-element.40), channel_id=1, source_target_pairs={{0,4},{4,0},{1,5},{5,1},{2,6},{6,2},{3,7},{7,3},{8,12},{12,8},{9,1... | collective-permute-start | bytes 1572872 | tf_op jit(solution)/shard_map/ppermute | solution.py:379
  77.3 8.6 %collective-permute-start.18 = (f32[128,256]{1,0:T(8,128)S(1)}, f32[128,256]{1,0:T(8,128)S(1)}, u32[]{:S(2)}, u32[]{:S(2)}) collective-permute-start(f32[128,256]{1,0:T(8,128)S(1)} %get-tuple-element.41.refs_0_), channel_id=1, source_target_pairs={{0,3},{1,0},{2,1},{3,2},{4,7},{5,4},{6,5},{7,6},{8,11},{9,8},{10,9... | collective-permute-start | bytes 393224 | tf_op jit(solution)/shard_map/ppermute | solution.py:379
  77.8 9.1 %collective-permute-start.17 = (f32[128,256]{1,0:T(8,128)S(1)}, f32[128,256]{1,0:T(8,128)S(1)}, u32[]{:S(2)}, u32[]{:S(2)}) collective-permute-start(f32[128,256]{1,0:T(8,128)S(1)} %get-tuple-element.41.refs_0_), channel_id=1, source_target_pairs={{0,2},{1,3},{2,0},{3,1},{4,6},{5,7},{6,4},{7,5},{8,10},{9,11},{10,... | collective-permute-start | bytes 393224 | tf_op jit(solution)/shard_map/ppermute | solution.py:379
  80.4 7.3 %collective-permute-start.16 = (f32[128,256]{1,0:T(8,128)S(1)}, f32[128,256]{1,0:T(8,128)S(1)}, u32[]{:S(2)}, u32[]{:S(2)}) collective-permute-start(f32[128,256]{1,0:T(8,128)S(1)} %get-tuple-element.41.refs_0_), channel_id=1, source_target_pairs={{0,1},{1,2},{2,3},{3,0},{4,5},{5,6},{6,7},{7,4},{8,9},{9,10},{10,1... | collective-permute-start | bytes 393224 | tf_op jit(solution)/shard_map/ppermute | solution.py:379
  82.4 8.0 %collective-permute-start.14 = (f32[8,16,256]{2,1,0:T(8,128)S(1)}, f32[8,16,256]{2,1,0:T(8,128)S(1)}, u32[]{:S(2)}, u32[]{:S(2)}) collective-permute-start(f32[8,16,256]{2,1,0:T(8,128)S(1)} %get-tuple-element.50), channel_id=1, source_target_pairs={{0,16},{8,24},{16,0},{24,8},{1,17},{9,25},{17,1},{25,9},{2,18},{10... | collective-permute-start | bytes 393224 | tf_op jit(solution)/shard_map/ppermute | solution.py:379
  83.4 7.1 %collective-permute-start.15 = (f32[8,16,256]{2,1,0:T(8,128)S(1)}, f32[8,16,256]{2,1,0:T(8,128)S(1)}, u32[]{:S(2)}, u32[]{:S(2)}) collective-permute-start(f32[8,16,256]{2,1,0:T(8,128)S(1)} %get-tuple-element.51), channel_id=1, source_target_pairs={{0,24},{8,0},{16,8},{24,16},{1,25},{9,1},{17,9},{25,17},{2,26},{10... | collective-permute-start | bytes 393224 | tf_op jit(solution)/shard_map/ppermute | solution.py:379
  85.9 6.3 %collective-permute-start.13 = (f32[8,16,256]{2,1,0:T(8,128)S(1)}, f32[8,16,256]{2,1,0:T(8,128)S(1)}, u32[]{:S(2)}, u32[]{:S(2)}) collective-permute-start(f32[8,16,256]{2,1,0:T(8,128)S(1)} %get-tuple-element.52), channel_id=1, source_target_pairs={{0,8},{8,16},{16,24},{24,0},{1,9},{9,17},{17,25},{25,1},{2,10},{10... | collective-permute-start | bytes 393224 | tf_op jit(solution)/shard_map/ppermute | solution.py:379
  87.8 8.5 %collective-permute-start.19 = (f32[128,256]{1,0:T(8,128)S(1)}, f32[128,256]{1,0:T(8,128)S(1)}, u32[]{:S(2)}, u32[]{:S(2)}) collective-permute-start(f32[128,256]{1,0:T(8,128)S(1)} %ordered_sum.1.mine), channel_id=1, source_target_pairs={{0,4},{4,0},{1,5},{5,1},{2,6},{6,2},{3,7},{7,3},{8,12},{12,8},{9,1... | collective-permute-start | bytes 393224 | tf_op jit(solution)/shard_map/ppermute | solution.py:379
  92.9 12.4 %all-to-all-start.2 = ((f32[8,16,256]{2,1,0:T(8,128)}), f32[8,16,256]{2,1,0:T(8,128)S(1)}, u32[]{:S(2)}, u32[]{:S(2)}) async-start(f32[8,16,256]{2,1,0:T(8,128)} %fusion), calls=%async_computation.2 | async-start | bytes 262144 | tf_op jit(solution)/shard_map/all_to_all | solution.py:416
  105.3 6.1 %collective-permute-start.22 = (f32[16,256]{1,0:T(8,128)S(1)}, f32[16,256]{1,0:T(8,128)S(1)}, u32[]{:S(2)}, u32[]{:S(2)}) collective-permute-start(f32[16,256]{1,0:T(8,128)S(1)} %reduce_sum.19.refs_0_), channel_id=1, source_target_pairs={{0,3},{1,0},{2,1},{3,2},{4,7},{5,4},{6,5},{7,6},{8,11},{9,8},{10,9... | collective-permute-start | bytes 49160 | tf_op jit(solution)/shard_map/ppermute | solution.py:379
  106.2 5.2 %collective-permute-start.21 = (f32[16,256]{1,0:T(8,128)S(1)}, f32[16,256]{1,0:T(8,128)S(1)}, u32[]{:S(2)}, u32[]{:S(2)}) collective-permute-start(f32[16,256]{1,0:T(8,128)S(1)} %reduce_sum.19.refs_0_), channel_id=1, source_target_pairs={{0,2},{1,3},{2,0},{3,1},{4,6},{5,7},{6,4},{7,5},{8,10},{9,11},{10,... | collective-permute-start | bytes 49160 | tf_op jit(solution)/shard_map/ppermute | solution.py:379
  108.9 4.0 %collective-permute-start.20 = (f32[16,256]{1,0:T(8,128)S(1)}, f32[16,256]{1,0:T(8,128)S(1)}, u32[]{:S(2)}, u32[]{:S(2)}) collective-permute-start(f32[16,256]{1,0:T(8,128)S(1)} %reduce_sum.19.refs_0_), channel_id=1, source_target_pairs={{0,1},{1,2},{2,3},{3,0},{4,5},{5,6},{6,7},{7,4},{8,9},{9,10},{10,1... | collective-permute-start | bytes 49160 | tf_op jit(solution)/shard_map/ppermute | solution.py:379
  (19 other events, 215.0 us)

commit v2 on v1

--- a/solution.py
+++ b/solution.py
@@ -1,3 +1,4 @@
+import functools
 import math
 
 import jax
@@ -8,6 +9,7 @@
 from jax.experimental.pallas import tpu as pltpu
 from jax.sharding import Mesh
 from jax.sharding import PartitionSpec as P
+
 
 ROWS = 4096
 KEEP = 1024
@@ -35,7 +37,7 @@
     eight = np.arange(8)[:, None] * lanes
     ahead = [f(a) for a in (np.pi * eight / 4, np.pi * (2 * eight + 1) / 8) for f in (np.cos, np.sin)]
     turn = np.pi * (2 * eight + 1) / 8192
-    tables = base + [np.stack(ahead + [np.cos(turn), np.sin(turn)])]
+    tables = np.stack(base), np.stack(ahead + [np.cos(turn), np.sin(turn)])
     return [jnp.asarray(table.astype(np.float32)) for table in tables]
 
 
@@ -74,16 +76,15 @@
 
 
 def dct_kernel(x0, x1, x2, x3, *refs):
-    base, ahead, outs = refs[:4], refs[4], refs[5:9]
-    held, rotated, total = refs[9:13], refs[13:15], refs[15]
+    base, ahead, outs = refs[0], refs[1], refs[2:6]
+    held, rotated, total = refs[6], refs[7:9], refs[9]
     high, low, high_t, low_t = outs
     step = pl.program_id(0)
 
     @pl.when(step == 0)
     def _():
         total[...] = jnp.zeros_like(total)
-        for ref, first in zip(held, base):
-            ref[...] = first[...]
+        held[...] = base[...]
         cos, sin = ahead[4], ahead[5]
         for t in range(STEP // 8):
             by_cos, by_sin = math.cos(math.pi * t / 512), math.sin(math.pi * t / 512)
@@ -93,17 +94,17 @@
     @pl.when(step > 0)
     def _():
         for pair in range(2):
-            cos, sin = held[2 * pair][...], held[2 * pair + 1][...]
+            cos, sin = held[2 * pair], held[2 * pair + 1]
             by_cos = jnp.concatenate([twice(ahead[2 * pair])] * 32, axis=0)
             by_sin = jnp.concatenate([twice(ahead[2 * pair + 1])] * 32, axis=0)
-            held[2 * pair][...] = cos * by_cos - sin * by_sin
-            held[2 * pair + 1][...] = sin * by_cos + cos * by_sin
+            held[2 * pair] = cos * by_cos - sin * by_sin
+            held[2 * pair + 1] = sin * by_cos + cos * by_sin
         cos, sin = rotated[0][...], rotated[1][...]
         by_cos, by_sin = math.cos(math.pi / 16), math.sin(math.pi / 16)
         rotated[0][...] = cos * by_cos - sin * by_sin
         rotated[1][...] = sin * by_cos + cos * by_sin
 
-    plain, even, odd = split(held[0][...]), split(held[2][...]), split(held[3][...])
+    plain, even, odd = split(held[0]), split(held[2]), split(held[3])
     cos, sin = twice(rotated[0][...]), twice(rotated[1][...])
     for s in range(2):
         first, third = x0[s], x2[s]
@@ -130,7 +131,6 @@
     tables = twiddles()
     steps = PART // STEP
     block = (2, STEP, COLS)
-    square = pltpu.VMEM((BAND, STEP), F32)
     turn = pltpu.VMEM((STEP, 128), F32)
     straight = jax.ShapeDtypeStruct((2, 4, BAND, COLS), BF16)
     crossed = jax.ShapeDtypeStruct((2, COLS, KEEP), BF16)
@@ -150,15 +150,30 @@
         + [whole(table.shape) for table in tables],
         out_specs=[whole(a.shape) for a in (straight, straight, crossed, crossed)],
         out_shape=[straight, straight, crossed, crossed],
-        scratch_shapes=[square] * 4 + [turn] * 2 + [pltpu.VMEM((2, 4, BAND, COLS), F32)],
+        scratch_shapes=[
+            pltpu.VMEM((4, BAND, STEP), F32),
+            turn,
+            turn,
+            pltpu.VMEM((2, 4, BAND, COLS), F32),
+        ],
         cost_estimate=pl.CostEstimate(flops=7_000_000_000, bytes_accessed=13_000_000, transcendentals=0),
-        compiler_params=room(24),
+        compiler_params=room(46),
         name="dct",
     )(*([snapshots] * 4), *tables)
 
 
 def place_of_own():
     return tuple(lax.axis_index(name) for name in ("z", "x", "c", "y"))
+
+
+FLIPS = (0, 3, 1, 2)
+
+
+def flipped(position, flip):
+    high, low = position // 2, position % 2
+    high = 1 - high if flip // 2 else high
+    low = 1 - low if flip % 2 else low
+    return 2 * high + low
 
 
 def own_weights(snap, z, x, core):
@@ -186,11 +201,10 @@
             sums[s] += dot3((high_t[s, :, place], low_t[s, :, place]), lines)
     weights = own_weights(snap, z, x, core)
     total[...] = sums[0] * weights[0] + sums[1] * weights[1]
-    for shift in range(NX):
-        target = lax.rem(x + shift, NX)
+    for at, flip in enumerate(FLIPS):
         for ref, owner in ((keep, core), (send, 1 - core)):
-            start = pl.multiple_of(owner * 128 + target * 32, 32)
-            ref[shift] = total[pl.ds(start, 32), :]
+            start = pl.multiple_of(owner * 128 + flipped(x, flip) * 32, 32)
+            ref[at] = total[pl.ds(start, 32), :]
 
 
 def totals(high_t, low_t, snap, mine, other):
@@ -252,7 +266,7 @@
     pen[...] = jnp.full((8, 128), penalty, F32)
 
 
-def system(kernel, snap, mine, other, scratch, name):
+def system(kernel, snap, mine, other, scratch):
     return pl.pallas_call(
         kernel,
         in_specs=[VMEM] * 3,
@@ -264,7 +278,6 @@
         scratch_shapes=[pltpu.VMEM(scratch, F32), pltpu.VMEM((2 * RANK, RANK), F32)],
         cost_estimate=pl.CostEstimate(flops=3_000_000_000, bytes_accessed=1_000_000, transcendentals=0),
         compiler_params=room(8),
-        name=name,
     )(snap, mine, other)
 
 
@@ -289,11 +302,10 @@
     total, mapped, gram = refs[13:]
     z, x, core, _ = place_of_own()
     for side in range(NC):
-        for shift in range(NX):
-            source = lax.rem(x - shift + NX, NX)
+        for at, flip in enumerate(FLIPS):
             owner = core if side == 0 else 1 - core
-            start = pl.multiple_of(owner * 128 + source * 32, 32)
-            total[pl.ds(start, 32), :] = pieces[side * NX + shift][...]
+            start = pl.multiple_of(owner * 128 + flipped(x, flip) * 32, 32)
+            total[pl.ds(start, 32), :] = pieces[side * NX + at][...]
     admm_update(total, inv, pen[0, 0], factor, dual, new, dual_new)
     primal = new[...]
     gram[...] = exact(primal.T, primal)
@@ -331,92 +343,125 @@
     )(high, low, snap, inv, pen, factor, dual, *pieces)
 
 
-def in_order(parts, held):
-    y = lax.axis_index("y")
-    for shift in range(NY):
-        held[lax.rem(y - shift + NY, NY)] = parts[shift][...]
-    return (held[0] + held[1]) + (held[2] + held[3])
-
-
-def sum_kernel(*refs):
-    parts, out, held = refs[:4], refs[4], refs[5]
-    out[...] = in_order(parts, held)
-
-
-def ordered_sum(parts):
-    shape = parts[0].shape
-    return pl.pallas_call(
-        sum_kernel,
-        in_specs=[VMEM] * 4,
-        out_specs=VMEM,
-        out_shape=jax.ShapeDtypeStruct(shape, F32),
-        scratch_shapes=[pltpu.VMEM((NY, *shape), F32)],
-        compiler_params=room(4),
-        name="ordered_sum",
-    )(*parts)
-
-
-def row_kernel(inv, pen, factor, dual, *refs):
-    parts, (new, dual_new), held = refs[:4], refs[4:6], refs[6]
-    held[0] = in_order(parts, held)
-    admm_update(held.at[0], inv, pen[0, 0], factor, dual, new, dual_new)
-
-
-def row_update(inv, pen, factor, dual, parts):
+def row_kernel(inv, pen, factor, dual, mine, other, new, dual_new, sums):
+    sums[...] = mine[...] + other[...]
+    admm_update(sums, inv, pen[0, 0], factor, dual, new, dual_new)
+
+
+def row_update(inv, pen, factor, dual, mine, other):
     own = jax.ShapeDtypeStruct((16, RANK), F32)
     return pl.pallas_call(
         row_kernel,
-        in_specs=[VMEM] * 8,
+        in_specs=[VMEM] * 6,
         out_specs=[VMEM] * 2,
         out_shape=[own] * 2,
-        scratch_shapes=[pltpu.VMEM((NY, 16, RANK), F32)],
+        scratch_shapes=[pltpu.VMEM((16, RANK), F32)],
         compiler_params=room(4),
         name="row_update",
-    )(inv, pen, factor, dual, *parts)
+    )(inv, pen, factor, dual, mine, other)
 
 
 def shifted(array, axis, size, by):
     return lax.ppermute(array, axis, [(i, (i + by) % size) for i in range(size)])
 
 
-def from_all(array, axis, size):
-    return [array] + [shifted(array, axis, size, by) for by in range(1, size)]
-
-
-def copied_along(array, axes, size):
-    whole = jnp.broadcast_to(array[None], (size, *array.shape))
+def swapped(array, axis, flip):
+    return lax.ppermute(array, axis, [(i, i ^ flip) for i in range(4)])
+
+
+def sum_kernel(count, *refs):
+    total = refs[0][...]
+    for ref in refs[1:count]:
+        total = total + ref[...]
+    outs = refs[count:]
+    for at, out in enumerate(outs):
+        share = total.shape[0] // len(outs)
+        own = total if len(outs) == 1 else total[at * share : (at + 1) * share]
+        out[...] = own.reshape(out.shape)
+
+
+def summed(parts, shape, count=1):
+    return pl.pallas_call(
+        functools.partial(sum_kernel, len(parts)),
+        in_specs=[VMEM] * len(parts),
+        out_specs=[VMEM] * count,
+        out_shape=[jax.ShapeDtypeStruct(shape, F32)] * count,
+        compiler_params=room(8),
+        name="summed",
+    )(*parts)
+
+
+def spread_kernel(count, *refs):
+    total = refs[0][...]
+    for ref in refs[1:count]:
+        total = total + ref[...]
+    for at in range(refs[count].shape[0]):
+        refs[count][at] = total
+
+
+def copied_along(parts, axes, size):
+    whole = pl.pallas_call(
+        functools.partial(spread_kernel, len(parts)),
+        in_specs=[VMEM] * len(parts),
+        out_specs=VMEM,
+        out_shape=jax.ShapeDtypeStruct((size, *parts[0].shape), F32),
+        compiler_params=room(8),
+        name="spread",
+    )(*parts)
     return lax.all_to_all(whole, axes, 0, 0, tiled=True)
 
 
+def fold_kernel(block, out):
+    half = [block[at] + block[at + 1] for at in range(0, NZ, 2)]
+    out[...] = (half[0] + half[1]) + (half[2] + half[3])
+
+
+def folded(block):
+    return pl.pallas_call(
+        fold_kernel,
+        in_specs=[VMEM],
+        out_specs=VMEM,
+        out_shape=jax.ShapeDtypeStruct(block.shape[1:], F32),
+        compiler_params=room(4),
+        name="folded",
+    )(block)
+
+
 def body(snapshots, snap_factor, row_factor, col_factor, row_dual, col_dual):
-    mine = copied_along(row_factor, ("z", "x"), NZ * NX)
+    mine = copied_along([row_factor], ("z", "x"), NZ * NX)
     high, low, high_t, low_t = dct(snapshots)
     mine, high_t = lax.optimization_barrier((mine, high_t))
     other = shifted(mine, "c", NC, 1)
     keep, send = totals(high_t, low_t, snap_factor, mine, other)
-    inv, pen = system(
-        col_system_kernel, snap_factor, mine, other, (2, KEEP, 128), "col_system"
-    )
-    half = keep + shifted(send, "c", NC, 1)
-    chunk = half[0] + sum(shifted(half[by], "x", NX, by) for by in range(1, NX))
-    chunk = copied_along(chunk, "z", NZ)
-    chunk, inv = lax.optimization_barrier((chunk, inv))
-    pieces = from_all(chunk.sum(axis=0), "x", NX)
+    inv, pen = system(col_system_kernel, snap_factor, mine, other, (2, KEEP, 128))
+    line = (32, RANK)
+    near, far = summed([keep, shifted(send, "c", NC, 1)], (2, *line), 2)
+    near, far = summed([near, swapped(far, "x", 1)], line, 2)
+    chunk = copied_along([near, swapped(far, "x", 3)], "z", NZ)
+    chunk, pen = lax.optimization_barrier((chunk, pen))
+    chunk = folded(chunk)
+    across = swapped(chunk, "x", 3)
+    pieces = [chunk, across, swapped(chunk, "x", 1), swapped(across, "x", 1)]
     pieces = pieces + [shifted(piece, "c", NC, 1) for piece in pieces]
     col_new, col_dual_new, keep, send, gram_half = col_update(
         high, low, snap_factor, inv, pen, col_factor, col_dual, pieces
     )
-    gram_mine = ordered_sum(from_all(gram_half, "y", NY))
+    blocks = summed([keep, shifted(send, "c", NC, 1)], (NZ, 16, RANK), NX)
+    moved = []
+    for by in range(1, NX):
+        moved.append(shifted(blocks[by], "x", NX, by))
+    gram_near = swapped(gram_half, "y", 1)
+    gram_near = summed([gram_half, gram_near], gram_half.shape)[0]
+    gram_mine = summed([gram_near, swapped(gram_near, "y", 3)], gram_half.shape)[0]
     gram_other = shifted(gram_mine, "c", NC, 1)
-    inv, pen = system(
-        row_system_kernel, snap_factor, gram_mine, gram_other, (RANK, RANK), "row_system"
-    )
-    half = keep + shifted(send, "c", NC, 1)
-    block = half[0] + sum(shifted(half[by], "x", NX, by) for by in range(1, NX))
+    inv, pen = system(row_system_kernel, snap_factor, gram_mine, gram_other, (RANK, RANK))
+    block = summed([blocks[0], *moved], (NZ, 16, RANK))[0]
     block = lax.all_to_all(block, "z", 0, 0, tiled=True)
-    block, inv = lax.optimization_barrier((block, inv))
+    block, pen = lax.optimization_barrier((block, pen))
+    mine = folded(block)
+    near = summed([mine, swapped(mine, "y", 1)], mine.shape)[0]
     row_new, row_dual_new = row_update(
-        inv, pen, row_factor, row_dual, from_all(block.sum(axis=0), "y", NY)
+        inv, pen, row_factor, row_dual, near, swapped(near, "y", 3)
     )
     return row_new, col_new, row_dual_new, col_dual_new
 

time: 116 us -> 119 us (1.026)
  the two profiles are of different devices: /device:TPU:8 before, /device:TPU:6 now
where the time goes in v2:
time: 119 us; the launch traced here: 118 us
  waiting for transfers between devices  54.4 us (46%)
  starting transfers between devices  30.2 us (25%)
  Pallas kernels  24.8 us (21%)
  local copies, waits for them, and re-layouts  7.81 us (7%)
    ppermute x9, waiting for transfers between devices, swapped(): return lax.ppermute(array, axis, [(i, i ^ flip) for i in range(4)])  28 us
    all_to_all x2, starting transfers between devices, copied_along(): return lax.all_to_all(whole, axes, 0, 0, tiled=True)  15 us
    ppermute x11, waiting for transfers between devices, shifted(): lax.ppermute(array, axis, [(i, (i + by) % size) for i in range(size)])  11 us
    all_to_all x2, waiting for transfers between devices, copied_along(): return lax.all_to_all(whole, axes, 0, 0, tiled=True)  10.2 us
    ppermute x9, starting transfers between devices, swapped(): return lax.ppermute(array, axis, [(i, i ^ flip) for i in range(4)])  8.68 us
    pallas_call x2, Pallas kernels, system(): pl.pallas_call(kernel, in_specs=[VMEM] * 3, out_specs=[VMEM] * 2, out_sha...  8.5 us
    pallas_call x1, Pallas kernels, dct(): pl.pallas_call(dct_kernel, grid=(steps,), in_specs=[pl.BlockSpec(block, l...  8.27 us
    unnamed x28, local copies, waits for them, and re-layouts  7.81 us
  transfers between devices with their start and end apart: 23, of which 17 were waited for; matrix products, arithmetic and copies ran while one was open for 0% of the time, Pallas kernels for 15%

profile of v2, /device:TPU:6, one launch (start us, length us, event | category | flops | bytes accessed | tf_op | source)
XLA Modules:
  0.0 118.1 jit_solution(11793196075418415676)
XLA Ops:
  2.2 11.6 %all-to-all-start = ((f32[32,16,256]{2,1,0:T(8,128)}), f32[32,16,256]{2,1,0:T(8,128)S(1)}, u32[]{:S(2)}, u32[]{:S(2)}) async-start(f32[32,16,256]{2,1,0:T(8,128)} %spread.2), calls=%async_computation | async-start | bytes 1048576 | tf_op jit(solution)/shard_map/all_to_all | solution.py:411
  15.8 8.3 %dct.1 = (bf16[2,4,256,256]{3,2,1,0:T(8,128)(2,1)S(1)}, bf16[2,4,256,256]{3,2,1,0:T(8,128)(2,1)S(1)}, bf16[2,256,1024]{2,1,0:T(8,128)(2,1)S(1)}, bf16[2,256,1024]{2,1,0:T(8,128)(2,1)S(1)}) custom-call(f32[2,4096,256]{2,1,0:T(8,128)} %x3.1, f32[2,4096,256]{2,1,0:T(8,128)} %x3.1, f32[2,4096,256]{2,1,0:T(8,128)} %x3.1, f32[2,4096,256]{2,1,0:T(8,128)} %x3.1, ...), custom_call_target="tpu_custom_call" | custom-call | flops 7000000000 | bytes 13000000 | tf_op jit(solution)/shard_map/dct/pallas_call | solution.py:141
  26.0 4.6 %all-to-all-done.mine = f32[32,16,256]{2,1,0:T(8,128)S(1)} async-done(((f32[32,16,256]{2,1,0:T(8,128)}), f32[32,16,256]{2,1,0:T(8,128)S(1)}, u32[]{:S(2)}, u32[]{:S(2)}) %all-to-all-start) | async-done | bytes 524320 | tf_op jit(solution)/shard_map/all_to_all | solution.py:411
  30.6 1.9 %collective-permute-done.other = f32[32,16,256]{2,1,0:T(8,128)S(1)} collective-permute-done((f32[32,16,256]{2,1,0:T(8,128)S(1)}, f32[32,16,256]{2,1,0:T(8,128)S(1)}, u32[]{:S(2)}, u32[]{:S(2)}) %collective-permute-start) | collective-permute-done | bytes 524320 | tf_op jit(solution)/shard_map/ppermute | solution.py:365
  36.1 3.4 %collective-permute-done.2.refs_1_ = f32[2,32,256]{2,1,0:T(8,128)S(1)} collective-permute-done((f32[2,32,256]{2,1,0:T(8,128)S(1)}, f32[2,32,256]{2,1,0:T(8,128)S(1)}, u32[]{:S(2)}, u32[]{:S(2)}) %collective-permute-start.2) | collective-permute-done | bytes 65568 | tf_op jit(solution)/shard_map/ppermute | solution.py:369
  40.8 4.0 %collective-permute-done.3.refs_1_ = f32[32,256]{1,0:T(8,128)S(1)} collective-permute-done((f32[32,256]{1,0:T(8,128)S(1)}, f32[32,256]{1,0:T(8,128)S(1)}, u32[]{:S(2)}, u32[]{:S(2)}) %collective-permute-start.3) | collective-permute-done | bytes 32800 | tf_op jit(solution)/shard_map/ppermute | solution.py:369
  45.4 3.4 %all-to-all-start.1 = ((f32[8,32,256]{2,1,0:T(8,128)}), f32[8,32,256]{2,1,0:T(8,128)S(1)}, u32[]{:S(2)}, u32[]{:S(2)}) async-start(f32[8,32,256]{2,1,0:T(8,128)} %spread.3), calls=%async_computation.1 | async-start | bytes 524288 | tf_op jit(solution)/shard_map/all_to_all | solution.py:411
  48.9 4.8 %shard_map.111 = (f32[256,256]{1,0:T(8,128)S(1)}, f32[8,128]{1,0:T(8,128)S(1)}) custom-call(f32[128,256]{1,0:T(8,128)S(1)} %copy-done.1, f32[32,16,256]{2,1,0:T(8,128)S(1)} %all-to-all-done.mine, f32[32,16,256]{2,1,0:T(8,128)S(1)} %collective-permute-done.other), custom_call_target="tpu_custom_call" | custom-call | flops 3000000000 | bytes 1000000 | tf_op jit(solution)/shard_map/pallas_call | solution.py:270
  53.7 5.6 %all-to-all-done.1.block = f32[8,32,256]{2,1,0:T(8,128)S(1)} async-done(((f32[8,32,256]{2,1,0:T(8,128)}), f32[8,32,256]{2,1,0:T(8,128)S(1)}, u32[]{:S(2)}, u32[]{:S(2)}) %all-to-all-start.1) | async-done | bytes 262176 | tf_op jit(solution)/shard_map/all_to_all | solution.py:411
  60.5 4.0 %collective-permute-done.4.refs_1_ = f32[32,256]{1,0:T(8,128)S(1)} collective-permute-done((f32[32,256]{1,0:T(8,128)S(1)}, f32[32,256]{1,0:T(8,128)S(1)}, u32[]{:S(2)}, u32[]{:S(2)}) %collective-permute-start.4) | collective-permute-done | bytes 32800 | tf_op jit(solution)/shard_map/ppermute | solution.py:369
  65.0 3.4 %collective-permute-done.6.refs_3_ = f32[32,256]{1,0:T(8,128)S(1)} collective-permute-done((f32[32,256]{1,0:T(8,128)S(1)}, f32[32,256]{1,0:T(8,128)S(1)}, u32[]{:S(2)}, u32[]{:S(2)}) %collective-permute-start.6) | collective-permute-done | bytes 32800 | tf_op jit(solution)/shard_map/ppermute | solution.py:369
  72.7 3.2 %col_update.1 = (f32[256,256]{1,0:T(8,128)}, f32[256,256]{1,0:T(8,128)}, f32[4,8,16,256]{3,2,1,0:T(8,128)S(1)}, f32[4,8,16,256]{3,2,1,0:T(8,128)S(1)}, f32[128,256]{1,0:T(8,128)S(1)}) custom-call(bf16[2,4,256,256]{3,2,1,0:T(8,128)(2,1)S(1)} %copy-done.7, bf16[2,4,256,256]{3,2,1,0:T(8,128)(2,1)S(1)} %copy-done.9, f32[128,256]{1,0:T(8,128)S(1)} %copy-done.1, ...), custom_call_target="tpu_custom_call" | custom-call | flops 1500000000 | bytes 5000000 | tf_op jit(solution)/shard_map/col_update/pallas_call | solution.py:330
  76.1 1.6 %collective-permute-start.11 = (f32[128,256]{1,0:T(8,128)S(1)}, f32[128,256]{1,0:T(8,128)S(1)}, u32[]{:S(2)}, u32[]{:S(2)}) collective-permute-start(f32[128,256]{1,0:T(8,128)S(1)} %get-tuple-element.51.refs_0_), channel_id=1, source_target_pairs={{0,1},{1,0},{2,3},{3,2},{4,5},{5,4},{6,7},{7,6},{8,9},{9,8},{10,11... | collective-permute-start | bytes 393224 | tf_op jit(solution)/shard_map/ppermute | solution.py:369
  77.7 4.2 %collective-permute-done.11.refs_1_ = f32[128,256]{1,0:T(8,128)S(1)} collective-permute-done((f32[128,256]{1,0:T(8,128)S(1)}, f32[128,256]{1,0:T(8,128)S(1)}, u32[]{:S(2)}, u32[]{:S(2)}) %collective-permute-start.11) | collective-permute-done | bytes 131104 | tf_op jit(solution)/shard_map/ppermute | solution.py:369
  81.9 3.1 %collective-permute-start.12 = (f32[128,256]{1,0:T(8,128)S(1)}, f32[128,256]{1,0:T(8,128)S(1)}, u32[]{:S(2)}, u32[]{:S(2)}) collective-permute-start(f32[128,256]{1,0:T(8,128)S(1)} %summed.9.refs_0_), channel_id=1, source_target_pairs={{0,3},{1,2},{2,1},{3,0},{4,7},{5,6},{6,5},{7,4},{8,11},{9,10},{10,... | collective-permute-start | bytes 393224 | tf_op jit(solution)/shard_map/ppermute | solution.py:369
  88.3 2.9 %collective-permute-done.15.refs_1_ = f32[8,16,256]{2,1,0:T(8,128)S(1)} collective-permute-done((f32[8,16,256]{2,1,0:T(8,128)S(1)}, f32[8,16,256]{2,1,0:T(8,128)S(1)}, u32[]{:S(2)}, u32[]{:S(2)}) %collective-permute-start.15) | collective-permute-done | bytes 131104 | tf_op jit(solution)/shard_map/ppermute | solution.py:365
  91.1 2.4 %collective-permute-done.16.refs_2_ = f32[8,16,256]{2,1,0:T(8,128)S(1)} collective-permute-done((f32[8,16,256]{2,1,0:T(8,128)S(1)}, f32[8,16,256]{2,1,0:T(8,128)S(1)}, u32[]{:S(2)}, u32[]{:S(2)}) %collective-permute-start.16) | collective-permute-done | bytes 131104 | tf_op jit(solution)/shard_map/ppermute | solution.py:365
  93.5 1.4 %collective-permute-done.17.refs_3_ = f32[8,16,256]{2,1,0:T(8,128)S(1)} collective-permute-done((f32[8,16,256]{2,1,0:T(8,128)S(1)}, f32[8,16,256]{2,1,0:T(8,128)S(1)}, u32[]{:S(2)}, u32[]{:S(2)}) %collective-permute-start.17) | collective-permute-done | bytes 131104 | tf_op jit(solution)/shard_map/ppermute | solution.py:365
  95.6 3.4 %all-to-all-start.2 = ((f32[8,16,256]{2,1,0:T(8,128)}), f32[8,16,256]{2,1,0:T(8,128)S(1)}, u32[]{:S(2)}, u32[]{:S(2)}) async-start(f32[8,16,256]{2,1,0:T(8,128)} %summed.12), calls=%async_computation.2 | async-start | bytes 262144 | tf_op jit(solution)/shard_map/all_to_all | solution.py:459
  99.0 3.7 %shard_map.112 = (f32[256,256]{1,0:T(8,128)S(1)}, f32[8,128]{1,0:T(8,128)S(1)}) custom-call(f32[128,256]{1,0:T(8,128)S(1)} %copy-done.1, f32[128,256]{1,0:T(8,128)S(1)} %summed.10.mine, f32[128,256]{1,0:T(8,128)S(1)} %collective-permute-done.13.other), custom_call_target="tpu_custom_call" | custom-call | flops 3000000000 | bytes 1000000 | tf_op jit(solution)/shard_map/pallas_call | solution.py:270
  102.7 5.3 %all-to-all-done.2.block = f32[8,16,256]{2,1,0:T(8,128)S(1)} async-done(((f32[8,16,256]{2,1,0:T(8,128)}), f32[8,16,256]{2,1,0:T(8,128)S(1)}, u32[]{:S(2)}, u32[]{:S(2)}) %all-to-all-start.2) | async-done | bytes 131104 | tf_op jit(solution)/shard_map/all_to_all | solution.py:459
  108.2 3.6 %collective-permute-done.18.refs_1_ = f32[16,256]{1,0:T(8,128)S(1)} collective-permute-done((f32[16,256]{1,0:T(8,128)S(1)}, f32[16,256]{1,0:T(8,128)S(1)}, u32[]{:S(2)}, u32[]{:S(2)}) %collective-permute-start.18) | collective-permute-done | bytes 16416 | tf_op jit(solution)/shard_map/ppermute | solution.py:369
  112.1 4.6 %collective-permute-done.19.other = f32[16,256]{1,0:T(8,128)S(1)} collective-permute-done((f32[16,256]{1,0:T(8,128)S(1)}, f32[16,256]{1,0:T(8,128)S(1)}, u32[]{:S(2)}, u32[]{:S(2)}) %collective-permute-start.19) | collective-permute-done | bytes 16416 | tf_op jit(solution)/shard_map/ppermute | solution.py:369
  116.8 1.3 %row_update.1 = (f32[16,256]{1,0:T(8,128)}, f32[16,256]{1,0:T(8,128)}) custom-call(f32[256,256]{1,0:T(8,128)S(1)} %get-tuple-element.52.inv, f32[8,128]{1,0:T(8,128)S(1)} %get-tuple-element.60.pen, f32[16,256]{1,0:T(8,128)S(1)} %copy-done.3, f32[16,256]{1,0:T(8,128)S(1)} %copy-done.5, f32[16,256]{1,0:T(8,128)S(1)} %summed.13.mine, ...), custom_call_target="tpu_custom_call" | custom-call | tf_op jit(solution)/shard_map/row_update/pallas_call | solution.py:353
  (67 shorter events, 21.9 us)
Async XLA Ops:
  2.2 28.4 %all-to-all-start = ((f32[32,16,256]{2,1,0:T(8,128)}), f32[32,16,256]{2,1,0:T(8,128)S(1)}, u32[]{:S(2)}, u32[]{:S(2)}) async-start(f32[32,16,256]{2,1,0:T(8,128)} %spread.2), calls=%async_computation | async-start | bytes 1048576 | tf_op jit(solution)/shard_map/all_to_all | solution.py:411
  26.0 43.6 %copy-start.10 = (f32[256,256]{1,0:T(8,128)S(1)}, f32[256,256]{1,0:T(8,128)}, u32[]{:S(2)}) copy-start(f32[256,256]{1,0:T(8,128)} %factor.2) | copy-start | bytes 786436
  30.6 1.9 %collective-permute-start = (f32[32,16,256]{2,1,0:T(8,128)S(1)}, f32[32,16,256]{2,1,0:T(8,128)S(1)}, u32[]{:S(2)}, u32[]{:S(2)}) collective-permute-start(f32[32,16,256]{2,1,0:T(8,128)S(1)} %all-to-all-done.mine), channel_id=1, source_target_pairs={{0,4},{4,0},{1,5},{5,1},{2,6},{6,2},{3,7},{7,3},{8,12},{12,8},{9,1... | collective-permute-start | bytes 1572872 | tf_op jit(solution)/shard_map/ppermute | solution.py:365
  33.7 1.4 %collective-permute-start.1 = (f32[4,32,256]{2,1,0:T(8,128)S(1)}, f32[4,32,256]{2,1,0:T(8,128)S(1)}, u32[]{:S(2)}, u32[]{:S(2)}) collective-permute-start(f32[4,32,256]{2,1,0:T(8,128)S(1)} %get-tuple-element.43), channel_id=1, source_target_pairs={{0,4},{4,0},{1,5},{5,1},{2,6},{6,2},{3,7},{7,3},{8,12},{12,8},{9,1... | collective-permute-start | bytes 393224 | tf_op jit(solution)/shard_map/ppermute | solution.py:365
  35.1 4.4 %collective-permute-start.2 = (f32[2,32,256]{2,1,0:T(8,128)S(1)}, f32[2,32,256]{2,1,0:T(8,128)S(1)}, u32[]{:S(2)}, u32[]{:S(2)}) collective-permute-start(f32[2,32,256]{2,1,0:T(8,128)S(1)} %get-tuple-element.45), channel_id=1, source_target_pairs={{0,8},{8,0},{16,24},{24,16},{1,9},{9,1},{17,25},{25,17},{2,10},{10... | collective-permute-start | bytes 196616 | tf_op jit(solution)/shard_map/ppermute | solution.py:369
  39.5 5.2 %collective-permute-start.3 = (f32[32,256]{1,0:T(8,128)S(1)}, f32[32,256]{1,0:T(8,128)S(1)}, u32[]{:S(2)}, u32[]{:S(2)}) collective-permute-start(f32[32,256]{1,0:T(8,128)S(1)} %get-tuple-element.47), channel_id=1, source_target_pairs={{0,24},{8,16},{16,8},{24,0},{1,25},{9,17},{17,9},{25,1},{2,26},{10... | collective-permute-start | bytes 98312 | tf_op jit(solution)/shard_map/ppermute | solution.py:369
  45.4 13.8 %all-to-all-start.1 = ((f32[8,32,256]{2,1,0:T(8,128)}), f32[8,32,256]{2,1,0:T(8,128)S(1)}, u32[]{:S(2)}, u32[]{:S(2)}) async-start(f32[8,32,256]{2,1,0:T(8,128)} %spread.3), calls=%async_computation.1 | async-start | bytes 524288 | tf_op jit(solution)/shard_map/all_to_all | solution.py:411
  59.3 5.2 %collective-permute-start.4 = (f32[32,256]{1,0:T(8,128)S(1)}, f32[32,256]{1,0:T(8,128)S(1)}, u32[]{:S(2)}, u32[]{:S(2)}) collective-permute-start(f32[32,256]{1,0:T(8,128)S(1)} %folded.2.refs_0_), channel_id=1, source_target_pairs={{0,24},{8,16},{16,8},{24,0},{1,25},{9,17},{17,9},{25,1},{2,26},{10... | collective-permute-start | bytes 98312 | tf_op jit(solution)/shard_map/ppermute | solution.py:369
  60.5 4.5 %collective-permute-start.5 = (f32[32,256]{1,0:T(8,128)S(1)}, f32[32,256]{1,0:T(8,128)S(1)}, u32[]{:S(2)}, u32[]{:S(2)}) collective-permute-start(f32[32,256]{1,0:T(8,128)S(1)} %folded.2.refs_0_), channel_id=1, source_target_pairs={{0,8},{8,0},{16,24},{24,16},{1,9},{9,1},{17,25},{25,17},{2,10},{10... | collective-permute-start | bytes 98312 | tf_op jit(solution)/shard_map/ppermute | solution.py:369
  64.5 3.9 %collective-permute-start.6 = (f32[32,256]{1,0:T(8,128)S(1)}, f32[32,256]{1,0:T(8,128)S(1)}, u32[]{:S(2)}, u32[]{:S(2)}) collective-permute-start(f32[32,256]{1,0:T(8,128)S(1)} %collective-permute-done.4.refs_1_), channel_id=1, source_target_pairs={{0,8},{8,0},{16,24},{24,16},{1,9},{9,1},{17,25},{25,17},{2,10},{10... | collective-permute-start | bytes 98312 | tf_op jit(solution)/shard_map/ppermute | solution.py:369
  64.5 3.9 %collective-permute-start.7 = (f32[32,256]{1,0:T(8,128)S(1)}, f32[32,256]{1,0:T(8,128)S(1)}, u32[]{:S(2)}, u32[]{:S(2)}) collective-permute-start(f32[32,256]{1,0:T(8,128)S(1)} %folded.2.refs_0_), channel_id=1, source_target_pairs={{0,4},{4,0},{1,5},{5,1},{2,6},{6,2},{3,7},{7,3},{8,12},{12,8},{9,1... | collective-permute-start | bytes 98312 | tf_op jit(solution)/shard_map/ppermute | solution.py:365
  64.5 3.9 %collective-permute-start.8 = (f32[32,256]{1,0:T(8,128)S(1)}, f32[32,256]{1,0:T(8,128)S(1)}, u32[]{:S(2)}, u32[]{:S(2)}) collective-permute-start(f32[32,256]{1,0:T(8,128)S(1)} %collective-permute-done.4.refs_1_), channel_id=1, source_target_pairs={{0,4},{4,0},{1,5},{5,1},{2,6},{6,2},{3,7},{7,3},{8,12},{12,8},{9,1... | collective-permute-start | bytes 98312 | tf_op jit(solution)/shard_map/ppermute | solution.py:365
  65.0 3.4 %collective-permute-start.9 = (f32[32,256]{1,0:T(8,128)S(1)}, f32[32,256]{1,0:T(8,128)S(1)}, u32[]{:S(2)}, u32[]{:S(2)}) collective-permute-start(f32[32,256]{1,0:T(8,128)S(1)} %collective-permute-done.5.refs_2_), channel_id=1, source_target_pairs={{0,4},{4,0},{1,5},{5,1},{2,6},{6,2},{3,7},{7,3},{8,12},{12,8},{9,1... | collective-permute-start | bytes 98312 | tf_op jit(solution)/shard_map/ppermute | solution.py:365
  68.4 1.2 %collective-permute-start.10 = (f32[32,256]{1,0:T(8,128)S(1)}, f32[32,256]{1,0:T(8,128)S(1)}, u32[]{:S(2)}, u32[]{:S(2)}) collective-permute-start(f32[32,256]{1,0:T(8,128)S(1)} %collective-permute-done.6.refs_3_), channel_id=1, source_target_pairs={{0,4},{4,0},{1,5},{5,1},{2,6},{6,2},{3,7},{7,3},{8,12},{12,8},{9,1... | collective-permute-start | bytes 98312 | tf_op jit(solution)/shard_map/ppermute | solution.py:365
  75.9 9.1 %collective-permute-start.14 = (f32[4,8,16,256]{3,2,1,0:T(8,128)S(1)}, f32[4,8,16,256]{3,2,1,0:T(8,128)S(1)}, u32[]{:S(2)}, u32[]{:S(2)}) collective-permute-start(f32[4,8,16,256]{3,2,1,0:T(8,128)S(1)} %get-tuple-element.54), channel_id=1, source_target_pairs={{0,4},{4,0},{1,5},{5,1},{2,6},{6,2},{3,7},{7,3},{8,12},{12,8},{9,1... | collective-permute-start | bytes 1572872 | tf_op jit(solution)/shard_map/ppermute | solution.py:365
  76.1 5.7 %collective-permute-start.11 = (f32[128,256]{1,0:T(8,128)S(1)}, f32[128,256]{1,0:T(8,128)S(1)}, u32[]{:S(2)}, u32[]{:S(2)}) collective-permute-start(f32[128,256]{1,0:T(8,128)S(1)} %get-tuple-element.51.refs_0_), channel_id=1, source_target_pairs={{0,1},{1,0},{2,3},{3,2},{4,5},{5,4},{6,7},{7,6},{8,9},{9,8},{10,11... | collective-permute-start | bytes 393224 | tf_op jit(solution)/shard_map/ppermute | solution.py:369
  81.9 6.3 %collective-permute-start.12 = (f32[128,256]{1,0:T(8,128)S(1)}, f32[128,256]{1,0:T(8,128)S(1)}, u32[]{:S(2)}, u32[]{:S(2)}) collective-permute-start(f32[128,256]{1,0:T(8,128)S(1)} %summed.9.refs_0_), channel_id=1, source_target_pairs={{0,3},{1,2},{2,1},{3,0},{4,7},{5,6},{6,5},{7,4},{8,11},{9,10},{10,... | collective-permute-start | bytes 393224 | tf_op jit(solution)/shard_map/ppermute | solution.py:369
  85.0 6.1 %collective-permute-start.15 = (f32[8,16,256]{2,1,0:T(8,128)S(1)}, f32[8,16,256]{2,1,0:T(8,128)S(1)}, u32[]{:S(2)}, u32[]{:S(2)}) collective-permute-start(f32[8,16,256]{2,1,0:T(8,128)S(1)} %get-tuple-element.56), channel_id=1, source_target_pairs={{0,8},{8,16},{16,24},{24,0},{1,9},{9,17},{17,25},{25,1},{2,10},{10... | collective-permute-start | bytes 393224 | tf_op jit(solution)/shard_map/ppermute | solution.py:365
  86.3 7.2 %collective-permute-start.16 = (f32[8,16,256]{2,1,0:T(8,128)S(1)}, f32[8,16,256]{2,1,0:T(8,128)S(1)}, u32[]{:S(2)}, u32[]{:S(2)}) collective-permute-start(f32[8,16,256]{2,1,0:T(8,128)S(1)} %get-tuple-element.57), channel_id=1, source_target_pairs={{0,16},{8,24},{16,0},{24,8},{1,17},{9,25},{17,1},{25,9},{2,18},{10... | collective-permute-start | bytes 393224 | tf_op jit(solution)/shard_map/ppermute | solution.py:365
  87.2 7.7 %collective-permute-start.17 = (f32[8,16,256]{2,1,0:T(8,128)S(1)}, f32[8,16,256]{2,1,0:T(8,128)S(1)}, u32[]{:S(2)}, u32[]{:S(2)}) collective-permute-start(f32[8,16,256]{2,1,0:T(8,128)S(1)} %get-tuple-element.58), channel_id=1, source_target_pairs={{0,24},{8,0},{16,8},{24,16},{1,25},{9,1},{17,9},{25,17},{2,26},{10... | collective-permute-start | bytes 393224 | tf_op jit(solution)/shard_map/ppermute | solution.py:365
  88.2 10.8 %collective-permute-start.13 = (f32[128,256]{1,0:T(8,128)S(1)}, f32[128,256]{1,0:T(8,128)S(1)}, u32[]{:S(2)}, u32[]{:S(2)}) collective-permute-start(f32[128,256]{1,0:T(8,128)S(1)} %summed.10.mine), channel_id=1, source_target_pairs={{0,4},{4,0},{1,5},{5,1},{2,6},{6,2},{3,7},{7,3},{8,12},{12,8},{9,1... | collective-permute-start | bytes 393224 | tf_op jit(solution)/shard_map/ppermute | solution.py:365
  95.6 12.4 %all-to-all-start.2 = ((f32[8,16,256]{2,1,0:T(8,128)}), f32[8,16,256]{2,1,0:T(8,128)S(1)}, u32[]{:S(2)}, u32[]{:S(2)}) async-start(f32[8,16,256]{2,1,0:T(8,128)} %summed.12), calls=%async_computation.2 | async-start | bytes 262144 | tf_op jit(solution)/shard_map/all_to_all | solution.py:459
  108.0 3.8 %collective-permute-start.18 = (f32[16,256]{1,0:T(8,128)S(1)}, f32[16,256]{1,0:T(8,128)S(1)}, u32[]{:S(2)}, u32[]{:S(2)}) collective-permute-start(f32[16,256]{1,0:T(8,128)S(1)} %folded.3.refs_0_), channel_id=1, source_target_pairs={{0,1},{1,0},{2,3},{3,2},{4,5},{5,4},{6,7},{7,6},{8,9},{9,8},{10,11... | collective-permute-start | bytes 49160 | tf_op jit(solution)/shard_map/ppermute | solution.py:369
  111.8 4.9 %collective-permute-start.19 = (f32[16,256]{1,0:T(8,128)S(1)}, f32[16,256]{1,0:T(8,128)S(1)}, u32[]{:S(2)}, u32[]{:S(2)}) collective-permute-start(f32[16,256]{1,0:T(8,128)S(1)} %summed.13.mine), channel_id=1, source_target_pairs={{0,3},{1,2},{2,1},{3,0},{4,7},{5,6},{6,5},{7,4},{8,11},{9,10},{10,... | collective-permute-start | bytes 49160 | tf_op jit(solution)/shard_map/ppermute | solution.py:369
  (13 other events, 158.2 us)

commit v3 on v2

v3 whole, which is shorter than its diff:
```python
import functools
import math

import jax
import jax.numpy as jnp
import numpy as np
from jax import lax
from jax.experimental import pallas as pl
from jax.experimental.pallas import tpu as pltpu
from jax.sharding import Mesh
from jax.sharding import PartitionSpec as P


ROWS = 4096
KEEP = 1024
RANK = 256
COLS = 256
ADMM_STEPS = 3
PART = ROWS // 4
BAND = KEEP // 4
HALF = BAND // 2
STEP = 256
NZ, NX, NC, NY = 8, 4, 2, 4
WIDE = ("z", "x", "c")
F32 = jnp.float32
BF16 = jnp.bfloat16
VMEM = pl.BlockSpec(memory_space=pltpu.VMEM)


def twiddles():
    odd = 2 * np.arange(STEP)[None, :] + 1
    half, group, low = np.meshgrid(np.arange(2), np.arange(32), np.arange(4), indexing="ij")
    degree = (8 * group + 4 * half + low).reshape(BAND, 1)
    scale = math.sqrt(2.0 / ROWS)
    angles = np.pi * odd * degree / 2048, np.pi * odd * (2 * degree + 1) / 4096
    weight = np.where(degree == 0, math.sqrt(1.0 / ROWS), scale), scale
    base = [w * f(a) for w, a in zip(weight, angles) for f in (np.cos, np.sin)]
    lanes = np.ones((1, 128))
    eight = np.arange(8)[:, None] * lanes
    near = np.stack([np.arange(8)[:, None] % 4 * lanes, np.arange(8)[:, None] % 4 * lanes + 4])
    ahead = [f(a) for a in (np.pi * near / 4, np.pi * (2 * near + 1) / 8) for f in (np.cos, np.sin)]
    turn = np.pi * (2 * eight + 1) / 8192
    tables = np.stack(base), np.concatenate([*ahead, [np.cos(turn), np.sin(turn)]])
    return [jnp.asarray(table.astype(np.float32)) for table in tables]


def room(mebibytes):
    return pltpu.CompilerParams(vmem_limit_bytes=mebibytes * 2**20)


def split(value):
    high = value.astype(BF16)
    return high, (value - high.astype(F32)).astype(BF16)


def dot(a, b):
    return jnp.dot(a, b, preferred_element_type=F32)


def dot3(a, b):
    return dot(a[0], b[0]) + (dot(a[1], b[0]) + dot(a[0], b[1]))


def exact(a, b):
    return jnp.dot(a, b, precision=lax.Precision.HIGHEST, preferred_element_type=F32)


def twice(value):
    return jnp.concatenate([value, value], axis=1)


def turned(ref, s):
    index = 7 - lax.broadcasted_iota(jnp.int32, (8, COLS), 0)
    tiles = []
    for t in range(STEP // 8):
        tile = ref[s, STEP - 8 * (t + 1) : STEP - 8 * t, :]
        tiles.append(jnp.take_along_axis(tile, index, axis=0, mode="promise_in_bounds"))
    return jnp.concatenate(tiles, axis=0)


def dct_kernel(x0, x1, x2, x3, *refs):
    base, ahead, keep, send = refs[:4]
    held, rotated, total = refs[4], refs[5:7], refs[7]
    step = pl.program_id(0)

    @pl.when(step == 0)
    def _():
        total[...] = jnp.zeros_like(total)
        held[...] = base[...]
        cos, sin = ahead[8], ahead[9]
        for t in range(STEP // 8):
            by_cos, by_sin = math.cos(math.pi * t / 512), math.sin(math.pi * t / 512)
            rotated[0][8 * t : 8 * t + 8, :] = cos * by_cos - sin * by_sin
            rotated[1][8 * t : 8 * t + 8, :] = sin * by_cos + cos * by_sin

    @pl.when(step > 0)
    def _():
        for pair in range(2):
            cos, sin = held[2 * pair], held[2 * pair + 1]
            by_cos, by_sin = (
                jnp.concatenate([twice(ahead[at])] * 16 + [twice(ahead[at + 1])] * 16, axis=0)
                for at in (4 * pair, 4 * pair + 2)
            )
            held[2 * pair] = cos * by_cos - sin * by_sin
            held[2 * pair + 1] = sin * by_cos + cos * by_sin
        cos, sin = rotated[0][...], rotated[1][...]
        by_cos, by_sin = math.cos(math.pi / 16), math.sin(math.pi / 16)
        rotated[0][...] = cos * by_cos - sin * by_sin
        rotated[1][...] = sin * by_cos + cos * by_sin

    plain, even, odd = split(held[0]), split(held[2]), split(held[3])
    cos, sin = twice(rotated[0][...]), twice(rotated[1][...])
    for s in range(2):
        first, third = x0[s], x2[s]
        second, fourth = turned(x1, s), turned(x3, s)
        outer, inner = first + fourth, second + third
        v, w = first - fourth, second - third
        total[s, 0] += dot3(plain, split(outer + inner))
        total[s, 2] += dot3(even, split(outer - inner))
        p = dot3(even, split(v * cos - w * sin))
        q = dot3(odd, split(v * sin + w * cos))
        total[s, 1] += p + q
        total[s, 3] += p - q

    @pl.when(step == pl.num_programs(0) - 1)
    def _():
        core = lax.axis_index("c")
        for ref, owner in ((keep, core), (send, 1 - core)):
            for s in range(2):
                for k in range(4):
                    ref[s, k] = total[s, k, pl.ds(pl.multiple_of(owner * HALF, HALF), HALF), :]


def dct(snapshots):
    tables = twiddles()
    steps = PART // STEP
    block = (2, STEP, COLS)
    turn = pltpu.VMEM((STEP, 128), F32)
    half = jax.ShapeDtypeStruct((2, 4, HALF, COLS), F32)

    def whole(shape):
        return pl.BlockSpec(shape, lambda i: (0,) * len(shape))

    return pl.pallas_call(
        dct_kernel,
        grid=(steps,),
        in_specs=[
            pl.BlockSpec(block, lambda i: (0, i, 0)),
            pl.BlockSpec(block, lambda i: (0, 2 * steps - 1 - i, 0)),
            pl.BlockSpec(block, lambda i: (0, 2 * steps + i, 0)),
            pl.BlockSpec(block, lambda i: (0, 4 * steps - 1 - i, 0)),
        ]
        + [whole(table.shape) for table in tables],
        out_specs=[whole(half.shape)] * 2,
        out_shape=[half] * 2,
        scratch_shapes=[
            pltpu.VMEM((4, BAND, STEP), F32),
            turn,
            turn,
            pltpu.VMEM((2, 4, BAND, COLS), F32),
        ],
        cost_estimate=pl.CostEstimate(flops=7_000_000_000, bytes_accessed=13_000_000, transcendentals=0),
        compiler_params=room(46),
        name="dct",
    )(*([snapshots] * 4), *tables)


def place_of_own():
    return tuple(lax.axis_index(name) for name in ("z", "x", "c", "y"))


def own_weights(snap, z, x, core):
    chip = (z * NX + x) * 4
    return [snap[pl.ds(chip + 2 * owner + s, 1), :] for owner in (core, 1 - core) for s in range(2)]


def prepare_kernel(own, other, snap, high, low, high_t, low_t, weights):
    z, x, core, _ = place_of_own()
    weights[...] = jnp.concatenate(own_weights(snap, z, x, core) * 2, axis=0)
    for s in range(4):
        source = own if s < 2 else other
        for k in range(4):
            value = source[s % 2, k]
            high[s, k], low[s, k] = split(value)
            place = slice(HALF * k, HALF * (k + 1))
            high_t[s, :, place], low_t[s, :, place] = split(value.T)


def prepare(own, other, snap):
    straight = jax.ShapeDtypeStruct((4, 4, HALF, COLS), BF16)
    crossed = jax.ShapeDtypeStruct((4, COLS, KEEP // 2), BF16)
    return pl.pallas_call(
        prepare_kernel,
        in_specs=[VMEM] * 3,
        out_specs=[VMEM] * 5,
        out_shape=[straight, straight, crossed, crossed, jax.ShapeDtypeStruct((8, RANK), F32)],
        compiler_params=room(12),
        cost_estimate=pl.CostEstimate(flops=10_000_000, bytes_accessed=6_000_000, transcendentals=0),
        name="prepare",
    )(own, other, snap)


def place_rows(x, pieces, rows):
    for shift in range(NX):
        source = lax.rem(x - shift + NX, NX)
        for z in range(NZ):
            start = pl.multiple_of(z * 64 + source * 16, 16)
            for half in range(2):
                rows[half, pl.ds(start, 16), :] = pieces[shift][z, :, 128 * half : 128 * half + 128]


def totals_kernel(high_t, low_t, weights, *refs):
    pieces, (keep, send), (rows, total) = refs[:4], refs[4:6], refs[6:]
    _, x, core, _ = place_of_own()
    place_rows(x, pieces, rows)
    sums = [0.0] * 4
    for k in range(4):
        line = [rows[half, pl.ds(k, HALF, stride=4), :] for half in range(2)]
        lines = split(jnp.concatenate(line, axis=1))
        place = slice(HALF * k, HALF * (k + 1))
        for s in range(4):
            sums[s] += dot3((high_t[s, :, place], low_t[s, :, place]), lines)
    total[...] = sum(part * weights[s : s + 1, :] for s, part in enumerate(sums))
    for shift in range(NX):
        target = lax.rem(x + shift, NX)
        for ref, owner in ((keep, core), (send, 1 - core)):
            start = pl.multiple_of(owner * 128 + target * 32, 32)
            ref[shift] = total[pl.ds(start, 32), :]


def totals(high_t, low_t, weights, pieces):
    part = jax.ShapeDtypeStruct((NX, 32, RANK), F32)
    return pl.pallas_call(
        totals_kernel,
        in_specs=[VMEM] * 7,
        out_specs=[VMEM] * 2,
        out_shape=[part] * 2,
        scratch_shapes=[pltpu.VMEM((2, KEEP // 2, 128), F32), pltpu.VMEM((COLS, RANK), F32)],
        compiler_params=room(12),
        cost_estimate=pl.CostEstimate(flops=800_000_000, bytes_accessed=4_000_000, transcendentals=0),
        name="totals",
    )(high_t, low_t, weights, *pieces)


def row_gram_kernel(*refs):
    pieces, out, rows = refs[:4], refs[4], refs[5]
    place_rows(lax.axis_index("x"), pieces, rows)
    lines = jnp.concatenate([rows[0], rows[1]], axis=1)
    out[...] = exact(lines.T, lines)


def row_gram(pieces):
    return pl.pallas_call(
        row_gram_kernel,
        in_specs=[VMEM] * 4,
        out_specs=VMEM,
        out_shape=jax.ShapeDtypeStruct((RANK, RANK), F32),
        scratch_shapes=[pltpu.VMEM((2, KEEP // 2, 128), F32)],
        compiler_params=room(8),
        cost_estimate=pl.CostEstimate(flops=400_000_000, bytes_accessed=800_000, transcendentals=0),
        name="row_gram",
    )(*pieces)


def inverse(gram, state):
    eye = (
        lax.broadcasted_iota(jnp.int32, (RANK, RANK), 0)
        == lax.broadcasted_iota(jnp.int32, (RANK, RANK), 1)
    ).astype(F32)
    penalty = jnp.sum(gram * eye) / RANK
    system = gram / penalty + eye
    middle = 2.0 / (1.0 + 257.0)
    state[:RANK] = middle * eye
    state[RANK:] = eye - middle * system

    def double(step, reach):
        doubled = 2.0 * reach * reach - 1.0
        gain = 2.0 * reach * reach / doubled
        both = state[...]
        product = gain * dot3(split(both), split(both[RANK:]))
        state[:RANK] = gain * both[:RANK] + product[:RANK]
        state[RANK:] = product[RANK:] - (1.0 / doubled) * eye
        return doubled

    lax.fori_loop(0, 6, double, jnp.float32(258.0 / 256.0))
    found = state[:RANK]
    found = found + dot3(split(found), split(eye - exact(system, found)))
    return found / penalty, penalty


FACTOR, DUAL = RANK + 16, RANK + 16 + COLS


def store_system(found, penalty, weights, inv):
    inv[:RANK] = found
    inv[RANK : RANK + 8] = jnp.full((8, RANK), penalty, F32)
    inv[RANK + 8 : FACTOR] = weights[...]


def col_system_kernel(snap, weights, mine, other, factor, dual, inv, gram, state):
    inv[FACTOR:DUAL] = factor[...]
    inv[DUAL:] = dual[...]
    snaps = snap[...]
    gram[...] = exact(snaps.T, snaps) * (mine[...] + other[...])
    store_system(*inverse(gram[...], state), weights, inv)


def row_system_kernel(snap, weights, mine, other, inv, gram, state):
    core = lax.axis_index("c")
    gram[pl.ds(pl.multiple_of(core * 128, 128), 128), :] = mine[...]
    gram[pl.ds(pl.multiple_of((1 - core) * 128, 128), 128), :] = other[...]
    snaps = snap[...]
    store_system(*inverse(exact(snaps.T, snaps) * gram[...], state), weights, inv)


def system(kernel, rows, *args):
    return pl.pallas_call(
        kernel,
        in_specs=[VMEM] * len(args),
        out_specs=VMEM,
        out_shape=jax.ShapeDtypeStruct((rows, RANK), F32),
        scratch_shapes=[pltpu.VMEM((RANK, RANK), F32), pltpu.VMEM((2 * RANK, RANK), F32)],
        cost_estimate=pl.CostEstimate(flops=3_000_000_000, bytes_accessed=1_000_000, transcendentals=0),
        compiler_params=room(8),
    )(*args)


def admm_update(sums, inv, new, dual_new):
    penalty = inv[RANK, 0]

    def update(step, carry):
        primal, multiplier = new[...], dual_new[...]
        solved = exact(sums[...] + penalty * (primal + multiplier), inv[:RANK])
        primal = jnp.maximum(solved - multiplier, 0.0)
        new[...] = primal
        dual_new[...] = multiplier + primal - solved
        return carry

    lax.fori_loop(0, ADMM_STEPS, update, 0)


def col_kernel(*refs):
    sources, inv, pieces = refs[:2], refs[2], refs[3:11]
    new, dual_new, gram_half, blocks = refs[11], refs[12], refs[13], refs[14:18]
    total, mapped, gram, high, low, sems = refs[18:]
    _, x, core, _ = place_of_own()
    copies = [
        pltpu.make_async_copy(source, target, sems.at[at])
        for at, (source, target) in enumerate(zip(sources, (high, low)))
    ]
    for copy in copies:
        copy.start()
    for side in range(NC):
        for shift in range(NX):
            source = lax.rem(x - shift + NX, NX)
            owner = core if side == 0 else 1 - core
            start = pl.multiple_of(owner * 128 + source * 32, 32)
            total[pl.ds(start, 32), :] = pieces[side * NX + shift][...]
    new[...] = inv[FACTOR:DUAL]
    dual_new[...] = inv[DUAL:]
    admm_update(total, inv, new, dual_new)
    primal = new[...]
    gram[...] = exact(primal.T, primal)
    gram_half[...] = gram[pl.ds(pl.multiple_of(core * 128, 128), 128), :]
    lines, weights = split(primal), inv[RANK + 8 : FACTOR]
    for copy in copies:
        copy.wait()
    for k in range(4):
        line = sum(dot3((high[s, k], low[s, k]), lines) * weights[s : s + 1] for s in range(4))
        for half in range(2):
            mapped[half, pl.ds(k, HALF, stride=4), :] = line[:, 128 * half : 128 * half + 128]
    for shift, block in enumerate(blocks):
        target = lax.rem(x + shift, NX)
        for row in range(NZ):
            start = pl.multiple_of(row * 64 + target * 16, 16)
            for half in range(2):
                block[row, :, 128 * half : 128 * half + 128] = mapped[half, pl.ds(start, 16), :]


def col_update(high, low, inv, pieces):
    square = jax.ShapeDtypeStruct((COLS, RANK), F32)
    block = jax.ShapeDtypeStruct((NZ, 16, RANK), F32)
    outs = [square, square, jax.ShapeDtypeStruct((128, RANK), F32)] + [block] * NX
    return pl.pallas_call(
        col_kernel,
        in_specs=[pl.BlockSpec(memory_space=pltpu.HBM)] * 2 + [VMEM] * 9,
        out_specs=[VMEM] * len(outs),
        out_shape=outs,
        scratch_shapes=[
            pltpu.VMEM((COLS, RANK), F32),
            pltpu.VMEM((2, KEEP // 2, 128), F32),
            pltpu.VMEM((RANK, RANK), F32),
            pltpu.VMEM((4, 4, HALF, COLS), BF16),
            pltpu.VMEM((4, 4, HALF, COLS), BF16),
            pltpu.SemaphoreType.DMA((2,)),
        ],
        cost_estimate=pl.CostEstimate(flops=1_500_000_000, bytes_accessed=5_000_000, transcendentals=0),
        compiler_params=room(16),
        name="col_update",
    )(high, low, inv, *pieces)


def gram_sum_kernel(*refs):
    parts, out, held = refs[:4], refs[4], refs[5]
    y = lax.axis_index("y")
    for shift in range(NY):
        held[lax.rem(y - shift + NY, NY)] = parts[shift][...]
    out[...] = (held[0] + held[1]) + (held[2] + held[3])


def gram_sum(parts):
    shape = parts[0].shape
    return pl.pallas_call(
        gram_sum_kernel,
        in_specs=[VMEM] * NY,
        out_specs=VMEM,
        out_shape=jax.ShapeDtypeStruct(shape, F32),
        scratch_shapes=[pltpu.VMEM((NY, *shape), F32)],
        compiler_params=room(4),
        name="gram_sum",
    )(*parts)


def row_kernel(inv, factor, dual, mine, other, new, dual_new, sums):
    sums[...] = mine[...] + other[...]
    new[...] = factor[...]
    dual_new[...] = dual[...]
    admm_update(sums, inv, new, dual_new)


def row_update(inv, factor, dual, mine, other):
    own = jax.ShapeDtypeStruct((16, RANK), F32)
    return pl.pallas_call(
        row_kernel,
        in_specs=[VMEM] * 5,
        out_specs=[VMEM] * 2,
        out_shape=[own] * 2,
        scratch_shapes=[pltpu.VMEM((16, RANK), F32)],
        compiler_params=room(4),
        name="row_update",
    )(inv, factor, dual, mine, other)


def shifted(array, axis, size, by):
    return lax.ppermute(array, axis, [(i, (i + by) % size) for i in range(size)])


def swapped(array, axis, flip):
    return lax.ppermute(array, axis, [(i, i ^ flip) for i in range(4)])


def sum_kernel(count, *refs):
    total = refs[0][...]
    for ref in refs[1:count]:
        total = total + ref[...]
    outs = refs[count:]
    for at, out in enumerate(outs):
        share = total.shape[0] // len(outs)
        own = total if len(outs) == 1 else total[at * share : (at + 1) * share]
        out[...] = own.reshape(out.shape)


def summed(parts, shape, count=1):
    return pl.pallas_call(
        functools.partial(sum_kernel, len(parts)),
        in_specs=[VMEM] * len(parts),
        out_specs=[VMEM] * count,
        out_shape=[jax.ShapeDtypeStruct(shape, F32)] * count,
        compiler_params=room(8),
        name="summed",
    )(*parts)


def spread_kernel(count, *refs):
    total = refs[0][...]
    for ref in refs[1:count]:
        total = total + ref[...]
    for at in range(refs[count].shape[0]):
        refs[count][at] = total


def copied_along(parts, axes, size):
    whole = pl.pallas_call(
        functools.partial(spread_kernel, len(parts)),
        in_specs=[VMEM] * len(parts),
        out_specs=VMEM,
        out_shape=jax.ShapeDtypeStruct((size, *parts[0].shape), F32),
        compiler_params=room(8),
        name="spread",
    )(*parts)
    return lax.all_to_all(whole, axes, 0, 0, tiled=True)


def fold_kernel(block, out):
    half = [block[at] + block[at + 1] for at in range(0, NZ, 2)]
    out[...] = (half[0] + half[1]) + (half[2] + half[3])


def folded(block):
    return pl.pallas_call(
        fold_kernel,
        in_specs=[VMEM],
        out_specs=VMEM,
        out_shape=jax.ShapeDtypeStruct(block.shape[1:], F32),
        compiler_params=room(4),
        name="folded",
    )(block)


def body(snapshots, snap_factor, row_factor, col_factor, row_dual, col_dual):
    mine = copied_along([row_factor], "z", NZ)
    own, send = dct(snapshots)
    mine, own, send = lax.optimization_barrier((mine, own, send))
    lines = [mine] + [shifted(mine, "x", NX, by) for by in range(1, NX)]
    high, low, high_t, low_t, weights = prepare(own, shifted(send, "c", NC, 1), snap_factor)
    keep, send = totals(high_t, low_t, weights, lines)
    gram = row_gram(lines)
    other = shifted(gram, "c", NC, 1)
    args = snap_factor, weights, gram, other
    inv = system(col_system_kernel, DUAL + COLS, *args, col_factor, col_dual)
    parts = summed([keep, shifted(send, "c", NC, 1)], (32, RANK), NX)
    parts = [parts[0]] + [shifted(parts[by], "x", NX, by) for by in range(1, NX)]
    chunk = copied_along(parts, "z", NZ)
    chunk, inv = lax.optimization_barrier((chunk, inv))
    chunk = folded(chunk)
    pieces = [chunk] + [shifted(chunk, "x", NX, by) for by in range(1, NX)]
    pieces = pieces + [shifted(piece, "c", NC, 1) for piece in pieces]
    col_new, col_dual_new, gram_half, *blocks = col_update(
        high, low, inv, pieces
    )
    grams = [gram_half]
    for by in range(1, NX):
        blocks[by] = shifted(blocks[by], "x", NX, by)
    for by in range(1, NY):
        grams.append(shifted(gram_half, "y", NY, by))
    block = summed(blocks, (NZ, 16, RANK))[0]
    _, *grams = lax.optimization_barrier((block, *grams))
    gram_mine = gram_sum(grams)
    other = shifted(gram_mine, "c", NC, 1)
    args = snap_factor, weights, gram_mine, other
    inv = system(row_system_kernel, FACTOR, *args)
    block = lax.all_to_all(block, "z", 0, 0, tiled=True)
    block, inv = lax.optimization_barrier((block, inv))
    mine = folded(block)
    near = summed([mine, swapped(mine, "y", 1)], mine.shape)[0]
    row_new, row_dual_new = row_update(inv, row_factor, row_dual, near, swapped(near, "y", 3))
    return row_new, col_new, row_dual_new, col_dual_new


def solution(mesh):
    fine = Mesh(mesh.devices.reshape(NZ, NX, NC, NY), ("z", "x", "c", "y"))
    return jax.shard_map(
        body,
        mesh=fine,
        in_specs=(
            P(WIDE, None, "y"),
            P(),
            P(WIDE, None),
            P("y", None),
            P(WIDE, None),
            P("y", None),
        ),
        out_specs=(P(WIDE, None), P("y", None), P(WIDE, None), P("y", None)),
        check_vma=False,
    )
```

time: 119 us -> 115 us (0.966)
  the two profiles are of different devices: /device:TPU:6 before, /device:TPU:24 now
where the time goes in v3:
time: 115 us; the launch traced here: 114 us
  starting transfers between devices  43.3 us (38%)
  waiting for transfers between devices  38.3 us (33%)
  Pallas kernels  24.8 us (22%)
  local copies, waits for them, and re-layouts  6.66 us (6%)
    ppermute x23, starting transfers between devices, shifted(): lax.ppermute(array, axis, [(i, (i + by) % size) for i in range(size)])  24.2 us
    ppermute x23, waiting for transfers between devices, shifted(): lax.ppermute(array, axis, [(i, (i + by) % size) for i in range(size)])  19.1 us
    all_to_all x2, starting transfers between devices, copied_along(): return lax.all_to_all(whole, axes, 0, 0, tiled=True)  15.7 us
    ppermute x2, waiting for transfers between devices, swapped(): return lax.ppermute(array, axis, [(i, i ^ flip) for i in range(4)])  8.67 us
    pallas_call x2, Pallas kernels, system(): pl.pallas_call(kernel, in_specs=[VMEM] * len(args), out_specs=VMEM, out_s...  7.41 us
    pallas_call x1, Pallas kernels, dct(): pl.pallas_call(dct_kernel, grid=(steps,), in_specs=[pl.BlockSpec(block, l...  7.34 us
    unnamed x20, local copies, waits for them, and re-layouts  6.66 us
    all_to_all x1, waiting for transfers between devices, body(): block = lax.all_to_all(block, 'z', 0, 0, tiled=True)  6.18 us
  transfers between devices with their start and end apart: 28, of which 15 were waited for; matrix products, arithmetic and copies ran while one was open for 0% of the time, Pallas kernels for 15%

profile of v3, /device:TPU:24, one launch (start us, length us, event | category | flops | bytes accessed | tf_op | source)
XLA Modules:
  0.0 113.9 jit_solution(2212614916860032089)
XLA Ops:
  2.0 8.5 %all-to-all-start = ((f32[8,16,256]{2,1,0:T(8,128)}), f32[8,16,256]{2,1,0:T(8,128)S(1)}, u32[]{:S(2)}, u32[]{:S(2)}) async-start(f32[8,16,256]{2,1,0:T(8,128)} %spread.2), calls=%async_computation | async-start | bytes 262144 | tf_op jit(solution)/shard_map/all_to_all | solution.py:491
  12.5 7.3 %dct.1 = (f32[2,4,128,256]{3,2,1,0:T(8,128)S(1)}, f32[2,4,128,256]{3,2,1,0:T(8,128)S(1)}) custom-call(f32[2,4096,256]{2,1,0:T(8,128)} %x3.1, f32[2,4096,256]{2,1,0:T(8,128)} %x3.1, f32[2,4096,256]{2,1,0:T(8,128)} %x3.1, f32[2,4096,256]{2,1,0:T(8,128)} %x3.1, f32[4,256,256]{2,1,0:T(8,128)S(1)} %copy-done, f32[10,8,128]{2,1,0:T(8,128)S(1)} %copy-done.4), custom_call_target="tpu_custom_call" | custom-call | flops 7000000000 | bytes 13000000 | tf_op jit(solution)/shard_map/dct/pallas_call | solution.py:144
  19.9 1.6 %collective-permute-start.1 = (f32[8,16,256]{2,1,0:T(8,128)S(1)}, f32[8,16,256]{2,1,0:T(8,128)S(1)}, u32[]{:S(2)}, u32[]{:S(2)}) collective-permute-start(f32[8,16,256]{2,1,0:T(8,128)S(1)} %all-to-all-done.refs_0_), channel_id=1, source_target_pairs={{0,8},{8,16},{16,24},{24,0},{1,9},{9,17},{17,25},{25,1},{2,10},{10... | collective-permute-start | bytes 393224 | tf_op jit(solution)/shard_map/ppermute | solution.py:445
  21.5 2.7 %collective-permute-start.2 = (f32[8,16,256]{2,1,0:T(8,128)S(1)}, f32[8,16,256]{2,1,0:T(8,128)S(1)}, u32[]{:S(2)}, u32[]{:S(2)}) collective-permute-start(f32[8,16,256]{2,1,0:T(8,128)S(1)} %all-to-all-done.refs_0_), channel_id=1, source_target_pairs={{0,16},{8,24},{16,0},{24,8},{1,17},{9,25},{17,1},{25,9},{2,18},{10... | collective-permute-start | bytes 393224 | tf_op jit(solution)/shard_map/ppermute | solution.py:445
  27.1 3.8 %collective-permute-done.2.refs_2_ = f32[8,16,256]{2,1,0:T(8,128)S(1)} collective-permute-done((f32[8,16,256]{2,1,0:T(8,128)S(1)}, f32[8,16,256]{2,1,0:T(8,128)S(1)}, u32[]{:S(2)}, u32[]{:S(2)}) %collective-permute-start.2) | collective-permute-done | bytes 131104 | tf_op jit(solution)/shard_map/ppermute | solution.py:445
  30.8 1.9 %totals.1 = (f32[4,32,256]{2,1,0:T(8,128)S(1)}, f32[4,32,256]{2,1,0:T(8,128)S(1)}) custom-call(bf16[4,256,512]{2,1,0:T(8,128)(2,1)S(1)} %get-tuple-element.43.high_t, bf16[4,256,512]{2,1,0:T(8,128)(2,1)S(1)} %get-tuple-element.44.low_t, f32[8,256]{1,0:T(8,128)S(1)} %get-tuple-element.45.weights, f32[8,16,256]{2,1,0:T(8,128)S(1)} %all-to-all-done.refs_0_, ...), custom_call_target="tpu_custom_call" | custom-call | flops 800000000 | bytes 4000000 | tf_op jit(solution)/shard_map/totals/pallas_call | solution.py:233
  35.6 2.4 %collective-permute-start.6 = (f32[32,256]{1,0:T(8,128)S(1)}, f32[32,256]{1,0:T(8,128)S(1)}, u32[]{:S(2)}, u32[]{:S(2)}) collective-permute-start(f32[32,256]{1,0:T(8,128)S(1)} %get-tuple-element.51), channel_id=1, source_target_pairs={{0,16},{8,24},{16,0},{24,8},{1,17},{9,25},{17,1},{25,9},{2,18},{10... | collective-permute-start | bytes 98312 | tf_op jit(solution)/shard_map/ppermute | solution.py:445
  38.0 1.6 %collective-permute-start.7 = (f32[32,256]{1,0:T(8,128)S(1)}, f32[32,256]{1,0:T(8,128)S(1)}, u32[]{:S(2)}, u32[]{:S(2)}) collective-permute-start(f32[32,256]{1,0:T(8,128)S(1)} %get-tuple-element.52), channel_id=1, source_target_pairs={{0,24},{8,0},{16,8},{24,16},{1,25},{9,1},{17,9},{25,17},{2,26},{10... | collective-permute-start | bytes 98312 | tf_op jit(solution)/shard_map/ppermute | solution.py:445
  42.6 7.2 %all-to-all-start.1 = ((f32[8,32,256]{2,1,0:T(8,128)}), f32[8,32,256]{2,1,0:T(8,128)S(1)}, u32[]{:S(2)}, u32[]{:S(2)}) async-start(f32[8,32,256]{2,1,0:T(8,128)} %spread.3), calls=%async_computation.1 | async-start | bytes 524288 | tf_op jit(solution)/shard_map/all_to_all | solution.py:491
  51.8 3.7 %shard_map.111.refs_2_ = f32[784,256]{1,0:T(8,128)S(1)} custom-call(f32[128,256]{1,0:T(8,128)S(1)} %copy-done.1, f32[8,256]{1,0:T(8,128)S(1)} %get-tuple-element.45.weights, f32[256,256]{1,0:T(8,128)S(1)} %row_gram.1.mine, f32[256,256]{1,0:T(8,128)S(1)} %collective-permute-done.8.other, f32[256,256]{1,0:T(8,128)S(1)} %copy-done.6, f32[256,256]{1,0:T(8,128)S(1)} %copy-done.7), custom_call_target="tpu_custom_call" | custom-call | flops 3000000000 | bytes 1000000 | tf_op jit(solution)/shard_map/pallas_call | solution.py:317
  56.4 4.3 %all-to-all-done.1.block = f32[8,32,256]{2,1,0:T(8,128)S(1)} async-done(((f32[8,32,256]{2,1,0:T(8,128)}), f32[8,32,256]{2,1,0:T(8,128)S(1)}, u32[]{:S(2)}, u32[]{:S(2)}) %all-to-all-start.1) | async-done | bytes 262176 | tf_op jit(solution)/shard_map/all_to_all | solution.py:491
  61.3 3.6 %collective-permute-start.10 = (f32[32,256]{1,0:T(8,128)S(1)}, f32[32,256]{1,0:T(8,128)S(1)}, u32[]{:S(2)}, u32[]{:S(2)}) collective-permute-start(f32[32,256]{1,0:T(8,128)S(1)} %folded.2.refs_3_), channel_id=1, source_target_pairs={{0,16},{8,24},{16,0},{24,8},{1,17},{9,25},{17,1},{25,9},{2,18},{10... | collective-permute-start | bytes 98312 | tf_op jit(solution)/shard_map/ppermute | solution.py:445
  67.1 1.7 %collective-permute-done.11.refs_6_ = f32[32,256]{1,0:T(8,128)S(1)} collective-permute-done((f32[32,256]{1,0:T(8,128)S(1)}, f32[32,256]{1,0:T(8,128)S(1)}, u32[]{:S(2)}, u32[]{:S(2)}) %collective-permute-start.11) | collective-permute-done | bytes 32800 | tf_op jit(solution)/shard_map/ppermute | solution.py:445
  71.2 3.3 %col_update.1 = (f32[256,256]{1,0:T(8,128)}, f32[256,256]{1,0:T(8,128)}, f32[128,256]{1,0:T(8,128)S(1)}, f32[8,16,256]{2,1,0:T(8,128)S(1)}, f32[8,16,256]{2,1,0:...) custom-call(bf16[4,4,128,256]{3,2,1,0:T(8,128)(2,1)S(1)} %get-tuple-element.41.refs_0_, ...), custom_call_target="tpu_custom_call" | custom-call | flops 1500000000 | bytes 5000000 | tf_op jit(solution)/shard_map/col_update/pallas_call | solution.py:384
  74.7 2.6 %collective-permute-start.17 = (f32[8,16,256]{2,1,0:T(8,128)S(1)}, f32[8,16,256]{2,1,0:T(8,128)S(1)}, u32[]{:S(2)}, u32[]{:S(2)}) collective-permute-start(f32[8,16,256]{2,1,0:T(8,128)S(1)} %get-tuple-element.57), channel_id=1, source_target_pairs={{0,16},{8,24},{16,0},{24,8},{1,17},{9,25},{17,1},{25,9},{2,18},{10... | collective-permute-start | bytes 393224 | tf_op jit(solution)/shard_map/ppermute | solution.py:445
  77.3 1.5 %collective-permute-start.18 = (f32[8,16,256]{2,1,0:T(8,128)S(1)}, f32[8,16,256]{2,1,0:T(8,128)S(1)}, u32[]{:S(2)}, u32[]{:S(2)}) collective-permute-start(f32[8,16,256]{2,1,0:T(8,128)S(1)} %get-tuple-element.58), channel_id=1, source_target_pairs={{0,24},{8,0},{16,8},{24,16},{1,25},{9,1},{17,9},{25,17},{2,26},{10... | collective-permute-start | bytes 393224 | tf_op jit(solution)/shard_map/ppermute | solution.py:445
  79.0 2.6 %collective-permute-start.20 = (f32[128,256]{1,0:T(8,128)S(1)}, f32[128,256]{1,0:T(8,128)S(1)}, u32[]{:S(2)}, u32[]{:S(2)}) collective-permute-start(f32[128,256]{1,0:T(8,128)S(1)} %get-tuple-element.60.refs_0_), channel_id=1, source_target_pairs={{0,2},{1,3},{2,0},{3,1},{4,6},{5,7},{6,4},{7,5},{8,10},{9,11},{10,... | collective-permute-start | bytes 393224 | tf_op jit(solution)/shard_map/ppermute | solution.py:445
  81.6 2.5 %collective-permute-done.16.refs_1_ = f32[8,16,256]{2,1,0:T(8,128)S(1)} collective-permute-done((f32[8,16,256]{2,1,0:T(8,128)S(1)}, f32[8,16,256]{2,1,0:T(8,128)S(1)}, u32[]{:S(2)}, u32[]{:S(2)}) %collective-permute-start.16) | collective-permute-done | bytes 131104 | tf_op jit(solution)/shard_map/ppermute | solution.py:445
  86.5 3.8 %collective-permute-done.21.refs_3_ = f32[128,256]{1,0:T(8,128)S(1)} collective-permute-done((f32[128,256]{1,0:T(8,128)S(1)}, f32[128,256]{1,0:T(8,128)S(1)}, u32[]{:S(2)}, u32[]{:S(2)}) %collective-permute-start.21) | collective-permute-done | bytes 131104 | tf_op jit(solution)/shard_map/ppermute | solution.py:445
  90.5 3.4 %all-to-all-start.2 = ((f32[8,16,256]{2,1,0:T(8,128)}), f32[8,16,256]{2,1,0:T(8,128)S(1)}, u32[]{:S(2)}, u32[]{:S(2)}) async-start(f32[8,16,256]{2,1,0:T(8,128)} %summed.4), calls=%async_computation.2 | async-start | bytes 262144 | tf_op jit(solution)/shard_map/all_to_all | solution.py:542
  93.9 3.7 %shard_map.112.inv = f32[272,256]{1,0:T(8,128)S(1)} custom-call(f32[128,256]{1,0:T(8,128)S(1)} %copy-done.1, f32[8,256]{1,0:T(8,128)S(1)} %get-tuple-element.45.weights, f32[128,256]{1,0:T(8,128)S(1)} %gram_sum.1.mine, f32[128,256]{1,0:T(8,128)S(1)} %collective-permute-done.22.other), custom_call_target="tpu_custom_call" | custom-call | flops 3000000000 | bytes 1000000 | tf_op jit(solution)/shard_map/pallas_call | solution.py:317
  97.6 6.2 %all-to-all-done.2.block = f32[8,16,256]{2,1,0:T(8,128)S(1)} async-done(((f32[8,16,256]{2,1,0:T(8,128)}), f32[8,16,256]{2,1,0:T(8,128)S(1)}, u32[]{:S(2)}, u32[]{:S(2)}) %all-to-all-start.2) | async-done | bytes 131104 | tf_op jit(solution)/shard_map/all_to_all | solution.py:542
  103.9 3.7 %collective-permute-done.23.refs_1_ = f32[16,256]{1,0:T(8,128)S(1)} collective-permute-done((f32[16,256]{1,0:T(8,128)S(1)}, f32[16,256]{1,0:T(8,128)S(1)}, u32[]{:S(2)}, u32[]{:S(2)}) %collective-permute-start.23) | collective-permute-done | bytes 16416 | tf_op jit(solution)/shard_map/ppermute | solution.py:449
  107.6 4.9 %collective-permute-done.24.other = f32[16,256]{1,0:T(8,128)S(1)} collective-permute-done((f32[16,256]{1,0:T(8,128)S(1)}, f32[16,256]{1,0:T(8,128)S(1)}, u32[]{:S(2)}, u32[]{:S(2)}) %collective-permute-start.24) | collective-permute-done | bytes 16416 | tf_op jit(solution)/shard_map/ppermute | solution.py:449
  (68 shorter events, 24.7 us)
Async XLA Ops:
  2.0 17.8 %all-to-all-start = ((f32[8,16,256]{2,1,0:T(8,128)}), f32[8,16,256]{2,1,0:T(8,128)S(1)}, u32[]{:S(2)}, u32[]{:S(2)}) async-start(f32[8,16,256]{2,1,0:T(8,128)} %spread.2), calls=%async_computation | async-start | bytes 262144 | tf_op jit(solution)/shard_map/all_to_all | solution.py:491
  19.8 5.8 %collective-permute-start = (f32[2,4,128,256]{3,2,1,0:T(8,128)S(1)}, f32[2,4,128,256]{3,2,1,0:T(8,128)S(1)}, u32[]{:S(2)}, u32[]{:S(2)}) collective-permute-start(f32[2,4,128,256]{3,2,1,0:T(8,128)S(1)} %get-tuple-element.40), channel_id=1, source_target_pairs={{0,4},{4,0},{1,5},{5,1},{2,6},{6,2},{3,7},{7,3},{8,12},{12,8},{9,1... | collective-permute-start | bytes 3145736 | tf_op jit(solution)/shard_map/ppermute | solution.py:445
  19.9 7.1 %collective-permute-start.1 = (f32[8,16,256]{2,1,0:T(8,128)S(1)}, f32[8,16,256]{2,1,0:T(8,128)S(1)}, u32[]{:S(2)}, u32[]{:S(2)}) collective-permute-start(f32[8,16,256]{2,1,0:T(8,128)S(1)} %all-to-all-done.refs_0_), channel_id=1, source_target_pairs={{0,8},{8,16},{16,24},{24,0},{1,9},{9,17},{17,25},{25,1},{2,10},{10... | collective-permute-start | bytes 393224 | tf_op jit(solution)/shard_map/ppermute | solution.py:445
  21.5 9.3 %collective-permute-start.2 = (f32[8,16,256]{2,1,0:T(8,128)S(1)}, f32[8,16,256]{2,1,0:T(8,128)S(1)}, u32[]{:S(2)}, u32[]{:S(2)}) collective-permute-start(f32[8,16,256]{2,1,0:T(8,128)S(1)} %all-to-all-done.refs_0_), channel_id=1, source_target_pairs={{0,16},{8,24},{16,0},{24,8},{1,17},{9,25},{17,1},{25,9},{2,18},{10... | collective-permute-start | bytes 393224 | tf_op jit(solution)/shard_map/ppermute | solution.py:445
  24.2 6.6 %collective-permute-start.3 = (f32[8,16,256]{2,1,0:T(8,128)S(1)}, f32[8,16,256]{2,1,0:T(8,128)S(1)}, u32[]{:S(2)}, u32[]{:S(2)}) collective-permute-start(f32[8,16,256]{2,1,0:T(8,128)S(1)} %all-to-all-done.refs_0_), channel_id=1, source_target_pairs={{0,24},{8,0},{16,8},{24,16},{1,25},{9,1},{17,9},{25,17},{2,26},{10... | collective-permute-start | bytes 393224 | tf_op jit(solution)/shard_map/ppermute | solution.py:445
  33.6 16.3 %collective-permute-start.8 = (f32[256,256]{1,0:T(8,128)S(1)}, f32[256,256]{1,0:T(8,128)S(1)}, u32[]{:S(2)}, u32[]{:S(2)}) collective-permute-start(f32[256,256]{1,0:T(8,128)S(1)} %row_gram.1.mine), channel_id=1, source_target_pairs={{0,4},{4,0},{1,5},{5,1},{2,6},{6,2},{3,7},{7,3},{8,12},{12,8},{9,1... | collective-permute-start | bytes 786440 | tf_op jit(solution)/shard_map/ppermute | solution.py:445
  34.2 5.4 %collective-permute-start.5 = (f32[32,256]{1,0:T(8,128)S(1)}, f32[32,256]{1,0:T(8,128)S(1)}, u32[]{:S(2)}, u32[]{:S(2)}) collective-permute-start(f32[32,256]{1,0:T(8,128)S(1)} %get-tuple-element.50), channel_id=1, source_target_pairs={{0,8},{8,16},{16,24},{24,0},{1,9},{9,17},{17,25},{25,1},{2,10},{10... | collective-permute-start | bytes 98312 | tf_op jit(solution)/shard_map/ppermute | solution.py:445
  35.6 5.4 %collective-permute-start.6 = (f32[32,256]{1,0:T(8,128)S(1)}, f32[32,256]{1,0:T(8,128)S(1)}, u32[]{:S(2)}, u32[]{:S(2)}) collective-permute-start(f32[32,256]{1,0:T(8,128)S(1)} %get-tuple-element.51), channel_id=1, source_target_pairs={{0,16},{8,24},{16,0},{24,8},{1,17},{9,25},{17,1},{25,9},{2,18},{10... | collective-permute-start | bytes 98312 | tf_op jit(solution)/shard_map/ppermute | solution.py:445
  38.0 3.9 %collective-permute-start.7 = (f32[32,256]{1,0:T(8,128)S(1)}, f32[32,256]{1,0:T(8,128)S(1)}, u32[]{:S(2)}, u32[]{:S(2)}) collective-permute-start(f32[32,256]{1,0:T(8,128)S(1)} %get-tuple-element.52), channel_id=1, source_target_pairs={{0,24},{8,0},{16,8},{24,16},{1,25},{9,1},{17,9},{25,17},{2,26},{10... | collective-permute-start | bytes 98312 | tf_op jit(solution)/shard_map/ppermute | solution.py:445
  42.6 18.1 %all-to-all-start.1 = ((f32[8,32,256]{2,1,0:T(8,128)}), f32[8,32,256]{2,1,0:T(8,128)S(1)}, u32[]{:S(2)}, u32[]{:S(2)}) async-start(f32[8,32,256]{2,1,0:T(8,128)} %spread.3), calls=%async_computation.1 | async-start | bytes 524288 | tf_op jit(solution)/shard_map/all_to_all | solution.py:491
  60.7 5.4 %collective-permute-start.9 = (f32[32,256]{1,0:T(8,128)S(1)}, f32[32,256]{1,0:T(8,128)S(1)}, u32[]{:S(2)}, u32[]{:S(2)}) collective-permute-start(f32[32,256]{1,0:T(8,128)S(1)} %folded.2.refs_3_), channel_id=1, source_target_pairs={{0,8},{8,16},{16,24},{24,0},{1,9},{9,17},{17,25},{25,1},{2,10},{10... | collective-permute-start | bytes 98312 | tf_op jit(solution)/shard_map/ppermute | solution.py:445
  61.3 5.8 %collective-permute-start.10 = (f32[32,256]{1,0:T(8,128)S(1)}, f32[32,256]{1,0:T(8,128)S(1)}, u32[]{:S(2)}, u32[]{:S(2)}) collective-permute-start(f32[32,256]{1,0:T(8,128)S(1)} %folded.2.refs_3_), channel_id=1, source_target_pairs={{0,16},{8,24},{16,0},{24,8},{1,17},{9,25},{17,1},{25,9},{2,18},{10... | collective-permute-start | bytes 98312 | tf_op jit(solution)/shard_map/ppermute | solution.py:445
  64.9 3.9 %collective-permute-start.11 = (f32[32,256]{1,0:T(8,128)S(1)}, f32[32,256]{1,0:T(8,128)S(1)}, u32[]{:S(2)}, u32[]{:S(2)}) collective-permute-start(f32[32,256]{1,0:T(8,128)S(1)} %folded.2.refs_3_), channel_id=1, source_target_pairs={{0,24},{8,0},{16,8},{24,16},{1,25},{9,1},{17,9},{25,17},{2,26},{10... | collective-permute-start | bytes 98312 | tf_op jit(solution)/shard_map/ppermute | solution.py:445
  65.0 3.8 %collective-permute-start.12 = (f32[32,256]{1,0:T(8,128)S(1)}, f32[32,256]{1,0:T(8,128)S(1)}, u32[]{:S(2)}, u32[]{:S(2)}) collective-permute-start(f32[32,256]{1,0:T(8,128)S(1)} %folded.2.refs_3_), channel_id=1, source_target_pairs={{0,4},{4,0},{1,5},{5,1},{2,6},{6,2},{3,7},{7,3},{8,12},{12,8},{9,1... | collective-permute-start | bytes 98312 | tf_op jit(solution)/shard_map/ppermute | solution.py:445
  74.4 9.7 %collective-permute-start.16 = (f32[8,16,256]{2,1,0:T(8,128)S(1)}, f32[8,16,256]{2,1,0:T(8,128)S(1)}, u32[]{:S(2)}, u32[]{:S(2)}) collective-permute-start(f32[8,16,256]{2,1,0:T(8,128)S(1)} %get-tuple-element.56), channel_id=1, source_target_pairs={{0,8},{8,16},{16,24},{24,0},{1,9},{9,17},{17,25},{25,1},{2,10},{10... | collective-permute-start | bytes 393224 | tf_op jit(solution)/shard_map/ppermute | solution.py:445
  74.7 10.2 %collective-permute-start.17 = (f32[8,16,256]{2,1,0:T(8,128)S(1)}, f32[8,16,256]{2,1,0:T(8,128)S(1)}, u32[]{:S(2)}, u32[]{:S(2)}) collective-permute-start(f32[8,16,256]{2,1,0:T(8,128)S(1)} %get-tuple-element.57), channel_id=1, source_target_pairs={{0,16},{8,24},{16,0},{24,8},{1,17},{9,25},{17,1},{25,9},{2,18},{10... | collective-permute-start | bytes 393224 | tf_op jit(solution)/shard_map/ppermute | solution.py:445
  77.3 7.6 %collective-permute-start.18 = (f32[8,16,256]{2,1,0:T(8,128)S(1)}, f32[8,16,256]{2,1,0:T(8,128)S(1)}, u32[]{:S(2)}, u32[]{:S(2)}) collective-permute-start(f32[8,16,256]{2,1,0:T(8,128)S(1)} %get-tuple-element.58), channel_id=1, source_target_pairs={{0,24},{8,0},{16,8},{24,16},{1,25},{9,1},{17,9},{25,17},{2,26},{10... | collective-permute-start | bytes 393224 | tf_op jit(solution)/shard_map/ppermute | solution.py:445
  78.8 6.7 %collective-permute-start.19 = (f32[128,256]{1,0:T(8,128)S(1)}, f32[128,256]{1,0:T(8,128)S(1)}, u32[]{:S(2)}, u32[]{:S(2)}) collective-permute-start(f32[128,256]{1,0:T(8,128)S(1)} %get-tuple-element.60.refs_0_), channel_id=1, source_target_pairs={{0,1},{1,2},{2,3},{3,0},{4,5},{5,6},{6,7},{7,4},{8,9},{9,10},{10,1... | collective-permute-start | bytes 393224 | tf_op jit(solution)/shard_map/ppermute | solution.py:445
  79.0 7.5 %collective-permute-start.20 = (f32[128,256]{1,0:T(8,128)S(1)}, f32[128,256]{1,0:T(8,128)S(1)}, u32[]{:S(2)}, u32[]{:S(2)}) collective-permute-start(f32[128,256]{1,0:T(8,128)S(1)} %get-tuple-element.60.refs_0_), channel_id=1, source_target_pairs={{0,2},{1,3},{2,0},{3,1},{4,6},{5,7},{6,4},{7,5},{8,10},{9,11},{10,... | collective-permute-start | bytes 393224 | tf_op jit(solution)/shard_map/ppermute | solution.py:445
  84.1 6.2 %collective-permute-start.21 = (f32[128,256]{1,0:T(8,128)S(1)}, f32[128,256]{1,0:T(8,128)S(1)}, u32[]{:S(2)}, u32[]{:S(2)}) collective-permute-start(f32[128,256]{1,0:T(8,128)S(1)} %get-tuple-element.60.refs_0_), channel_id=1, source_target_pairs={{0,3},{1,0},{2,1},{3,2},{4,7},{5,4},{6,5},{7,6},{8,11},{9,8},{10,9... | collective-permute-start | bytes 393224 | tf_op jit(solution)/shard_map/ppermute | solution.py:445
  90.4 3.5 %collective-permute-start.22 = (f32[128,256]{1,0:T(8,128)S(1)}, f32[128,256]{1,0:T(8,128)S(1)}, u32[]{:S(2)}, u32[]{:S(2)}) collective-permute-start(f32[128,256]{1,0:T(8,128)S(1)} %gram_sum.1.mine), channel_id=1, source_target_pairs={{0,4},{4,0},{1,5},{5,1},{2,6},{6,2},{3,7},{7,3},{8,12},{12,8},{9,1... | collective-permute-start | bytes 393224 | tf_op jit(solution)/shard_map/ppermute | solution.py:445
  90.5 13.3 %all-to-all-start.2 = ((f32[8,16,256]{2,1,0:T(8,128)}), f32[8,16,256]{2,1,0:T(8,128)S(1)}, u32[]{:S(2)}, u32[]{:S(2)}) async-start(f32[8,16,256]{2,1,0:T(8,128)} %summed.4), calls=%async_computation.2 | async-start | bytes 262144 | tf_op jit(solution)/shard_map/all_to_all | solution.py:542
  103.8 3.8 %collective-permute-start.23 = (f32[16,256]{1,0:T(8,128)S(1)}, f32[16,256]{1,0:T(8,128)S(1)}, u32[]{:S(2)}, u32[]{:S(2)}) collective-permute-start(f32[16,256]{1,0:T(8,128)S(1)} %folded.3.refs_0_), channel_id=1, source_target_pairs={{0,1},{1,0},{2,3},{3,2},{4,5},{5,4},{6,7},{7,6},{8,9},{9,8},{10,11... | collective-permute-start | bytes 49160 | tf_op jit(solution)/shard_map/ppermute | solution.py:449
  107.6 4.9 %collective-permute-start.24 = (f32[16,256]{1,0:T(8,128)S(1)}, f32[16,256]{1,0:T(8,128)S(1)}, u32[]{:S(2)}, u32[]{:S(2)}) collective-permute-start(f32[16,256]{1,0:T(8,128)S(1)} %summed.5.mine), channel_id=1, source_target_pairs={{0,3},{1,2},{2,1},{3,0},{4,7},{5,6},{6,5},{7,4},{8,11},{9,10},{10,... | collective-permute-start | bytes 49160 | tf_op jit(solution)/shard_map/ppermute | solution.py:449
  (14 other events, 109.8 us)

commit v4 on v3

--- a/solution.py
+++ b/solution.py
@@ -29,8 +29,9 @@
 
 def twiddles():
     odd = 2 * np.arange(STEP)[None, :] + 1
-    half, group, low = np.meshgrid(np.arange(2), np.arange(32), np.arange(4), indexing="ij")
-    degree = (8 * group + 4 * half + low).reshape(BAND, 1)
+    sizes = (NC, NX, NZ, 4)
+    half, x, z, low = np.meshgrid(*map(np.arange, sizes), indexing="ij")
+    degree = (8 * (NX * z + x) + 4 * half + low).reshape(BAND, 1)
     scale = math.sqrt(2.0 / ROWS)
     angles = np.pi * odd * degree / 2048, np.pi * odd * (2 * degree + 1) / 4096
     weight = np.where(degree == 0, math.sqrt(1.0 / ROWS), scale), scale
@@ -174,26 +175,29 @@
     return [snap[pl.ds(chip + 2 * owner + s, 1), :] for owner in (core, 1 - core) for s in range(2)]
 
 
-def prepare_kernel(own, other, snap, high, low, high_t, low_t, weights):
+def prepare_kernel(own, other, snap, high_t, low_t, weights, *blocks):
     z, x, core, _ = place_of_own()
-    weights[...] = jnp.concatenate(own_weights(snap, z, x, core) * 2, axis=0)
+    lines = [own_weights(snap, z, lax.rem(x - shift + NX, NX), core) for shift in range(NX)]
+    weights[...] = jnp.concatenate(sum(lines, []), axis=0)
     for s in range(4):
         source = own if s < 2 else other
         for k in range(4):
-            value = source[s % 2, k]
-            high[s, k], low[s, k] = split(value)
             place = slice(HALF * k, HALF * (k + 1))
-            high_t[s, :, place], low_t[s, :, place] = split(value.T)
+            high_t[s, :, place], low_t[s, :, place] = split(source[s % 2, k].T)
+            for shift, block in enumerate(blocks):
+                start = pl.multiple_of(lax.rem(x + shift, NX) * 32, 32)
+                block[s, k] = source[s % 2, k, pl.ds(start, 32), :]
 
 
 def prepare(own, other, snap):
-    straight = jax.ShapeDtypeStruct((4, 4, HALF, COLS), BF16)
     crossed = jax.ShapeDtypeStruct((4, COLS, KEEP // 2), BF16)
+    block = jax.ShapeDtypeStruct((4, 4, 32, COLS), F32)
+    outs = [crossed, crossed, jax.ShapeDtypeStruct((16, RANK), F32)] + [block] * NX
     return pl.pallas_call(
         prepare_kernel,
         in_specs=[VMEM] * 3,
-        out_specs=[VMEM] * 5,
-        out_shape=[straight, straight, crossed, crossed, jax.ShapeDtypeStruct((8, RANK), F32)],
+        out_specs=[VMEM] * len(outs),
+        out_shape=outs,
         compiler_params=room(12),
         cost_estimate=pl.CostEstimate(flops=10_000_000, bytes_accessed=6_000_000, transcendentals=0),
         name="prepare",
@@ -204,7 +208,7 @@
     for shift in range(NX):
         source = lax.rem(x - shift + NX, NX)
         for z in range(NZ):
-            start = pl.multiple_of(z * 64 + source * 16, 16)
+            start = pl.multiple_of(source * 128 + z * 16, 16)
             for half in range(2):
                 rows[half, pl.ds(start, 16), :] = pieces[shift][z, :, 128 * half : 128 * half + 128]
 
@@ -288,7 +292,7 @@
     return found / penalty, penalty
 
 
-FACTOR, DUAL = RANK + 16, RANK + 16 + COLS
+FACTOR, DUAL = RANK + 24, RANK + 24 + COLS
 
 
 def store_system(found, penalty, weights, inv):
@@ -340,13 +344,13 @@
 
 
 def col_kernel(*refs):
-    sources, inv, pieces = refs[:2], refs[2], refs[3:11]
-    new, dual_new, gram_half, blocks = refs[11], refs[12], refs[13], refs[14:18]
-    total, mapped, gram, high, low, sems = refs[18:]
+    sources, inv, pieces = refs[:4], refs[4], refs[5:13]
+    new, dual_new, gram_half, block = refs[13:17]
+    total, mapped, gram, held, sems = refs[17:]
     _, x, core, _ = place_of_own()
     copies = [
-        pltpu.make_async_copy(source, target, sems.at[at])
-        for at, (source, target) in enumerate(zip(sources, (high, low)))
+        pltpu.make_async_copy(source, held.at[at], sems.at[at])
+        for at, source in enumerate(sources)
     ]
     for copy in copies:
         copy.start()
@@ -365,39 +369,42 @@
     lines, weights = split(primal), inv[RANK + 8 : FACTOR]
     for copy in copies:
         copy.wait()
+    sums = 0.0
+    for shift in range(NX):
+        product = dot3(split(held[shift].reshape(512, COLS)), lines)
+        for s in range(4):
+            at = 4 * shift + s
+            sums += product[128 * s : 128 * s + 128] * weights[at : at + 1]
     for k in range(4):
-        line = sum(dot3((high[s, k], low[s, k]), lines) * weights[s : s + 1] for s in range(4))
         for half in range(2):
-            mapped[half, pl.ds(k, HALF, stride=4), :] = line[:, 128 * half : 128 * half + 128]
-    for shift, block in enumerate(blocks):
-        target = lax.rem(x + shift, NX)
-        for row in range(NZ):
-            start = pl.multiple_of(row * 64 + target * 16, 16)
-            for half in range(2):
-                block[row, :, 128 * half : 128 * half + 128] = mapped[half, pl.ds(start, 16), :]
-
-
-def col_update(high, low, inv, pieces):
+            line = sums[32 * k : 32 * k + 32, 128 * half : 128 * half + 128]
+            mapped[half, pl.ds(k, 32, stride=4), :] = line
+    for row in range(NZ):
+        for half in range(2):
+            place = slice(128 * half, 128 * half + 128)
+            block[row, :, place] = mapped[half, 16 * row : 16 * row + 16, :]
+
+
+def col_update(coefficients, inv, pieces):
     square = jax.ShapeDtypeStruct((COLS, RANK), F32)
     block = jax.ShapeDtypeStruct((NZ, 16, RANK), F32)
-    outs = [square, square, jax.ShapeDtypeStruct((128, RANK), F32)] + [block] * NX
+    outs = [square, square, jax.ShapeDtypeStruct((128, RANK), F32), block]
     return pl.pallas_call(
         col_kernel,
-        in_specs=[pl.BlockSpec(memory_space=pltpu.HBM)] * 2 + [VMEM] * 9,
+        in_specs=[pl.BlockSpec(memory_space=pltpu.HBM)] * 4 + [VMEM] * 9,
         out_specs=[VMEM] * len(outs),
         out_shape=outs,
         scratch_shapes=[
             pltpu.VMEM((COLS, RANK), F32),
-            pltpu.VMEM((2, KEEP // 2, 128), F32),
+            pltpu.VMEM((2, 128, 128), F32),
             pltpu.VMEM((RANK, RANK), F32),
-            pltpu.VMEM((4, 4, HALF, COLS), BF16),
-            pltpu.VMEM((4, 4, HALF, COLS), BF16),
-            pltpu.SemaphoreType.DMA((2,)),
+            pltpu.VMEM((NX, 4, 4, 32, COLS), F32),
+            pltpu.SemaphoreType.DMA((4,)),
         ],
         cost_estimate=pl.CostEstimate(flops=1_500_000_000, bytes_accessed=5_000_000, transcendentals=0),
         compiler_params=room(16),
         name="col_update",
-    )(high, low, inv, *pieces)
+    )(*coefficients, inv, *pieces)
 
 
 def gram_sum_kernel(*refs):
@@ -507,34 +514,34 @@
     )(block)
 
 
-def body(snapshots, snap_factor, row_factor, col_factor, row_dual, col_dual):
+def around(array, axis):
+    moved = []
+    for by in range(1, 4):
+        given = array[by] if isinstance(array, list) else array
+        moved.append(shifted(given, axis, 4, by))
+    return moved
+
+
+def update(snapshots, snap_factor, row_factor, col_factor, row_dual, col_dual):
     mine = copied_along([row_factor], "z", NZ)
     own, send = dct(snapshots)
     mine, own, send = lax.optimization_barrier((mine, own, send))
-    lines = [mine] + [shifted(mine, "x", NX, by) for by in range(1, NX)]
-    high, low, high_t, low_t, weights = prepare(own, shifted(send, "c", NC, 1), snap_factor)
+    lines = [mine, *around(mine, "x")]
+    high_t, low_t, weights, *blocks = prepare(own, shifted(send, "c", NC, 1), snap_factor)
     keep, send = totals(high_t, low_t, weights, lines)
     gram = row_gram(lines)
     other = shifted(gram, "c", NC, 1)
     args = snap_factor, weights, gram, other
     inv = system(col_system_kernel, DUAL + COLS, *args, col_factor, col_dual)
-    parts = summed([keep, shifted(send, "c", NC, 1)], (32, RANK), NX)
-    parts = [parts[0]] + [shifted(parts[by], "x", NX, by) for by in range(1, NX)]
-    chunk = copied_along(parts, "z", NZ)
+    parts = list(summed([keep, shifted(send, "c", NC, 1)], (32, RANK), NX))
+    chunk = copied_along([parts[0], *around(parts, "x")], "z", NZ)
+    coefficients = [blocks[0], *around(list(blocks), "x")]
     chunk, inv = lax.optimization_barrier((chunk, inv))
     chunk = folded(chunk)
-    pieces = [chunk] + [shifted(chunk, "x", NX, by) for by in range(1, NX)]
+    pieces = [chunk, *around(chunk, "x")]
     pieces = pieces + [shifted(piece, "c", NC, 1) for piece in pieces]
-    col_new, col_dual_new, gram_half, *blocks = col_update(
-        high, low, inv, pieces
-    )
-    grams = [gram_half]
-    for by in range(1, NX):
-        blocks[by] = shifted(blocks[by], "x", NX, by)
-    for by in range(1, NY):
-        grams.append(shifted(gram_half, "y", NY, by))
-    block = summed(blocks, (NZ, 16, RANK))[0]
-    _, *grams = lax.optimization_barrier((block, *grams))
+    col_new, col_dual_new, gram_half, block = col_update(coefficients, inv, pieces)
+    grams = [gram_half, *around(gram_half, "y")]
     gram_mine = gram_sum(grams)
     other = shifted(gram_mine, "c", NC, 1)
     args = snap_factor, weights, gram_mine, other
@@ -550,7 +557,7 @@
 def solution(mesh):
     fine = Mesh(mesh.devices.reshape(NZ, NX, NC, NY), ("z", "x", "c", "y"))
     return jax.shard_map(
-        body,
+        update,
         mesh=fine,
         in_specs=(
             P(WIDE, None, "y"),

time: 115 us -> 134 us (1.17)
  the two profiles are of different devices: /device:TPU:24 before, /device:TPU:8 now
where the time goes in v4:
time: 134 us; the launch traced here: 132 us
  waiting for transfers between devices  49.7 us (37%)
  starting transfers between devices  45.6 us (34%)
  Pallas kernels  27.3 us (20%)
  local copies, waits for them, and re-layouts  8.51 us (6%)
    ppermute x23, waiting for transfers between devices, shifted(): lax.ppermute(array, axis, [(i, (i + by) % size) for i in range(size)])  35.4 us
    ppermute x23, starting transfers between devices, shifted(): lax.ppermute(array, axis, [(i, (i + by) % size) for i in range(size)])  22 us
    all_to_all x2, starting transfers between devices, copied_along(): return lax.all_to_all(whole, axes, 0, 0, tiled=True)  15.7 us
    unnamed x24, local copies, waits for them, and re-layouts  8.51 us
    pallas_call x2, Pallas kernels, system(): pl.pallas_call(kernel, in_specs=[VMEM] * len(args), out_specs=VMEM, out_s...  8.47 us
    pallas_call x1, Pallas kernels, dct(): pl.pallas_call(dct_kernel, grid=(steps,), in_specs=[pl.BlockSpec(block, l...  7.33 us
    all_to_all x1, waiting for transfers between devices, update(): block = lax.all_to_all(block, 'z', 0, 0, tiled=True)  6 us
    all_to_all x1, starting transfers between devices, update(): block = lax.all_to_all(block, 'z', 0, 0, tiled=True)  5.78 us
  transfers between devices with their start and end apart: 28, of which 14 were waited for; matrix products, arithmetic and copies ran while one was open for 0% of the time, Pallas kernels for 15%

profile of v4, /device:TPU:8, one launch (start us, length us, event | category | flops | bytes accessed | tf_op | source)
XLA Modules:
  0.0 132.0 jit_solution(8985262681538404431)
XLA Ops:
  2.0 8.5 %all-to-all-start = ((f32[8,16,256]{2,1,0:T(8,128)}), f32[8,16,256]{2,1,0:T(8,128)S(1)}, u32[]{:S(2)}, u32[]{:S(2)}) async-start(f32[8,16,256]{2,1,0:T(8,128)} %spread.2), calls=%async_computation | async-start | bytes 262144 | tf_op jit(solution)/shard_map/all_to_all | solution.py:498
  12.5 7.3 %dct.1 = (f32[2,4,128,256]{3,2,1,0:T(8,128)S(1)}, f32[2,4,128,256]{3,2,1,0:T(8,128)S(1)}) custom-call(f32[2,4096,256]{2,1,0:T(8,128)} %x3.1, f32[2,4096,256]{2,1,0:T(8,128)} %x3.1, f32[2,4096,256]{2,1,0:T(8,128)} %x3.1, f32[2,4096,256]{2,1,0:T(8,128)} %x3.1, f32[4,256,256]{2,1,0:T(8,128)S(1)} %copy-done, f32[10,8,128]{2,1,0:T(8,128)S(1)} %copy-done.4), custom_call_target="tpu_custom_call" | custom-call | flops 7000000000 | bytes 13000000 | tf_op jit(solution)/shard_map/dct/pallas_call | solution.py:145
  19.9 1.6 %collective-permute-start.4 = (f32[8,16,256]{2,1,0:T(8,128)S(1)}, f32[8,16,256]{2,1,0:T(8,128)S(1)}, u32[]{:S(2)}, u32[]{:S(2)}) collective-permute-start(f32[8,16,256]{2,1,0:T(8,128)S(1)} %all-to-all-done.refs_0_), channel_id=1, source_target_pairs={{0,8},{8,16},{16,24},{24,0},{1,9},{9,17},{17,25},{25,1},{2,10},{10... | collective-permute-start | bytes 393224 | tf_op jit(solution)/shard_map/ppermute | solution.py:452
  21.5 2.7 %collective-permute-start.5 = (f32[8,16,256]{2,1,0:T(8,128)S(1)}, f32[8,16,256]{2,1,0:T(8,128)S(1)}, u32[]{:S(2)}, u32[]{:S(2)}) collective-permute-start(f32[8,16,256]{2,1,0:T(8,128)S(1)} %all-to-all-done.refs_0_), channel_id=1, source_target_pairs={{0,16},{8,24},{16,0},{24,8},{1,17},{9,25},{17,1},{25,9},{2,18},{10... | collective-permute-start | bytes 393224 | tf_op jit(solution)/shard_map/ppermute | solution.py:452
  25.7 1.6 %prepare.1 = (bf16[4,256,512]{2,1,0:T(8,128)(2,1)S(1)}, bf16[4,256,512]{2,1,0:T(8,128)(2,1)S(1)}, f32[16,256]{1,0:T(8,128)S(1)}, f32[4,4,32,256]{3,2,1,0:T(8,128...) custom-call(f32[2,4,128,256]{3,2,1,0:T(8,128)S(1)} %get-tuple-element.34.own, ...), custom_call_target="tpu_custom_call" | custom-call | flops 10000000 | bytes 6000000 | tf_op jit(solution)/shard_map/prepare/pallas_call | solution.py:196
  27.2 3.6 %collective-permute-done.5.refs_2_ = f32[8,16,256]{2,1,0:T(8,128)S(1)} collective-permute-done((f32[8,16,256]{2,1,0:T(8,128)S(1)}, f32[8,16,256]{2,1,0:T(8,128)S(1)}, u32[]{:S(2)}, u32[]{:S(2)}) %collective-permute-start.5) | collective-permute-done | bytes 131104 | tf_op jit(solution)/shard_map/ppermute | solution.py:452
  30.9 1.8 %totals.1 = (f32[4,32,256]{2,1,0:T(8,128)S(1)}, f32[4,32,256]{2,1,0:T(8,128)S(1)}) custom-call(bf16[4,256,512]{2,1,0:T(8,128)(2,1)S(1)} %get-tuple-element.40.high_t, bf16[4,256,512]{2,1,0:T(8,128)(2,1)S(1)} %get-tuple-element.41.low_t, f32[16,256]{1,0:T(8,128)S(1)} %get-tuple-element.42.weights, f32[8,16,256]{2,1,0:T(8,128)S(1)} %all-to-all-done.refs_0_, ...), custom_call_target="tpu_custom_call" | custom-call | flops 800000000 | bytes 4000000 | tf_op jit(solution)/shard_map/totals/pallas_call | solution.py:237
  32.8 1.5 %row_gram.1.mine = f32[256,256]{1,0:T(8,128)} custom-call(f32[8,16,256]{2,1,0:T(8,128)S(1)} %all-to-all-done.refs_0_, f32[8,16,256]{2,1,0:T(8,128)S(1)} %collective-permute-done.4.refs_1_, f32[8,16,256]{2,1,0:T(8,128)S(1)} %collective-permute-done.5.refs_2_, f32[8,16,256]{2,1,0:T(8,128)S(1)} %collective-permute-done.6.refs_3_), custom_call_target="tpu_custom_call" | custom-call | flops 400000000 | bytes 800000 | tf_op jit(solution)/shard_map/row_gram/pallas_call | solution.py:257
  34.8 2.3 %collective-permute-start.10 = (f32[32,256]{1,0:T(8,128)S(1)}, f32[32,256]{1,0:T(8,128)S(1)}, u32[]{:S(2)}, u32[]{:S(2)}) collective-permute-start(f32[32,256]{1,0:T(8,128)S(1)} %get-tuple-element.49), channel_id=1, source_target_pairs={{0,24},{8,0},{16,8},{24,16},{1,25},{9,1},{17,9},{25,17},{2,26},{10... | collective-permute-start | bytes 98312 | tf_op jit(solution)/shard_map/ppermute | solution.py:452
  38.2 3.6 %collective-permute-start.9 = (f32[32,256]{1,0:T(8,128)S(1)}, f32[32,256]{1,0:T(8,128)S(1)}, u32[]{:S(2)}, u32[]{:S(2)}) collective-permute-start(f32[32,256]{1,0:T(8,128)S(1)} %get-tuple-element.48), channel_id=1, source_target_pairs={{0,16},{8,24},{16,0},{24,8},{1,17},{9,25},{17,1},{25,9},{2,18},{10... | collective-permute-start | bytes 98312 | tf_op jit(solution)/shard_map/ppermute | solution.py:452
  41.9 22.9 %collective-permute-done.8.refs_1_ = f32[32,256]{1,0:T(8,128)S(1)} collective-permute-done((f32[32,256]{1,0:T(8,128)S(1)}, f32[32,256]{1,0:T(8,128)S(1)}, u32[]{:S(2)}, u32[]{:S(2)}) %collective-permute-start.8) | collective-permute-done | bytes 32800 | tf_op jit(solution)/shard_map/ppermute | solution.py:452
  65.5 7.2 %all-to-all-start.1 = ((f32[8,32,256]{2,1,0:T(8,128)}), f32[8,32,256]{2,1,0:T(8,128)S(1)}, u32[]{:S(2)}, u32[]{:S(2)}) async-start(f32[8,32,256]{2,1,0:T(8,128)} %spread.3), calls=%async_computation.1 | async-start | bytes 524288 | tf_op jit(solution)/shard_map/all_to_all | solution.py:498
  74.6 4.8 %shard_map.111.refs_4_ = f32[792,256]{1,0:T(8,128)S(1)} custom-call(f32[128,256]{1,0:T(8,128)S(1)} %copy-done.1, f32[16,256]{1,0:T(8,128)S(1)} %get-tuple-element.42.weights, f32[256,256]{1,0:T(8,128)} %row_gram.1.mine, f32[256,256]{1,0:T(8,128)} %collective-permute-done.11.other, f32[256,256]{1,0:T(8,128)S(1)} %copy-done.8, f32[256,256]{1,0:T(8,128)S(1)} %copy-done.9), custom_call_target="tpu_custom_call" | custom-call | flops 3000000000 | bytes 1000000 | tf_op jit(solution)/shard_map/pallas_call | solution.py:321
  80.3 2.9 %all-to-all-done.1.block = f32[8,32,256]{2,1,0:T(8,128)S(1)} async-done(((f32[8,32,256]{2,1,0:T(8,128)}), f32[8,32,256]{2,1,0:T(8,128)S(1)}, u32[]{:S(2)}, u32[]{:S(2)}) %all-to-all-start.1) | async-done | bytes 262176 | tf_op jit(solution)/shard_map/all_to_all | solution.py:498
  84.3 2.2 %collective-permute-start.14 = (f32[32,256]{1,0:T(8,128)S(1)}, f32[32,256]{1,0:T(8,128)S(1)}, u32[]{:S(2)}, u32[]{:S(2)}) collective-permute-start(f32[32,256]{1,0:T(8,128)S(1)} %folded.2.refs_5_), channel_id=1, source_target_pairs={{0,24},{8,0},{16,8},{24,16},{1,25},{9,1},{17,9},{25,17},{2,26},{10... | collective-permute-start | bytes 98312 | tf_op jit(solution)/shard_map/ppermute | solution.py:452
  93.0 3.8 %col_update.1 = (f32[256,256]{1,0:T(8,128)}, f32[256,256]{1,0:T(8,128)}, f32[128,256]{1,0:T(8,128)S(1)}, f32[8,16,256]{2,1,0:T(8,128)}) custom-call(f32[4,4,32,256]{3,2,1,0:T(8,128)S(1)} %get-tuple-element.36.refs_0_, f32[4,4,32,256]{3,2,1,0:T(8,128)S(1)} %collective-permute-done.1.refs_1_, f32[4,4,32,256]{3,2,1,0:T(8,128)S(1)} %copy-done.7, ...), custom_call_target="tpu_custom_call" | custom-call | flops 1500000000 | bytes 5000000 | tf_op jit(solution)/shard_map/col_update/pallas_call | solution.py:392
  96.8 1.6 %collective-permute-start.19 = (f32[128,256]{1,0:T(8,128)S(1)}, f32[128,256]{1,0:T(8,128)S(1)}, u32[]{:S(2)}, u32[]{:S(2)}) collective-permute-start(f32[128,256]{1,0:T(8,128)S(1)} %get-tuple-element.53.refs_0_), channel_id=1, source_target_pairs={{0,1},{1,2},{2,3},{3,0},{4,5},{5,6},{6,7},{7,4},{8,9},{9,10},{10,1... | collective-permute-start | bytes 393224 | tf_op jit(solution)/shard_map/ppermute | solution.py:452
  99.4 2.4 %collective-permute-start.21 = (f32[128,256]{1,0:T(8,128)S(1)}, f32[128,256]{1,0:T(8,128)S(1)}, u32[]{:S(2)}, u32[]{:S(2)}) collective-permute-start(f32[128,256]{1,0:T(8,128)S(1)} %get-tuple-element.53.refs_0_), channel_id=1, source_target_pairs={{0,3},{1,0},{2,1},{3,2},{4,7},{5,4},{6,5},{7,6},{8,11},{9,8},{10,9... | collective-permute-start | bytes 393224 | tf_op jit(solution)/shard_map/ppermute | solution.py:452
  102.7 3.7 %collective-permute-done.20.refs_2_ = f32[128,256]{1,0:T(8,128)S(1)} collective-permute-done((f32[128,256]{1,0:T(8,128)S(1)}, f32[128,256]{1,0:T(8,128)S(1)}, u32[]{:S(2)}, u32[]{:S(2)}) %collective-permute-start.20) | collective-permute-done | bytes 131104 | tf_op jit(solution)/shard_map/ppermute | solution.py:452
  107.6 5.8 %all-to-all-start.2 = ((f32[8,16,256]{2,1,0:T(8,128)}), f32[8,16,256]{2,1,0:T(8,128)S(1)}, u32[]{:S(2)}, u32[]{:S(2)}) async-start(f32[8,16,256]{2,1,0:T(8,128)} %get-tuple-element.52), calls=%async_computation.2 | async-start | bytes 262144 | tf_op jit(solution)/shard_map/all_to_all | solution.py:549
  113.4 3.7 %shard_map.112.inv = f32[280,256]{1,0:T(8,128)S(1)} custom-call(f32[128,256]{1,0:T(8,128)S(1)} %copy-done.1, f32[16,256]{1,0:T(8,128)S(1)} %get-tuple-element.42.weights, f32[128,256]{1,0:T(8,128)S(1)} %gram_sum.1.mine, f32[128,256]{1,0:T(8,128)S(1)} %collective-permute-done.22.other), custom_call_target="tpu_custom_call" | custom-call | flops 3000000000 | bytes 1000000 | tf_op jit(solution)/shard_map/pallas_call | solution.py:321
  117.1 6.0 %all-to-all-done.2.block = f32[8,16,256]{2,1,0:T(8,128)S(1)} async-done(((f32[8,16,256]{2,1,0:T(8,128)}), f32[8,16,256]{2,1,0:T(8,128)S(1)}, u32[]{:S(2)}, u32[]{:S(2)}) %all-to-all-start.2) | async-done | bytes 131104 | tf_op jit(solution)/shard_map/all_to_all | solution.py:549
  124.0 3.0 %collective-permute-done.23.refs_1_ = f32[16,256]{1,0:T(8,128)S(1)} collective-permute-done((f32[16,256]{1,0:T(8,128)S(1)}, f32[16,256]{1,0:T(8,128)S(1)}, u32[]{:S(2)}, u32[]{:S(2)}) %collective-permute-start.23) | collective-permute-done | bytes 16416 | tf_op jit(solution)/shard_map/ppermute | solution.py:456
  128.2 2.4 %collective-permute-done.24.other = f32[16,256]{1,0:T(8,128)S(1)} collective-permute-done((f32[16,256]{1,0:T(8,128)S(1)}, f32[16,256]{1,0:T(8,128)S(1)}, u32[]{:S(2)}, u32[]{:S(2)}) %collective-permute-start.24) | collective-permute-done | bytes 16416 | tf_op jit(solution)/shard_map/ppermute | solution.py:456
  (71 shorter events, 24.3 us)
Async XLA Ops:
  2.0 17.8 %all-to-all-start = ((f32[8,16,256]{2,1,0:T(8,128)}), f32[8,16,256]{2,1,0:T(8,128)S(1)}, u32[]{:S(2)}, u32[]{:S(2)}) async-start(f32[8,16,256]{2,1,0:T(8,128)} %spread.2), calls=%async_computation | async-start | bytes 262144 | tf_op jit(solution)/shard_map/all_to_all | solution.py:498
  19.8 5.8 %collective-permute-start = (f32[2,4,128,256]{3,2,1,0:T(8,128)S(1)}, f32[2,4,128,256]{3,2,1,0:T(8,128)S(1)}, u32[]{:S(2)}, u32[]{:S(2)}) collective-permute-start(f32[2,4,128,256]{3,2,1,0:T(8,128)S(1)} %get-tuple-element.35), channel_id=1, source_target_pairs={{0,4},{4,0},{1,5},{5,1},{2,6},{6,2},{3,7},{7,3},{8,12},{12,8},{9,1... | collective-permute-start | bytes 3145736 | tf_op jit(solution)/shard_map/ppermute | solution.py:452
  19.9 7.3 %collective-permute-start.4 = (f32[8,16,256]{2,1,0:T(8,128)S(1)}, f32[8,16,256]{2,1,0:T(8,128)S(1)}, u32[]{:S(2)}, u32[]{:S(2)}) collective-permute-start(f32[8,16,256]{2,1,0:T(8,128)S(1)} %all-to-all-done.refs_0_), channel_id=1, source_target_pairs={{0,8},{8,16},{16,24},{24,0},{1,9},{9,17},{17,25},{25,1},{2,10},{10... | collective-permute-start | bytes 393224 | tf_op jit(solution)/shard_map/ppermute | solution.py:452
  21.5 9.3 %collective-permute-start.5 = (f32[8,16,256]{2,1,0:T(8,128)S(1)}, f32[8,16,256]{2,1,0:T(8,128)S(1)}, u32[]{:S(2)}, u32[]{:S(2)}) collective-permute-start(f32[8,16,256]{2,1,0:T(8,128)S(1)} %all-to-all-done.refs_0_), channel_id=1, source_target_pairs={{0,16},{8,24},{16,0},{24,8},{1,17},{9,25},{17,1},{25,9},{2,18},{10... | collective-permute-start | bytes 393224 | tf_op jit(solution)/shard_map/ppermute | solution.py:452
  24.2 6.6 %collective-permute-start.6 = (f32[8,16,256]{2,1,0:T(8,128)S(1)}, f32[8,16,256]{2,1,0:T(8,128)S(1)}, u32[]{:S(2)}, u32[]{:S(2)}) collective-permute-start(f32[8,16,256]{2,1,0:T(8,128)S(1)} %all-to-all-done.refs_0_), channel_id=1, source_target_pairs={{0,24},{8,0},{16,8},{24,16},{1,25},{9,1},{17,9},{25,17},{2,26},{10... | collective-permute-start | bytes 393224 | tf_op jit(solution)/shard_map/ppermute | solution.py:452
  34.3 38.4 %collective-permute-start.11 = (f32[256,256]{1,0:T(8,128)}, f32[256,256]{1,0:T(8,128)}, u32[]{:S(2)}, u32[]{:S(2)}) collective-permute-start(f32[256,256]{1,0:T(8,128)} %row_gram.1.mine), channel_id=1, source_target_pairs={{0,4},{4,0},{1,5},{5,1},{2,6},{6,2},{3,7},{7,3},{8,12},{12,8},{9,1... | collective-permute-start | bytes 786440 | tf_op jit(solution)/shard_map/ppermute | solution.py:452
  34.8 7.0 %collective-permute-start.10 = (f32[32,256]{1,0:T(8,128)S(1)}, f32[32,256]{1,0:T(8,128)S(1)}, u32[]{:S(2)}, u32[]{:S(2)}) collective-permute-start(f32[32,256]{1,0:T(8,128)S(1)} %get-tuple-element.49), channel_id=1, source_target_pairs={{0,24},{8,0},{16,8},{24,16},{1,25},{9,1},{17,9},{25,17},{2,26},{10... | collective-permute-start | bytes 98312 | tf_op jit(solution)/shard_map/ppermute | solution.py:452
  37.1 47.2 %collective-permute-start.1 = (f32[4,4,32,256]{3,2,1,0:T(8,128)}, f32[4,4,32,256]{3,2,1,0:T(8,128)S(1)}, u32[]{:S(2)}, u32[]{:S(2)}) collective-permute-start(f32[4,4,32,256]{3,2,1,0:T(8,128)} %get-tuple-element.37), channel_id=1, source_target_pairs={{0,8},{8,16},{16,24},{24,0},{1,9},{9,17},{17,25},{25,1},{2,10},{10... | collective-permute-start | bytes 1572872 | tf_op jit(solution)/shard_map/ppermute | solution.py:452
  37.1 27.6 %collective-permute-start.8 = (f32[32,256]{1,0:T(8,128)S(1)}, f32[32,256]{1,0:T(8,128)S(1)}, u32[]{:S(2)}, u32[]{:S(2)}) collective-permute-start(f32[32,256]{1,0:T(8,128)S(1)} %get-tuple-element.47), channel_id=1, source_target_pairs={{0,8},{8,16},{16,24},{24,0},{1,9},{9,17},{17,25},{25,1},{2,10},{10... | collective-permute-start | bytes 98312 | tf_op jit(solution)/shard_map/ppermute | solution.py:452
  38.2 26.5 %collective-permute-start.9 = (f32[32,256]{1,0:T(8,128)S(1)}, f32[32,256]{1,0:T(8,128)S(1)}, u32[]{:S(2)}, u32[]{:S(2)}) collective-permute-start(f32[32,256]{1,0:T(8,128)S(1)} %get-tuple-element.48), channel_id=1, source_target_pairs={{0,16},{8,24},{16,0},{24,8},{1,17},{9,25},{17,1},{25,9},{2,18},{10... | collective-permute-start | bytes 98312 | tf_op jit(solution)/shard_map/ppermute | solution.py:452
  41.8 44.7 %collective-permute-start.2 = (f32[4,4,32,256]{3,2,1,0:T(8,128)S(1)}, f32[4,4,32,256]{3,2,1,0:T(8,128)S(1)}, u32[]{:S(2)}, u32[]{:S(2)}) collective-permute-start(f32[4,4,32,256]{3,2,1,0:T(8,128)S(1)} %get-tuple-element.38), channel_id=1, source_target_pairs={{0,16},{8,24},{16,0},{24,8},{1,17},{9,25},{17,1},{25,9},{2,18},{10... | collective-permute-start | bytes 1572872 | tf_op jit(solution)/shard_map/ppermute | solution.py:452
  65.5 17.7 %all-to-all-start.1 = ((f32[8,32,256]{2,1,0:T(8,128)}), f32[8,32,256]{2,1,0:T(8,128)S(1)}, u32[]{:S(2)}, u32[]{:S(2)}) async-start(f32[8,32,256]{2,1,0:T(8,128)} %spread.3), calls=%async_computation.1 | async-start | bytes 524288 | tf_op jit(solution)/shard_map/all_to_all | solution.py:498
  72.7 16.9 %collective-permute-start.3 = (f32[4,4,32,256]{3,2,1,0:T(8,128)S(1)}, f32[4,4,32,256]{3,2,1,0:T(8,128)}, u32[]{:S(2)}, u32[]{:S(2)}) collective-permute-start(f32[4,4,32,256]{3,2,1,0:T(8,128)S(1)} %get-tuple-element.39), channel_id=1, source_target_pairs={{0,24},{8,0},{16,8},{24,16},{1,25},{9,1},{17,9},{25,17},{2,26},{10... | collective-permute-start | bytes 1572872 | tf_op jit(solution)/shard_map/ppermute | solution.py:452
  83.2 5.2 %collective-permute-start.12 = (f32[32,256]{1,0:T(8,128)S(1)}, f32[32,256]{1,0:T(8,128)S(1)}, u32[]{:S(2)}, u32[]{:S(2)}) collective-permute-start(f32[32,256]{1,0:T(8,128)S(1)} %folded.2.refs_5_), channel_id=1, source_target_pairs={{0,8},{8,16},{16,24},{24,0},{1,9},{9,17},{17,25},{25,1},{2,10},{10... | collective-permute-start | bytes 98312 | tf_op jit(solution)/shard_map/ppermute | solution.py:452
  83.3 5.5 %collective-permute-start.13 = (f32[32,256]{1,0:T(8,128)S(1)}, f32[32,256]{1,0:T(8,128)S(1)}, u32[]{:S(2)}, u32[]{:S(2)}) collective-permute-start(f32[32,256]{1,0:T(8,128)S(1)} %folded.2.refs_5_), channel_id=1, source_target_pairs={{0,16},{8,24},{16,0},{24,8},{1,17},{9,25},{17,1},{25,9},{2,18},{10... | collective-permute-start | bytes 98312 | tf_op jit(solution)/shard_map/ppermute | solution.py:452
  84.3 5.3 %collective-permute-start.14 = (f32[32,256]{1,0:T(8,128)S(1)}, f32[32,256]{1,0:T(8,128)S(1)}, u32[]{:S(2)}, u32[]{:S(2)}) collective-permute-start(f32[32,256]{1,0:T(8,128)S(1)} %folded.2.refs_5_), channel_id=1, source_target_pairs={{0,24},{8,0},{16,8},{24,16},{1,25},{9,1},{17,9},{25,17},{2,26},{10... | collective-permute-start | bytes 98312 | tf_op jit(solution)/shard_map/ppermute | solution.py:452
  87.4 2.3 %collective-permute-start.15 = (f32[32,256]{1,0:T(8,128)S(1)}, f32[32,256]{1,0:T(8,128)S(1)}, u32[]{:S(2)}, u32[]{:S(2)}) collective-permute-start(f32[32,256]{1,0:T(8,128)S(1)} %folded.2.refs_5_), channel_id=1, source_target_pairs={{0,4},{4,0},{1,5},{5,1},{2,6},{6,2},{3,7},{7,3},{8,12},{12,8},{9,1... | collective-permute-start | bytes 98312 | tf_op jit(solution)/shard_map/ppermute | solution.py:452
  96.8 5.8 %collective-permute-start.19 = (f32[128,256]{1,0:T(8,128)S(1)}, f32[128,256]{1,0:T(8,128)S(1)}, u32[]{:S(2)}, u32[]{:S(2)}) collective-permute-start(f32[128,256]{1,0:T(8,128)S(1)} %get-tuple-element.53.refs_0_), channel_id=1, source_target_pairs={{0,1},{1,2},{2,3},{3,0},{4,5},{5,6},{6,7},{7,4},{8,9},{9,10},{10,1... | collective-permute-start | bytes 393224 | tf_op jit(solution)/shard_map/ppermute | solution.py:452
  98.5 7.9 %collective-permute-start.20 = (f32[128,256]{1,0:T(8,128)S(1)}, f32[128,256]{1,0:T(8,128)S(1)}, u32[]{:S(2)}, u32[]{:S(2)}) collective-permute-start(f32[128,256]{1,0:T(8,128)S(1)} %get-tuple-element.53.refs_0_), channel_id=1, source_target_pairs={{0,2},{1,3},{2,0},{3,1},{4,6},{5,7},{6,4},{7,5},{8,10},{9,11},{10,... | collective-permute-start | bytes 393224 | tf_op jit(solution)/shard_map/ppermute | solution.py:452
  99.4 8.0 %collective-permute-start.21 = (f32[128,256]{1,0:T(8,128)S(1)}, f32[128,256]{1,0:T(8,128)S(1)}, u32[]{:S(2)}, u32[]{:S(2)}) collective-permute-start(f32[128,256]{1,0:T(8,128)S(1)} %get-tuple-element.53.refs_0_), channel_id=1, source_target_pairs={{0,3},{1,0},{2,1},{3,2},{4,7},{5,4},{6,5},{7,6},{8,11},{9,8},{10,9... | collective-permute-start | bytes 393224 | tf_op jit(solution)/shard_map/ppermute | solution.py:452
  107.5 5.9 %collective-permute-start.22 = (f32[128,256]{1,0:T(8,128)S(1)}, f32[128,256]{1,0:T(8,128)S(1)}, u32[]{:S(2)}, u32[]{:S(2)}) collective-permute-start(f32[128,256]{1,0:T(8,128)S(1)} %gram_sum.1.mine), channel_id=1, source_target_pairs={{0,4},{4,0},{1,5},{5,1},{2,6},{6,2},{3,7},{7,3},{8,12},{12,8},{9,1... | collective-permute-start | bytes 393224 | tf_op jit(solution)/shard_map/ppermute | solution.py:452
  107.6 15.5 %all-to-all-start.2 = ((f32[8,16,256]{2,1,0:T(8,128)}), f32[8,16,256]{2,1,0:T(8,128)S(1)}, u32[]{:S(2)}, u32[]{:S(2)}) async-start(f32[8,16,256]{2,1,0:T(8,128)} %get-tuple-element.52), calls=%async_computation.2 | async-start | bytes 262144 | tf_op jit(solution)/shard_map/all_to_all | solution.py:549
  123.1 3.8 %collective-permute-start.23 = (f32[16,256]{1,0:T(8,128)S(1)}, f32[16,256]{1,0:T(8,128)S(1)}, u32[]{:S(2)}, u32[]{:S(2)}) collective-permute-start(f32[16,256]{1,0:T(8,128)S(1)} %folded.3.refs_0_), channel_id=1, source_target_pairs={{0,1},{1,0},{2,3},{3,2},{4,5},{5,4},{6,7},{7,6},{8,9},{9,8},{10,11... | collective-permute-start | bytes 49160 | tf_op jit(solution)/shard_map/ppermute | solution.py:456
  126.9 3.7 %collective-permute-start.24 = (f32[16,256]{1,0:T(8,128)S(1)}, f32[16,256]{1,0:T(8,128)S(1)}, u32[]{:S(2)}, u32[]{:S(2)}) collective-permute-start(f32[16,256]{1,0:T(8,128)S(1)} %summed.3.mine), channel_id=1, source_target_pairs={{0,3},{1,2},{2,1},{3,0},{4,7},{5,6},{6,5},{7,4},{8,11},{9,10},{10,... | collective-permute-start | bytes 49160 | tf_op jit(solution)/shard_map/ppermute | solution.py:456
  (16 other events, 102.8 us)

commit v5 on v4

--- a/solution.py
+++ b/solution.py
@@ -41,8 +41,10 @@
     near = np.stack([np.arange(8)[:, None] % 4 * lanes, np.arange(8)[:, None] % 4 * lanes + 4])
     ahead = [f(a) for a in (np.pi * near / 4, np.pi * (2 * near + 1) / 8) for f in (np.cos, np.sin)]
     turn = np.pi * (2 * eight + 1) / 8192
-    tables = np.stack(base), np.concatenate([*ahead, [np.cos(turn), np.sin(turn)]])
-    return [jnp.asarray(table.astype(np.float32)) for table in tables]
+    turns = [np.cos(turn), np.sin(turn)] * 2
+    parts = [base, [np.concatenate(part) for part in ahead], turns]
+    parts = [np.stack([np.tile(p, (1, STEP // p.shape[1])) for p in part]) for part in parts]
+    return jnp.asarray(np.concatenate(parts, axis=1).astype(np.float32))
 
 
 def room(mebibytes):
@@ -79,65 +81,61 @@
     return jnp.concatenate(tiles, axis=0)
 
 
-def dct_kernel(x0, x1, x2, x3, *refs):
-    base, ahead, keep, send = refs[:4]
-    held, rotated, total = refs[4], refs[5:7], refs[7]
+def dct_kernel(x0, x1, x2, x3, table, keep, send, held, rotated, total):
     step = pl.program_id(0)
 
     @pl.when(step == 0)
     def _():
         total[...] = jnp.zeros_like(total)
-        held[...] = base[...]
-        cos, sin = ahead[8], ahead[9]
+        held[...] = table[:, :BAND]
+        cos, sin = table[0, BAND + 16 :, :128], table[1, BAND + 16 :, :128]
         for t in range(STEP // 8):
             by_cos, by_sin = math.cos(math.pi * t / 512), math.sin(math.pi * t / 512)
-            rotated[0][8 * t : 8 * t + 8, :] = cos * by_cos - sin * by_sin
-            rotated[1][8 * t : 8 * t + 8, :] = sin * by_cos + cos * by_sin
+            rotated[0, 8 * t : 8 * t + 8, :] = cos * by_cos - sin * by_sin
+            rotated[1, 8 * t : 8 * t + 8, :] = sin * by_cos + cos * by_sin
 
     @pl.when(step > 0)
     def _():
         for pair in range(2):
             cos, sin = held[2 * pair], held[2 * pair + 1]
             by_cos, by_sin = (
-                jnp.concatenate([twice(ahead[at])] * 16 + [twice(ahead[at + 1])] * 16, axis=0)
-                for at in (4 * pair, 4 * pair + 2)
+                jnp.concatenate(
+                    [table[at, BAND : BAND + 8]] * 16 + [table[at, BAND + 8 : BAND + 16]] * 16, axis=0
+                )
+                for at in (2 * pair, 2 * pair + 1)
             )
             held[2 * pair] = cos * by_cos - sin * by_sin
             held[2 * pair + 1] = sin * by_cos + cos * by_sin
-        cos, sin = rotated[0][...], rotated[1][...]
+        cos, sin = rotated[0], rotated[1]
         by_cos, by_sin = math.cos(math.pi / 16), math.sin(math.pi / 16)
-        rotated[0][...] = cos * by_cos - sin * by_sin
-        rotated[1][...] = sin * by_cos + cos * by_sin
+        rotated[0] = cos * by_cos - sin * by_sin
+        rotated[1] = sin * by_cos + cos * by_sin
 
     plain, even, odd = split(held[0]), split(held[2]), split(held[3])
-    cos, sin = twice(rotated[0][...]), twice(rotated[1][...])
-    for s in range(2):
-        first, third = x0[s], x2[s]
-        second, fourth = turned(x1, s), turned(x3, s)
-        outer, inner = first + fourth, second + third
-        v, w = first - fourth, second - third
-        total[s, 0] += dot3(plain, split(outer + inner))
-        total[s, 2] += dot3(even, split(outer - inner))
-        p = dot3(even, split(v * cos - w * sin))
-        q = dot3(odd, split(v * sin + w * cos))
-        total[s, 1] += p + q
-        total[s, 3] += p - q
+    cos, sin = twice(rotated[0]), twice(rotated[1])
+    first, third = x0[0], x2[0]
+    second, fourth = turned(x1, 0), turned(x3, 0)
+    outer, inner = first + fourth, second + third
+    v, w = first - fourth, second - third
+    total[0] += dot3(plain, split(outer + inner))
+    total[2] += dot3(even, split(outer - inner))
+    p = dot3(even, split(v * cos - w * sin))
+    q = dot3(odd, split(v * sin + w * cos))
+    total[1] += p + q
+    total[3] += p - q
 
     @pl.when(step == pl.num_programs(0) - 1)
     def _():
         core = lax.axis_index("c")
         for ref, owner in ((keep, core), (send, 1 - core)):
-            for s in range(2):
-                for k in range(4):
-                    ref[s, k] = total[s, k, pl.ds(pl.multiple_of(owner * HALF, HALF), HALF), :]
-
-
-def dct(snapshots):
-    tables = twiddles()
+            for k in range(4):
+                ref[k] = total[k, pl.ds(pl.multiple_of(owner * HALF, HALF), HALF), :]
+
+
+def dct(snapshots, table, at):
     steps = PART // STEP
-    block = (2, STEP, COLS)
-    turn = pltpu.VMEM((STEP, 128), F32)
-    half = jax.ShapeDtypeStruct((2, 4, HALF, COLS), F32)
+    block = (1, STEP, COLS)
+    half = jax.ShapeDtypeStruct((4, HALF, COLS), F32)
 
     def whole(shape):
         return pl.BlockSpec(shape, lambda i: (0,) * len(shape))
@@ -146,24 +144,23 @@
         dct_kernel,
         grid=(steps,),
         in_specs=[
-            pl.BlockSpec(block, lambda i: (0, i, 0)),
-            pl.BlockSpec(block, lambda i: (0, 2 * steps - 1 - i, 0)),
-            pl.BlockSpec(block, lambda i: (0, 2 * steps + i, 0)),
-            pl.BlockSpec(block, lambda i: (0, 4 * steps - 1 - i, 0)),
-        ]
-        + [whole(table.shape) for table in tables],
+            pl.BlockSpec(block, lambda i: (at, i, 0)),
+            pl.BlockSpec(block, lambda i: (at, 2 * steps - 1 - i, 0)),
+            pl.BlockSpec(block, lambda i: (at, 2 * steps + i, 0)),
+            pl.BlockSpec(block, lambda i: (at, 4 * steps - 1 - i, 0)),
+            whole(table.shape),
+        ],
         out_specs=[whole(half.shape)] * 2,
         out_shape=[half] * 2,
         scratch_shapes=[
             pltpu.VMEM((4, BAND, STEP), F32),
-            turn,
-            turn,
-            pltpu.VMEM((2, 4, BAND, COLS), F32),
+            pltpu.VMEM((2, STEP, 128), F32),
+            pltpu.VMEM((4, BAND, COLS), F32),
         ],
-        cost_estimate=pl.CostEstimate(flops=7_000_000_000, bytes_accessed=13_000_000, transcendentals=0),
-        compiler_params=room(46),
+        compiler_params=room(58),
+        cost_estimate=pl.CostEstimate(flops=3_500_000_000, bytes_accessed=6_000_000, transcendentals=0),
         name="dct",
-    )(*([snapshots] * 4), *tables)
+    )(*([snapshots] * 4), table)
 
 
 def place_of_own():
@@ -175,33 +172,34 @@
     return [snap[pl.ds(chip + 2 * owner + s, 1), :] for owner in (core, 1 - core) for s in range(2)]
 
 
-def prepare_kernel(own, other, snap, high_t, low_t, weights, *blocks):
+def prepare_kernel(*refs):
+    sources, snap, high_t, low_t, weights, blocks = refs[:4], *refs[4:8], refs[8:]
     z, x, core, _ = place_of_own()
     lines = [own_weights(snap, z, lax.rem(x - shift + NX, NX), core) for shift in range(NX)]
     weights[...] = jnp.concatenate(sum(lines, []), axis=0)
     for s in range(4):
-        source = own if s < 2 else other
+        source = sources[s]
         for k in range(4):
             place = slice(HALF * k, HALF * (k + 1))
-            high_t[s, :, place], low_t[s, :, place] = split(source[s % 2, k].T)
+            high_t[s, :, place], low_t[s, :, place] = split(source[k].T)
             for shift, block in enumerate(blocks):
                 start = pl.multiple_of(lax.rem(x + shift, NX) * 32, 32)
-                block[s, k] = source[s % 2, k, pl.ds(start, 32), :]
-
-
-def prepare(own, other, snap):
+                block[s, k] = source[k, pl.ds(start, 32), :]
+
+
+def prepare(sources, snap):
     crossed = jax.ShapeDtypeStruct((4, COLS, KEEP // 2), BF16)
     block = jax.ShapeDtypeStruct((4, 4, 32, COLS), F32)
     outs = [crossed, crossed, jax.ShapeDtypeStruct((16, RANK), F32)] + [block] * NX
     return pl.pallas_call(
         prepare_kernel,
-        in_specs=[VMEM] * 3,
+        in_specs=[VMEM] * 5,
         out_specs=[VMEM] * len(outs),
         out_shape=outs,
         compiler_params=room(12),
         cost_estimate=pl.CostEstimate(flops=10_000_000, bytes_accessed=6_000_000, transcendentals=0),
         name="prepare",
-    )(own, other, snap)
+    )(*sources, snap)
 
 
 def place_rows(x, pieces, rows):
@@ -366,15 +364,20 @@
     primal = new[...]
     gram[...] = exact(primal.T, primal)
     gram_half[...] = gram[pl.ds(pl.multiple_of(core * 128, 128), 128), :]
-    lines, weights = split(primal), inv[RANK + 8 : FACTOR]
+    lines = split(primal)
     for copy in copies:
         copy.wait()
-    sums = 0.0
-    for shift in range(NX):
+    gram[:128] = jnp.zeros((128, RANK), F32)
+
+    def add(shift, carry):
         product = dot3(split(held[shift].reshape(512, COLS)), lines)
         for s in range(4):
-            at = 4 * shift + s
-            sums += product[128 * s : 128 * s + 128] * weights[at : at + 1]
+            weight = inv[pl.ds(RANK + 8 + 4 * shift + s, 1), :]
+            gram[:128] += product[128 * s : 128 * s + 128] * weight
+        return carry
+
+    lax.fori_loop(0, NX, add, 0)
+    sums = gram[:128]
     for k in range(4):
         for half in range(2):
             line = sums[32 * k : 32 * k + 32, 128 * half : 128 * half + 128]
@@ -524,10 +527,13 @@
 
 def update(snapshots, snap_factor, row_factor, col_factor, row_dual, col_dual):
     mine = copied_along([row_factor], "z", NZ)
-    own, send = dct(snapshots)
-    mine, own, send = lax.optimization_barrier((mine, own, send))
+    table = twiddles()
+    early, send_early = dct(snapshots, table, 0)
+    mine, early, send_early = lax.optimization_barrier((mine, early, send_early))
     lines = [mine, *around(mine, "x")]
-    high_t, low_t, weights, *blocks = prepare(own, shifted(send, "c", NC, 1), snap_factor)
+    late, send_late = dct(snapshots, table, 1)
+    others = [shifted(send, "c", NC, 1) for send in (send_early, send_late)]
+    high_t, low_t, weights, *blocks = prepare([early, late, *others], snap_factor)
     keep, send = totals(high_t, low_t, weights, lines)
     gram = row_gram(lines)
     other = shifted(gram, "c", NC, 1)
@@ -547,10 +553,11 @@
     args = snap_factor, weights, gram_mine, other
     inv = system(row_system_kernel, FACTOR, *args)
     block = lax.all_to_all(block, "z", 0, 0, tiled=True)
-    block, inv = lax.optimization_barrier((block, inv))
     mine = folded(block)
-    near = summed([mine, swapped(mine, "y", 1)], mine.shape)[0]
-    row_new, row_dual_new = row_update(inv, row_factor, row_dual, near, swapped(near, "y", 3))
+    near = swapped(mine, "y", 1)
+    near = summed([mine, near], mine.shape)[0]
+    far = swapped(near, "y", 3)
+    row_new, row_dual_new = row_update(inv, row_factor, row_dual, near, far)
     return row_new, col_new, row_dual_new, col_dual_new
 
 

time: 134 us -> 130 us (0.970)
  waiting for transfers between devices: 49.7 us -> 42.5 us
  Pallas kernels: 27.3 us -> 31.8 us
  local copies, waits for them, and re-layouts: 8.51 us -> 5.7 us
    ppermute x23 -> x24, waiting for transfers between devices: 35.4 us -> 28.3 us  [shifted(): lax.ppermute(array, axis, [(i, (i + by) % size) for i in range(size)])]
    pallas_call x1 -> x2, Pallas kernels: 7.33 us -> 13.2 us  [dct(): pl.pallas_call(dct_kernel, grid=(steps,), in_specs=[pl.BlockSpec(block, l...]
    ppermute x2, waiting for transfers between devices: 5.4 us -> 2.4 us  [swapped(): return lax.ppermute(array, axis, [(i, i ^ flip) for i in range(4)])]
    all_to_all x1, waiting for transfers between devices: 6 us -> 8.83 us  [update(): block = lax.all_to_all(block, 'z', 0, 0, tiled=True)]
    unnamed x24 -> x20, local copies, waits for them, and re-layouts: 8.51 us -> 5.7 us
    ppermute x23 -> x24, starting transfers between devices: 22 us -> 23.9 us  [shifted(): lax.ppermute(array, axis, [(i, (i + by) % size) for i in range(size)])]
  transfers between devices with their start and end apart: 28 -> 29, of which waited for: 14 -> 10; matrix products, arithmetic and copies ran while one was open for 0% -> 0% of each run, Pallas kernels for 15% -> 19%
where the time goes in v5:
time: 130 us; the launch traced here: 127 us
  starting transfers between devices  46.6 us (36%)
  waiting for transfers between devices  42.5 us (33%)
  Pallas kernels  31.8 us (24%)
  local copies, waits for them, and re-layouts  5.7 us (4%)
    ppermute x24, waiting for transfers between devices, shifted(): lax.ppermute(array, axis, [(i, (i + by) % size) for i in range(size)])  28.3 us
    ppermute x24, starting transfers between devices, shifted(): lax.ppermute(array, axis, [(i, (i + by) % size) for i in range(size)])  23.9 us
    all_to_all x2, starting transfers between devices, copied_along(): return lax.all_to_all(whole, axes, 0, 0, tiled=True)  15.7 us
    pallas_call x2, Pallas kernels, dct(): pl.pallas_call(dct_kernel, grid=(steps,), in_specs=[pl.BlockSpec(block, l...  13.2 us
    all_to_all x1, waiting for transfers between devices, update(): block = lax.all_to_all(block, 'z', 0, 0, tiled=True)  8.83 us
    pallas_call x2, Pallas kernels, system(): pl.pallas_call(kernel, in_specs=[VMEM] * len(args), out_specs=VMEM, out_s...  8.39 us
    unnamed x20, local copies, waits for them, and re-layouts  5.7 us
    all_to_all x1, starting transfers between devices, update(): block = lax.all_to_all(block, 'z', 0, 0, tiled=True)  5.52 us
  transfers between devices with their start and end apart: 29, of which 10 were waited for; matrix products, arithmetic and copies ran while one was open for 0% of the time, Pallas kernels for 19%

profile of v5, /device:TPU:8, one launch (start us, length us, event | category | flops | bytes accessed | tf_op | source)
XLA Modules:
  0.0 127.5 jit_solution(7397487311628474024)
XLA Ops:
  2.0 8.5 %all-to-all-start = ((f32[8,16,256]{2,1,0:T(8,128)}), f32[8,16,256]{2,1,0:T(8,128)S(1)}, u32[]{:S(2)}, u32[]{:S(2)}) async-start(f32[8,16,256]{2,1,0:T(8,128)} %spread.2), calls=%async_computation | async-start | bytes 262144 | tf_op jit(solution)/shard_map/all_to_all | solution.py:501
  10.5 6.6 %dct.3 = (f32[4,128,256]{2,1,0:T(8,128)}, f32[4,128,256]{2,1,0:T(8,128)}) custom-call(f32[2,4096,256]{2,1,0:T(8,128)} %x3.3, f32[2,4096,256]{2,1,0:T(8,128)} %x3.3, f32[2,4096,256]{2,1,0:T(8,128)} %x3.3, f32[2,4096,256]{2,1,0:T(8,128)} %x3.3, f32[4,280,256]{2,1,0:T(8,128)} %constant.2.clone.table), custom_call_target="tpu_custom_call" | custom-call | flops 3500000000 | bytes 6000000 | tf_op jit(solution)/shard_map/dct/pallas_call | solution.py:143
  17.2 6.6 %dct.2 = (f32[4,128,256]{2,1,0:T(8,128)}, f32[4,128,256]{2,1,0:T(8,128)}) custom-call(f32[2,4096,256]{2,1,0:T(8,128)} %x3.3, f32[2,4096,256]{2,1,0:T(8,128)} %x3.3, f32[2,4096,256]{2,1,0:T(8,128)} %x3.3, f32[2,4096,256]{2,1,0:T(8,128)} %x3.3, f32[4,280,256]{2,1,0:T(8,128)} %constant.2.clone.table), custom_call_target="tpu_custom_call" | custom-call | flops 3500000000 | bytes 6000000 | tf_op jit(solution)/shard_map/dct/pallas_call | solution.py:143
  24.3 1.5 %collective-permute-start.5 = (f32[8,16,256]{2,1,0:T(8,128)S(1)}, f32[8,16,256]{2,1,0:T(8,128)S(1)}, u32[]{:S(2)}, u32[]{:S(2)}) collective-permute-start(f32[8,16,256]{2,1,0:T(8,128)S(1)} %all-to-all-done.refs_0_), channel_id=1, source_target_pairs={{0,8},{8,16},{16,24},{24,0},{1,9},{9,17},{17,25},{25,1},{2,10},{10... | collective-permute-start | bytes 393224 | tf_op jit(solution)/shard_map/ppermute | solution.py:455
  25.7 2.7 %collective-permute-start.6 = (f32[8,16,256]{2,1,0:T(8,128)S(1)}, f32[8,16,256]{2,1,0:T(8,128)S(1)}, u32[]{:S(2)}, u32[]{:S(2)}) collective-permute-start(f32[8,16,256]{2,1,0:T(8,128)S(1)} %all-to-all-done.refs_0_), channel_id=1, source_target_pairs={{0,16},{8,24},{16,0},{24,8},{1,17},{9,25},{17,1},{25,9},{2,18},{10... | collective-permute-start | bytes 393224 | tf_op jit(solution)/shard_map/ppermute | solution.py:455
  28.5 1.4 %collective-permute-start.7 = (f32[8,16,256]{2,1,0:T(8,128)S(1)}, f32[8,16,256]{2,1,0:T(8,128)S(1)}, u32[]{:S(2)}, u32[]{:S(2)}) collective-permute-start(f32[8,16,256]{2,1,0:T(8,128)S(1)} %all-to-all-done.refs_0_), channel_id=1, source_target_pairs={{0,24},{8,0},{16,8},{24,16},{1,25},{9,1},{17,9},{25,17},{2,26},{10... | collective-permute-start | bytes 393224 | tf_op jit(solution)/shard_map/ppermute | solution.py:455
  31.7 3.0 %collective-permute-done.6.refs_2_ = f32[8,16,256]{2,1,0:T(8,128)S(1)} collective-permute-done((f32[8,16,256]{2,1,0:T(8,128)S(1)}, f32[8,16,256]{2,1,0:T(8,128)S(1)}, u32[]{:S(2)}, u32[]{:S(2)}) %collective-permute-start.6) | collective-permute-done | bytes 131104 | tf_op jit(solution)/shard_map/ppermute | solution.py:455
  34.8 1.8 %totals.1 = (f32[4,32,256]{2,1,0:T(8,128)S(1)}, f32[4,32,256]{2,1,0:T(8,128)S(1)}) custom-call(bf16[4,256,512]{2,1,0:T(8,128)(2,1)S(1)} %get-tuple-element.43.high_t, bf16[4,256,512]{2,1,0:T(8,128)(2,1)S(1)} %get-tuple-element.44.low_t, f32[16,256]{1,0:T(8,128)S(1)} %get-tuple-element.38.weights, f32[8,16,256]{2,1,0:T(8,128)S(1)} %all-to-all-done.refs_0_, ...), custom_call_target="tpu_custom_call" | custom-call | flops 800000000 | bytes 4000000 | tf_op jit(solution)/shard_map/totals/pallas_call | solution.py:235
  38.1 2.7 %collective-permute-start.10 = (f32[32,256]{1,0:T(8,128)S(1)}, f32[32,256]{1,0:T(8,128)S(1)}, u32[]{:S(2)}, u32[]{:S(2)}) collective-permute-start(f32[32,256]{1,0:T(8,128)S(1)} %get-tuple-element.50), channel_id=1, source_target_pairs={{0,16},{8,24},{16,0},{24,8},{1,17},{9,25},{17,1},{25,9},{2,18},{10... | collective-permute-start | bytes 98312 | tf_op jit(solution)/shard_map/ppermute | solution.py:455
  41.3 2.8 %collective-permute-start.11 = (f32[32,256]{1,0:T(8,128)S(1)}, f32[32,256]{1,0:T(8,128)S(1)}, u32[]{:S(2)}, u32[]{:S(2)}) collective-permute-start(f32[32,256]{1,0:T(8,128)S(1)} %get-tuple-element.51), channel_id=1, source_target_pairs={{0,24},{8,0},{16,8},{24,16},{1,25},{9,1},{17,9},{25,17},{2,26},{10... | collective-permute-start | bytes 98312 | tf_op jit(solution)/shard_map/ppermute | solution.py:455
  44.1 2.5 %collective-permute-start.3 = (f32[4,4,32,256]{3,2,1,0:T(8,128)S(1)}, f32[4,4,32,256]{3,2,1,0:T(8,128)}, u32[]{:S(2)}, u32[]{:S(2)}) collective-permute-start(f32[4,4,32,256]{3,2,1,0:T(8,128)S(1)} %get-tuple-element.41), channel_id=1, source_target_pairs={{0,16},{8,24},{16,0},{24,8},{1,17},{9,25},{17,1},{25,9},{2,18},{10... | collective-permute-start | bytes 1572872 | tf_op jit(solution)/shard_map/ppermute | solution.py:455
  46.6 21.0 %collective-permute-done.9.refs_1_ = f32[32,256]{1,0:T(8,128)S(1)} collective-permute-done((f32[32,256]{1,0:T(8,128)S(1)}, f32[32,256]{1,0:T(8,128)S(1)}, u32[]{:S(2)}, u32[]{:S(2)}) %collective-permute-start.9) | collective-permute-done | bytes 32800 | tf_op jit(solution)/shard_map/ppermute | solution.py:455
  68.4 7.2 %all-to-all-start.1 = ((f32[8,32,256]{2,1,0:T(8,128)}), f32[8,32,256]{2,1,0:T(8,128)S(1)}, u32[]{:S(2)}, u32[]{:S(2)}) async-start(f32[8,32,256]{2,1,0:T(8,128)} %spread.3), calls=%async_computation.1 | async-start | bytes 524288 | tf_op jit(solution)/shard_map/all_to_all | solution.py:501
  77.5 4.7 %shard_map.102.refs_4_ = f32[792,256]{1,0:T(8,128)S(1)} custom-call(f32[128,256]{1,0:T(8,128)S(1)} %copy-done.2, f32[16,256]{1,0:T(8,128)S(1)} %get-tuple-element.38.weights, f32[256,256]{1,0:T(8,128)S(1)} %row_gram.1.mine, f32[256,256]{1,0:T(8,128)} %collective-permute-done.12.other, f32[256,256]{1,0:T(8,128)S(1)} %copy-done.6, f32[256,256]{1,0:T(8,128)S(1)} %copy-done.7), custom_call_target="tpu_custom_call" | custom-call | flops 3000000000 | bytes 1000000 | tf_op jit(solution)/shard_map/pallas_call | solution.py:319
  83.1 3.0 %all-to-all-done.1.block = f32[8,32,256]{2,1,0:T(8,128)S(1)} async-done(((f32[8,32,256]{2,1,0:T(8,128)}), f32[8,32,256]{2,1,0:T(8,128)S(1)}, u32[]{:S(2)}, u32[]{:S(2)}) %all-to-all-start.1) | async-done | bytes 262176 | tf_op jit(solution)/shard_map/all_to_all | solution.py:501
  87.2 2.2 %collective-permute-start.15 = (f32[32,256]{1,0:T(8,128)S(1)}, f32[32,256]{1,0:T(8,128)S(1)}, u32[]{:S(2)}, u32[]{:S(2)}) collective-permute-start(f32[32,256]{1,0:T(8,128)S(1)} %folded.2.refs_5_), channel_id=1, source_target_pairs={{0,24},{8,0},{16,8},{24,16},{1,25},{9,1},{17,9},{25,17},{2,26},{10... | collective-permute-start | bytes 98312 | tf_op jit(solution)/shard_map/ppermute | solution.py:455
  89.4 1.9 %collective-permute-done.13.refs_6_ = f32[32,256]{1,0:T(8,128)S(1)} collective-permute-done((f32[32,256]{1,0:T(8,128)S(1)}, f32[32,256]{1,0:T(8,128)S(1)}, u32[]{:S(2)}, u32[]{:S(2)}) %collective-permute-start.13) | collective-permute-done | bytes 32800 | tf_op jit(solution)/shard_map/ppermute | solution.py:455
  94.9 4.1 %col_update.1 = (f32[256,256]{1,0:T(8,128)}, f32[256,256]{1,0:T(8,128)}, f32[128,256]{1,0:T(8,128)S(1)}, f32[8,16,256]{2,1,0:T(8,128)}) custom-call(f32[4,4,32,256]{3,2,1,0:T(8,128)S(1)} %get-tuple-element.39.refs_0_, f32[4,4,32,256]{3,2,1,0:T(8,128)S(1)} %collective-permute-done.2.refs_1_, f32[4,4,32,256]{3,2,1,0:T(8,128)} %collective-permute-done.3.refs_2_, ...), custom_call_target="tpu_custom_call" | custom-call | flops 1500000000 | bytes 5000000 | tf_op jit(solution)/shard_map/col_update/pallas_call | solution.py:395
  98.9 1.7 %collective-permute-start.20 = (f32[128,256]{1,0:T(8,128)S(1)}, f32[128,256]{1,0:T(8,128)S(1)}, u32[]{:S(2)}, u32[]{:S(2)}) collective-permute-start(f32[128,256]{1,0:T(8,128)S(1)} %get-tuple-element.54.refs_0_), channel_id=1, source_target_pairs={{0,1},{1,2},{2,3},{3,0},{4,5},{5,6},{6,7},{7,4},{8,9},{9,10},{10,1... | collective-permute-start | bytes 393224 | tf_op jit(solution)/shard_map/ppermute | solution.py:455
  101.5 2.4 %collective-permute-start.22 = (f32[128,256]{1,0:T(8,128)S(1)}, f32[128,256]{1,0:T(8,128)S(1)}, u32[]{:S(2)}, u32[]{:S(2)}) collective-permute-start(f32[128,256]{1,0:T(8,128)S(1)} %get-tuple-element.54.refs_0_), channel_id=1, source_target_pairs={{0,3},{1,0},{2,1},{3,2},{4,7},{5,4},{6,5},{7,6},{8,11},{9,8},{10,9... | collective-permute-start | bytes 393224 | tf_op jit(solution)/shard_map/ppermute | solution.py:455
  103.9 5.5 %all-to-all-start.2 = ((f32[8,16,256]{2,1,0:T(8,128)}), f32[8,16,256]{2,1,0:T(8,128)S(1)}, u32[]{:S(2)}, u32[]{:S(2)}) async-start(f32[8,16,256]{2,1,0:T(8,128)} %get-tuple-element.55), calls=%async_computation.2 | async-start | bytes 262144 | tf_op jit(solution)/shard_map/all_to_all | solution.py:555
  109.7 8.8 %all-to-all-done.2.block = f32[8,16,256]{2,1,0:T(8,128)S(1)} async-done(((f32[8,16,256]{2,1,0:T(8,128)}), f32[8,16,256]{2,1,0:T(8,128)S(1)}, u32[]{:S(2)}, u32[]{:S(2)}) %all-to-all-start.2) | async-done | bytes 131104 | tf_op jit(solution)/shard_map/all_to_all | solution.py:555
  120.0 2.4 %collective-permute-done.24.refs_1_ = f32[16,256]{1,0:T(8,128)S(1)} collective-permute-done((f32[16,256]{1,0:T(8,128)S(1)}, f32[16,256]{1,0:T(8,128)S(1)}, u32[]{:S(2)}, u32[]{:S(2)}) %collective-permute-start.24) | collective-permute-done | bytes 16416 | tf_op jit(solution)/shard_map/ppermute | solution.py:459
  122.4 3.7 %shard_map.103.inv = f32[280,256]{1,0:T(8,128)S(1)} custom-call(f32[128,256]{1,0:T(8,128)S(1)} %copy-done.2, f32[16,256]{1,0:T(8,128)S(1)} %get-tuple-element.38.weights, f32[128,256]{1,0:T(8,128)S(1)} %gram_sum.1.mine, f32[128,256]{1,0:T(8,128)S(1)} %collective-permute-done.23.other), custom_call_target="tpu_custom_call" | custom-call | flops 3000000000 | bytes 1000000 | tf_op jit(solution)/shard_map/pallas_call | solution.py:319
  (70 shorter events, 17.8 us)
Async XLA Ops:
  2.0 21.8 %all-to-all-start = ((f32[8,16,256]{2,1,0:T(8,128)}), f32[8,16,256]{2,1,0:T(8,128)S(1)}, u32[]{:S(2)}, u32[]{:S(2)}) async-start(f32[8,16,256]{2,1,0:T(8,128)} %spread.2), calls=%async_computation | async-start | bytes 262144 | tf_op jit(solution)/shard_map/all_to_all | solution.py:501
  17.1 12.9 %collective-permute-start.1 = (f32[4,128,256]{2,1,0:T(8,128)}, f32[4,128,256]{2,1,0:T(8,128)S(1)}, u32[]{:S(2)}, u32[]{:S(2)}) collective-permute-start(f32[4,128,256]{2,1,0:T(8,128)} %get-tuple-element.37), channel_id=1, source_target_pairs={{0,4},{4,0},{1,5},{5,1},{2,6},{6,2},{3,7},{7,3},{8,12},{12,8},{9,1... | collective-permute-start | bytes 1572872 | tf_op jit(solution)/shard_map/ppermute | solution.py:455
  23.8 6.1 %collective-permute-start = (f32[4,128,256]{2,1,0:T(8,128)}, f32[4,128,256]{2,1,0:T(8,128)S(1)}, u32[]{:S(2)}, u32[]{:S(2)}) collective-permute-start(f32[4,128,256]{2,1,0:T(8,128)} %get-tuple-element.36), channel_id=1, source_target_pairs={{0,4},{4,0},{1,5},{5,1},{2,6},{6,2},{3,7},{7,3},{8,12},{12,8},{9,1... | collective-permute-start | bytes 1572872 | tf_op jit(solution)/shard_map/ppermute | solution.py:455
  24.3 7.5 %collective-permute-start.5 = (f32[8,16,256]{2,1,0:T(8,128)S(1)}, f32[8,16,256]{2,1,0:T(8,128)S(1)}, u32[]{:S(2)}, u32[]{:S(2)}) collective-permute-start(f32[8,16,256]{2,1,0:T(8,128)S(1)} %all-to-all-done.refs_0_), channel_id=1, source_target_pairs={{0,8},{8,16},{16,24},{24,0},{1,9},{9,17},{17,25},{25,1},{2,10},{10... | collective-permute-start | bytes 393224 | tf_op jit(solution)/shard_map/ppermute | solution.py:455
  25.7 9.0 %collective-permute-start.6 = (f32[8,16,256]{2,1,0:T(8,128)S(1)}, f32[8,16,256]{2,1,0:T(8,128)S(1)}, u32[]{:S(2)}, u32[]{:S(2)}) collective-permute-start(f32[8,16,256]{2,1,0:T(8,128)S(1)} %all-to-all-done.refs_0_), channel_id=1, source_target_pairs={{0,16},{8,24},{16,0},{24,8},{1,17},{9,25},{17,1},{25,9},{2,18},{10... | collective-permute-start | bytes 393224 | tf_op jit(solution)/shard_map/ppermute | solution.py:455
  28.5 6.3 %collective-permute-start.7 = (f32[8,16,256]{2,1,0:T(8,128)S(1)}, f32[8,16,256]{2,1,0:T(8,128)S(1)}, u32[]{:S(2)}, u32[]{:S(2)}) collective-permute-start(f32[8,16,256]{2,1,0:T(8,128)S(1)} %all-to-all-done.refs_0_), channel_id=1, source_target_pairs={{0,24},{8,0},{16,8},{24,16},{1,25},{9,1},{17,9},{25,17},{2,26},{10... | collective-permute-start | bytes 393224 | tf_op jit(solution)/shard_map/ppermute | solution.py:455
  37.5 38.1 %collective-permute-start.12 = (f32[256,256]{1,0:T(8,128)S(1)}, f32[256,256]{1,0:T(8,128)}, u32[]{:S(2)}, u32[]{:S(2)}) collective-permute-start(f32[256,256]{1,0:T(8,128)S(1)} %row_gram.1.mine), channel_id=1, source_target_pairs={{0,4},{4,0},{1,5},{5,1},{2,6},{6,2},{3,7},{7,3},{8,12},{12,8},{9,1... | collective-permute-start | bytes 786440 | tf_op jit(solution)/shard_map/ppermute | solution.py:455
  38.1 6.0 %collective-permute-start.10 = (f32[32,256]{1,0:T(8,128)S(1)}, f32[32,256]{1,0:T(8,128)S(1)}, u32[]{:S(2)}, u32[]{:S(2)}) collective-permute-start(f32[32,256]{1,0:T(8,128)S(1)} %get-tuple-element.50), channel_id=1, source_target_pairs={{0,16},{8,24},{16,0},{24,8},{1,17},{9,25},{17,1},{25,9},{2,18},{10... | collective-permute-start | bytes 98312 | tf_op jit(solution)/shard_map/ppermute | solution.py:455
  40.8 46.4 %collective-permute-start.2 = (f32[4,4,32,256]{3,2,1,0:T(8,128)S(1)}, f32[4,4,32,256]{3,2,1,0:T(8,128)S(1)}, u32[]{:S(2)}, u32[]{:S(2)}) collective-permute-start(f32[4,4,32,256]{3,2,1,0:T(8,128)S(1)} %get-tuple-element.40), channel_id=1, source_target_pairs={{0,8},{8,16},{16,24},{24,0},{1,9},{9,17},{17,25},{25,1},{2,10},{10... | collective-permute-start | bytes 1572872 | tf_op jit(solution)/shard_map/ppermute | solution.py:455
  41.3 5.3 %collective-permute-start.11 = (f32[32,256]{1,0:T(8,128)S(1)}, f32[32,256]{1,0:T(8,128)S(1)}, u32[]{:S(2)}, u32[]{:S(2)}) collective-permute-start(f32[32,256]{1,0:T(8,128)S(1)} %get-tuple-element.51), channel_id=1, source_target_pairs={{0,24},{8,0},{16,8},{24,16},{1,25},{9,1},{17,9},{25,17},{2,26},{10... | collective-permute-start | bytes 98312 | tf_op jit(solution)/shard_map/ppermute | solution.py:455
  44.1 23.6 %collective-permute-start.9 = (f32[32,256]{1,0:T(8,128)S(1)}, f32[32,256]{1,0:T(8,128)S(1)}, u32[]{:S(2)}, u32[]{:S(2)}) collective-permute-start(f32[32,256]{1,0:T(8,128)S(1)} %get-tuple-element.49), channel_id=1, source_target_pairs={{0,8},{8,16},{16,24},{24,0},{1,9},{9,17},{17,25},{25,1},{2,10},{10... | collective-permute-start | bytes 98312 | tf_op jit(solution)/shard_map/ppermute | solution.py:455
  44.1 45.3 %collective-permute-start.3 = (f32[4,4,32,256]{3,2,1,0:T(8,128)S(1)}, f32[4,4,32,256]{3,2,1,0:T(8,128)}, u32[]{:S(2)}, u32[]{:S(2)}) collective-permute-start(f32[4,4,32,256]{3,2,1,0:T(8,128)S(1)} %get-tuple-element.41), channel_id=1, source_target_pairs={{0,16},{8,24},{16,0},{24,8},{1,17},{9,25},{17,1},{25,9},{2,18},{10... | collective-permute-start | bytes 1572872 | tf_op jit(solution)/shard_map/ppermute | solution.py:455
  68.4 17.7 %all-to-all-start.1 = ((f32[8,32,256]{2,1,0:T(8,128)}), f32[8,32,256]{2,1,0:T(8,128)S(1)}, u32[]{:S(2)}, u32[]{:S(2)}) async-start(f32[8,32,256]{2,1,0:T(8,128)} %spread.3), calls=%async_computation.1 | async-start | bytes 524288 | tf_op jit(solution)/shard_map/all_to_all | solution.py:501
  75.6 16.9 %collective-permute-start.4 = (f32[4,4,32,256]{3,2,1,0:T(8,128)S(1)}, f32[4,4,32,256]{3,2,1,0:T(8,128)}, u32[]{:S(2)}, u32[]{:S(2)}) collective-permute-start(f32[4,4,32,256]{3,2,1,0:T(8,128)S(1)} %get-tuple-element.42), channel_id=1, source_target_pairs={{0,24},{8,0},{16,8},{24,16},{1,25},{9,1},{17,9},{25,17},{2,26},{10... | collective-permute-start | bytes 1572872 | tf_op jit(solution)/shard_map/ppermute | solution.py:455
  86.1 5.2 %collective-permute-start.13 = (f32[32,256]{1,0:T(8,128)S(1)}, f32[32,256]{1,0:T(8,128)S(1)}, u32[]{:S(2)}, u32[]{:S(2)}) collective-permute-start(f32[32,256]{1,0:T(8,128)S(1)} %folded.2.refs_5_), channel_id=1, source_target_pairs={{0,8},{8,16},{16,24},{24,0},{1,9},{9,17},{17,25},{25,1},{2,10},{10... | collective-permute-start | bytes 98312 | tf_op jit(solution)/shard_map/ppermute | solution.py:455
  86.2 5.5 %collective-permute-start.14 = (f32[32,256]{1,0:T(8,128)S(1)}, f32[32,256]{1,0:T(8,128)S(1)}, u32[]{:S(2)}, u32[]{:S(2)}) collective-permute-start(f32[32,256]{1,0:T(8,128)S(1)} %folded.2.refs_5_), channel_id=1, source_target_pairs={{0,16},{8,24},{16,0},{24,8},{1,17},{9,25},{17,1},{25,9},{2,18},{10... | collective-permute-start | bytes 98312 | tf_op jit(solution)/shard_map/ppermute | solution.py:455
  87.2 5.3 %collective-permute-start.15 = (f32[32,256]{1,0:T(8,128)S(1)}, f32[32,256]{1,0:T(8,128)S(1)}, u32[]{:S(2)}, u32[]{:S(2)}) collective-permute-start(f32[32,256]{1,0:T(8,128)S(1)} %folded.2.refs_5_), channel_id=1, source_target_pairs={{0,24},{8,0},{16,8},{24,16},{1,25},{9,1},{17,9},{25,17},{2,26},{10... | collective-permute-start | bytes 98312 | tf_op jit(solution)/shard_map/ppermute | solution.py:455
  98.9 10.5 %collective-permute-start.20 = (f32[128,256]{1,0:T(8,128)S(1)}, f32[128,256]{1,0:T(8,128)S(1)}, u32[]{:S(2)}, u32[]{:S(2)}) collective-permute-start(f32[128,256]{1,0:T(8,128)S(1)} %get-tuple-element.54.refs_0_), channel_id=1, source_target_pairs={{0,1},{1,2},{2,3},{3,0},{4,5},{5,6},{6,7},{7,4},{8,9},{9,10},{10,1... | collective-permute-start | bytes 393224 | tf_op jit(solution)/shard_map/ppermute | solution.py:455
  100.6 8.9 %collective-permute-start.21 = (f32[128,256]{1,0:T(8,128)S(1)}, f32[128,256]{1,0:T(8,128)S(1)}, u32[]{:S(2)}, u32[]{:S(2)}) collective-permute-start(f32[128,256]{1,0:T(8,128)S(1)} %get-tuple-element.54.refs_0_), channel_id=1, source_target_pairs={{0,2},{1,3},{2,0},{3,1},{4,6},{5,7},{6,4},{7,5},{8,10},{9,11},{10,... | collective-permute-start | bytes 393224 | tf_op jit(solution)/shard_map/ppermute | solution.py:455
  101.5 8.0 %collective-permute-start.22 = (f32[128,256]{1,0:T(8,128)S(1)}, f32[128,256]{1,0:T(8,128)S(1)}, u32[]{:S(2)}, u32[]{:S(2)}) collective-permute-start(f32[128,256]{1,0:T(8,128)S(1)} %get-tuple-element.54.refs_0_), channel_id=1, source_target_pairs={{0,3},{1,0},{2,1},{3,2},{4,7},{5,4},{6,5},{7,6},{8,11},{9,8},{10,9... | collective-permute-start | bytes 393224 | tf_op jit(solution)/shard_map/ppermute | solution.py:455
  103.9 14.6 %all-to-all-start.2 = ((f32[8,16,256]{2,1,0:T(8,128)}), f32[8,16,256]{2,1,0:T(8,128)S(1)}, u32[]{:S(2)}, u32[]{:S(2)}) async-start(f32[8,16,256]{2,1,0:T(8,128)} %get-tuple-element.55), calls=%async_computation.2 | async-start | bytes 262144 | tf_op jit(solution)/shard_map/all_to_all | solution.py:555
  109.6 12.8 %collective-permute-start.23 = (f32[128,256]{1,0:T(8,128)S(1)}, f32[128,256]{1,0:T(8,128)S(1)}, u32[]{:S(2)}, u32[]{:S(2)}) collective-permute-start(f32[128,256]{1,0:T(8,128)S(1)} %gram_sum.1.mine), channel_id=1, source_target_pairs={{0,4},{4,0},{1,5},{5,1},{2,6},{6,2},{3,7},{7,3},{8,12},{12,8},{9,1... | collective-permute-start | bytes 393224 | tf_op jit(solution)/shard_map/ppermute | solution.py:455
  118.5 3.8 %collective-permute-start.24 = (f32[16,256]{1,0:T(8,128)S(1)}, f32[16,256]{1,0:T(8,128)S(1)}, u32[]{:S(2)}, u32[]{:S(2)}) collective-permute-start(f32[16,256]{1,0:T(8,128)S(1)} %folded.3.refs_0_), channel_id=1, source_target_pairs={{0,1},{1,0},{2,3},{3,2},{4,5},{5,4},{6,7},{7,6},{8,9},{9,8},{10,11... | collective-permute-start | bytes 49160 | tf_op jit(solution)/shard_map/ppermute | solution.py:459
  122.4 3.7 %collective-permute-start.25 = (f32[16,256]{1,0:T(8,128)S(1)}, f32[16,256]{1,0:T(8,128)S(1)}, u32[]{:S(2)}, u32[]{:S(2)}) collective-permute-start(f32[16,256]{1,0:T(8,128)S(1)} %summed.3.mine), channel_id=1, source_target_pairs={{0,3},{1,2},{2,1},{3,0},{4,7},{5,6},{6,5},{7,4},{8,11},{9,10},{10,... | collective-permute-start | bytes 49160 | tf_op jit(solution)/shard_map/ppermute | solution.py:459
  (15 other events, 102.2 us)

commit v6 on v5

--- a/solution.py
+++ b/solution.py
@@ -113,29 +113,31 @@
 
     plain, even, odd = split(held[0]), split(held[2]), split(held[3])
     cos, sin = twice(rotated[0]), twice(rotated[1])
-    first, third = x0[0], x2[0]
-    second, fourth = turned(x1, 0), turned(x3, 0)
-    outer, inner = first + fourth, second + third
-    v, w = first - fourth, second - third
-    total[0] += dot3(plain, split(outer + inner))
-    total[2] += dot3(even, split(outer - inner))
-    p = dot3(even, split(v * cos - w * sin))
-    q = dot3(odd, split(v * sin + w * cos))
-    total[1] += p + q
-    total[3] += p - q
+    for s in range(2):
+        first, third = x0[s], x2[s]
+        second, fourth = turned(x1, s), turned(x3, s)
+        outer, inner = first + fourth, second + third
+        v, w = first - fourth, second - third
+        total[s, 0] += dot3(plain, split(outer + inner))
+        total[s, 2] += dot3(even, split(outer - inner))
+        p = dot3(even, split(v * cos - w * sin))
+        q = dot3(odd, split(v * sin + w * cos))
+        total[s, 1] += p + q
+        total[s, 3] += p - q
 
     @pl.when(step == pl.num_programs(0) - 1)
     def _():
         core = lax.axis_index("c")
         for ref, owner in ((keep, core), (send, 1 - core)):
-            for k in range(4):
-                ref[k] = total[k, pl.ds(pl.multiple_of(owner * HALF, HALF), HALF), :]
-
-
-def dct(snapshots, table, at):
+            for s in range(2):
+                for k in range(4):
+                    ref[s, k] = total[s, k, pl.ds(pl.multiple_of(owner * HALF, HALF), HALF), :]
+
+
+def dct(snapshots, table):
     steps = PART // STEP
-    block = (1, STEP, COLS)
-    half = jax.ShapeDtypeStruct((4, HALF, COLS), F32)
+    block = (2, STEP, COLS)
+    half = jax.ShapeDtypeStruct((2, 4, HALF, COLS), F32)
 
     def whole(shape):
         return pl.BlockSpec(shape, lambda i: (0,) * len(shape))
@@ -144,10 +146,10 @@
         dct_kernel,
         grid=(steps,),
         in_specs=[
-            pl.BlockSpec(block, lambda i: (at, i, 0)),
-            pl.BlockSpec(block, lambda i: (at, 2 * steps - 1 - i, 0)),
-            pl.BlockSpec(block, lambda i: (at, 2 * steps + i, 0)),
-            pl.BlockSpec(block, lambda i: (at, 4 * steps - 1 - i, 0)),
+            pl.BlockSpec(block, lambda i: (0, i, 0)),
+            pl.BlockSpec(block, lambda i: (0, 2 * steps - 1 - i, 0)),
+            pl.BlockSpec(block, lambda i: (0, 2 * steps + i, 0)),
+            pl.BlockSpec(block, lambda i: (0, 4 * steps - 1 - i, 0)),
             whole(table.shape),
         ],
         out_specs=[whole(half.shape)] * 2,
@@ -155,10 +157,10 @@
         scratch_shapes=[
             pltpu.VMEM((4, BAND, STEP), F32),
             pltpu.VMEM((2, STEP, 128), F32),
-            pltpu.VMEM((4, BAND, COLS), F32),
+            pltpu.VMEM((2, 4, BAND, COLS), F32),
         ],
         compiler_params=room(58),
-        cost_estimate=pl.CostEstimate(flops=3_500_000_000, bytes_accessed=6_000_000, transcendentals=0),
+        cost_estimate=pl.CostEstimate(flops=7_000_000_000, bytes_accessed=12_000_000, transcendentals=0),
         name="dct",
     )(*([snapshots] * 4), table)
 
@@ -173,33 +175,34 @@
 
 
 def prepare_kernel(*refs):
-    sources, snap, high_t, low_t, weights, blocks = refs[:4], *refs[4:8], refs[8:]
+    own, other, snap, high_t, low_t, weights = refs[:6]
+    blocks = refs[6:]
     z, x, core, _ = place_of_own()
     lines = [own_weights(snap, z, lax.rem(x - shift + NX, NX), core) for shift in range(NX)]
     weights[...] = jnp.concatenate(sum(lines, []), axis=0)
     for s in range(4):
-        source = sources[s]
+        source = own if s < 2 else other
         for k in range(4):
             place = slice(HALF * k, HALF * (k + 1))
-            high_t[s, :, place], low_t[s, :, place] = split(source[k].T)
+            high_t[s, :, place], low_t[s, :, place] = split(source[s % 2, k].T)
             for shift, block in enumerate(blocks):
                 start = pl.multiple_of(lax.rem(x + shift, NX) * 32, 32)
-                block[s, k] = source[k, pl.ds(start, 32), :]
-
-
-def prepare(sources, snap):
+                block[s, k] = source[s % 2, k, pl.ds(start, 32), :]
+
+
+def prepare(own, other, snap):
     crossed = jax.ShapeDtypeStruct((4, COLS, KEEP // 2), BF16)
     block = jax.ShapeDtypeStruct((4, 4, 32, COLS), F32)
     outs = [crossed, crossed, jax.ShapeDtypeStruct((16, RANK), F32)] + [block] * NX
     return pl.pallas_call(
         prepare_kernel,
-        in_specs=[VMEM] * 5,
+        in_specs=[VMEM] * 3,
         out_specs=[VMEM] * len(outs),
         out_shape=outs,
         compiler_params=room(12),
         cost_estimate=pl.CostEstimate(flops=10_000_000, bytes_accessed=6_000_000, transcendentals=0),
         name="prepare",
-    )(*sources, snap)
+    )(own, other, snap)
 
 
 def place_rows(x, pieces, rows):
@@ -410,27 +413,6 @@
     )(*coefficients, inv, *pieces)
 
 
-def gram_sum_kernel(*refs):
-    parts, out, held = refs[:4], refs[4], refs[5]
-    y = lax.axis_index("y")
-    for shift in range(NY):
-        held[lax.rem(y - shift + NY, NY)] = parts[shift][...]
-    out[...] = (held[0] + held[1]) + (held[2] + held[3])
-
-
-def gram_sum(parts):
-    shape = parts[0].shape
-    return pl.pallas_call(
-        gram_sum_kernel,
-        in_specs=[VMEM] * NY,
-        out_specs=VMEM,
-        out_shape=jax.ShapeDtypeStruct(shape, F32),
-        scratch_shapes=[pltpu.VMEM((NY, *shape), F32)],
-        compiler_params=room(4),
-        name="gram_sum",
-    )(*parts)
-
-
 def row_kernel(inv, factor, dual, mine, other, new, dual_new, sums):
     sums[...] = mine[...] + other[...]
     new[...] = factor[...]
@@ -527,28 +509,28 @@
 
 def update(snapshots, snap_factor, row_factor, col_factor, row_dual, col_dual):
     mine = copied_along([row_factor], "z", NZ)
-    table = twiddles()
-    early, send_early = dct(snapshots, table, 0)
-    mine, early, send_early = lax.optimization_barrier((mine, early, send_early))
+    own, send = dct(snapshots, twiddles())
+    mine, own, send = lax.optimization_barrier((mine, own, send))
     lines = [mine, *around(mine, "x")]
-    late, send_late = dct(snapshots, table, 1)
-    others = [shifted(send, "c", NC, 1) for send in (send_early, send_late)]
-    high_t, low_t, weights, *blocks = prepare([early, late, *others], snap_factor)
+    high_t, low_t, weights, *blocks = prepare(own, shifted(send, "c", NC, 1), snap_factor)
     keep, send = totals(high_t, low_t, weights, lines)
     gram = row_gram(lines)
     other = shifted(gram, "c", NC, 1)
     args = snap_factor, weights, gram, other
     inv = system(col_system_kernel, DUAL + COLS, *args, col_factor, col_dual)
     parts = list(summed([keep, shifted(send, "c", NC, 1)], (32, RANK), NX))
-    chunk = copied_along([parts[0], *around(parts, "x")], "z", NZ)
+    parts = [parts[0], *around(parts, "x")]
+    chunk = copied_along(parts, "z", NZ)
     coefficients = [blocks[0], *around(list(blocks), "x")]
     chunk, inv = lax.optimization_barrier((chunk, inv))
     chunk = folded(chunk)
     pieces = [chunk, *around(chunk, "x")]
     pieces = pieces + [shifted(piece, "c", NC, 1) for piece in pieces]
     col_new, col_dual_new, gram_half, block = col_update(coefficients, inv, pieces)
-    grams = [gram_half, *around(gram_half, "y")]
-    gram_mine = gram_sum(grams)
+    other = swapped(gram_half, "y", 1)
+    gram_near = summed([gram_half, other], gram_half.shape)[0]
+    other = swapped(gram_near, "y", 3)
+    gram_mine = summed([gram_near, other], gram_half.shape)[0]
     other = shifted(gram_mine, "c", NC, 1)
     args = snap_factor, weights, gram_mine, other
     inv = system(row_system_kernel, FACTOR, *args)

time: 130 us -> 128 us (0.985)
  waiting for transfers between devices: 42.5 us -> 49.8 us
  starting transfers between devices: 46.6 us -> 42.1 us
  Pallas kernels: 31.8 us -> 28.5 us
    ppermute x24 -> x20, starting transfers between devices: 23.9 us -> 16.9 us  [shifted(): lax.ppermute(array, axis, [(i, (i + by) % size) for i in range(size)])]
    ppermute x2 -> x4, waiting for transfers between devices: 2.4 us -> 6.98 us  [swapped(): return lax.ppermute(array, axis, [(i, i ^ flip) for i in range(4)])]
    pallas_call x2 -> x1, Pallas kernels: 13.2 us -> 9.13 us  [dct(): pl.pallas_call(dct_kernel, grid=(steps,), in_specs=[pl.BlockSpec(block, l...]
    ppermute x2 -> x4, starting transfers between devices: 1.44 us -> 4.62 us  [swapped(): return lax.ppermute(array, axis, [(i, i ^ flip) for i in range(4)])]
    ppermute x24 -> x20, waiting for transfers between devices: 28.3 us -> 30.1 us  [shifted(): lax.ppermute(array, axis, [(i, (i + by) % size) for i in range(size)])]
    unnamed x20 -> x18, local copies, waits for them, and re-layouts: 5.7 us -> 4.94 us
  transfers between devices with their start and end apart: 29 -> 27, of which waited for: 10 -> 11; matrix products, arithmetic and copies ran while one was open for 0% -> 0% of each run, Pallas kernels for 19% -> 16%
where the time goes in v6:
time: 128 us; the launch traced here: 126 us
  waiting for transfers between devices  49.8 us (39%)
  starting transfers between devices  42.1 us (33%)
  Pallas kernels  28.5 us (22%)
  local copies, waits for them, and re-layouts  4.94 us (4%)
    ppermute x20, waiting for transfers between devices, shifted(): lax.ppermute(array, axis, [(i, (i + by) % size) for i in range(size)])  30.1 us
    ppermute x20, starting transfers between devices, shifted(): lax.ppermute(array, axis, [(i, (i + by) % size) for i in range(size)])  16.9 us
    all_to_all x2, starting transfers between devices, copied_along(): return lax.all_to_all(whole, axes, 0, 0, tiled=True)  15.7 us
    pallas_call x1, Pallas kernels, dct(): pl.pallas_call(dct_kernel, grid=(steps,), in_specs=[pl.BlockSpec(block, l...  9.13 us
    all_to_all x1, waiting for transfers between devices, update(): block = lax.all_to_all(block, 'z', 0, 0, tiled=True)  8.95 us
    pallas_call x2, Pallas kernels, system(): pl.pallas_call(kernel, in_specs=[VMEM] * len(args), out_specs=VMEM, out_s...  8.47 us
    ppermute x4, waiting for transfers between devices, swapped(): return lax.ppermute(array, axis, [(i, i ^ flip) for i in range(4)])  6.98 us
    unnamed x18, local copies, waits for them, and re-layouts  4.94 us
  transfers between devices with their start and end apart: 27, of which 11 were waited for; matrix products, arithmetic and copies ran while one was open for 0% of the time, Pallas kernels for 16%

profile of v6, /device:TPU:8, one launch (start us, length us, event | category | flops | bytes accessed | tf_op | source)
XLA Modules:
  0.0 126.2 jit_solution(7334814757673939344)
XLA Ops:
  2.0 8.5 %all-to-all-start = ((f32[8,16,256]{2,1,0:T(8,128)}), f32[8,16,256]{2,1,0:T(8,128)S(1)}, u32[]{:S(2)}, u32[]{:S(2)}) async-start(f32[8,16,256]{2,1,0:T(8,128)} %spread.2), calls=%async_computation | async-start | bytes 262144 | tf_op jit(solution)/shard_map/all_to_all | solution.py:483
  10.5 9.1 %dct.1 = (f32[2,4,128,256]{3,2,1,0:T(8,128)}, f32[2,4,128,256]{3,2,1,0:T(8,128)}) custom-call(f32[2,4096,256]{2,1,0:T(8,128)} %x3.1, f32[2,4096,256]{2,1,0:T(8,128)} %x3.1, f32[2,4096,256]{2,1,0:T(8,128)} %x3.1, f32[2,4096,256]{2,1,0:T(8,128)} %x3.1, f32[4,280,256]{2,1,0:T(8,128)} %constant.2.clone.table), custom_call_target="tpu_custom_call" | custom-call | flops 7000000000 | bytes 12000000 | tf_op jit(solution)/shard_map/dct/pallas_call | solution.py:145
  19.6 1.6 %collective-permute-start.4 = (f32[8,16,256]{2,1,0:T(8,128)S(1)}, f32[8,16,256]{2,1,0:T(8,128)S(1)}, u32[]{:S(2)}, u32[]{:S(2)}) collective-permute-start(f32[8,16,256]{2,1,0:T(8,128)S(1)} %all-to-all-done.refs_0_), channel_id=1, source_target_pairs={{0,8},{8,16},{16,24},{24,0},{1,9},{9,17},{17,25},{25,1},{2,10},{10... | collective-permute-start | bytes 393224 | tf_op jit(solution)/shard_map/ppermute | solution.py:437
  21.2 2.7 %collective-permute-start.5 = (f32[8,16,256]{2,1,0:T(8,128)S(1)}, f32[8,16,256]{2,1,0:T(8,128)S(1)}, u32[]{:S(2)}, u32[]{:S(2)}) collective-permute-start(f32[8,16,256]{2,1,0:T(8,128)S(1)} %all-to-all-done.refs_0_), channel_id=1, source_target_pairs={{0,16},{8,24},{16,0},{24,8},{1,17},{9,25},{17,1},{25,9},{2,18},{10... | collective-permute-start | bytes 393224 | tf_op jit(solution)/shard_map/ppermute | solution.py:437
  23.9 1.4 %collective-permute-start.6 = (f32[8,16,256]{2,1,0:T(8,128)S(1)}, f32[8,16,256]{2,1,0:T(8,128)S(1)}, u32[]{:S(2)}, u32[]{:S(2)}) collective-permute-start(f32[8,16,256]{2,1,0:T(8,128)S(1)} %all-to-all-done.refs_0_), channel_id=1, source_target_pairs={{0,24},{8,0},{16,8},{24,16},{1,25},{9,1},{17,9},{25,17},{2,26},{10... | collective-permute-start | bytes 393224 | tf_op jit(solution)/shard_map/ppermute | solution.py:437
  27.4 3.2 %collective-permute-done.5.refs_2_ = f32[8,16,256]{2,1,0:T(8,128)S(1)} collective-permute-done((f32[8,16,256]{2,1,0:T(8,128)S(1)}, f32[8,16,256]{2,1,0:T(8,128)S(1)}, u32[]{:S(2)}, u32[]{:S(2)}) %collective-permute-start.5) | collective-permute-done | bytes 131104 | tf_op jit(solution)/shard_map/ppermute | solution.py:437
  30.6 1.8 %totals.1 = (f32[4,32,256]{2,1,0:T(8,128)S(1)}, f32[4,32,256]{2,1,0:T(8,128)S(1)}) custom-call(bf16[4,256,512]{2,1,0:T(8,128)(2,1)S(1)} %get-tuple-element.39.high_t, bf16[4,256,512]{2,1,0:T(8,128)(2,1)S(1)} %get-tuple-element.40.low_t, f32[16,256]{1,0:T(8,128)S(1)} %get-tuple-element.34.weights, f32[8,16,256]{2,1,0:T(8,128)S(1)} %all-to-all-done.refs_0_, ...), custom_call_target="tpu_custom_call" | custom-call | flops 800000000 | bytes 4000000 | tf_op jit(solution)/shard_map/totals/pallas_call | solution.py:238
  32.5 1.5 %row_gram.1.mine = f32[256,256]{1,0:T(8,128)} custom-call(f32[8,16,256]{2,1,0:T(8,128)S(1)} %all-to-all-done.refs_0_, f32[8,16,256]{2,1,0:T(8,128)S(1)} %collective-permute-done.4.refs_1_, f32[8,16,256]{2,1,0:T(8,128)S(1)} %collective-permute-done.5.refs_2_, f32[8,16,256]{2,1,0:T(8,128)S(1)} %collective-permute-done.6.refs_3_), custom_call_target="tpu_custom_call" | custom-call | flops 400000000 | bytes 800000 | tf_op jit(solution)/shard_map/row_gram/pallas_call | solution.py:258
  34.5 2.3 %collective-permute-start.10 = (f32[32,256]{1,0:T(8,128)S(1)}, f32[32,256]{1,0:T(8,128)S(1)}, u32[]{:S(2)}, u32[]{:S(2)}) collective-permute-start(f32[32,256]{1,0:T(8,128)S(1)} %get-tuple-element.47), channel_id=1, source_target_pairs={{0,24},{8,0},{16,8},{24,16},{1,25},{9,1},{17,9},{25,17},{2,26},{10... | collective-permute-start | bytes 98312 | tf_op jit(solution)/shard_map/ppermute | solution.py:437
  37.9 3.6 %collective-permute-start.9 = (f32[32,256]{1,0:T(8,128)S(1)}, f32[32,256]{1,0:T(8,128)S(1)}, u32[]{:S(2)}, u32[]{:S(2)}) collective-permute-start(f32[32,256]{1,0:T(8,128)S(1)} %get-tuple-element.46), channel_id=1, source_target_pairs={{0,16},{8,24},{16,0},{24,8},{1,17},{9,25},{17,1},{25,9},{2,18},{10... | collective-permute-start | bytes 98312 | tf_op jit(solution)/shard_map/ppermute | solution.py:437
  41.6 22.7 %collective-permute-done.8.refs_1_ = f32[32,256]{1,0:T(8,128)S(1)} collective-permute-done((f32[32,256]{1,0:T(8,128)S(1)}, f32[32,256]{1,0:T(8,128)S(1)}, u32[]{:S(2)}, u32[]{:S(2)}) %collective-permute-start.8) | collective-permute-done | bytes 32800 | tf_op jit(solution)/shard_map/ppermute | solution.py:437
  65.0 7.2 %all-to-all-start.1 = ((f32[8,32,256]{2,1,0:T(8,128)}), f32[8,32,256]{2,1,0:T(8,128)S(1)}, u32[]{:S(2)}, u32[]{:S(2)}) async-start(f32[8,32,256]{2,1,0:T(8,128)} %spread.3), calls=%async_computation.1 | async-start | bytes 524288 | tf_op jit(solution)/shard_map/all_to_all | solution.py:483
  73.2 4.8 %shard_map.102.refs_4_ = f32[792,256]{1,0:T(8,128)S(1)} custom-call(f32[128,256]{1,0:T(8,128)S(1)} %copy-done.1, f32[16,256]{1,0:T(8,128)S(1)} %get-tuple-element.34.weights, f32[256,256]{1,0:T(8,128)} %row_gram.1.mine, f32[256,256]{1,0:T(8,128)} %collective-permute-done.11.other, f32[256,256]{1,0:T(8,128)S(1)} %copy-done.5, f32[256,256]{1,0:T(8,128)S(1)} %copy-done.6), custom_call_target="tpu_custom_call" | custom-call | flops 3000000000 | bytes 1000000 | tf_op jit(solution)/shard_map/pallas_call | solution.py:322
  78.9 3.8 %all-to-all-done.1.block = f32[8,32,256]{2,1,0:T(8,128)S(1)} async-done(((f32[8,32,256]{2,1,0:T(8,128)}), f32[8,32,256]{2,1,0:T(8,128)S(1)}, u32[]{:S(2)}, u32[]{:S(2)}) %all-to-all-start.1) | async-done | bytes 262176 | tf_op jit(solution)/shard_map/all_to_all | solution.py:483
  83.8 2.2 %collective-permute-start.14 = (f32[32,256]{1,0:T(8,128)S(1)}, f32[32,256]{1,0:T(8,128)S(1)}, u32[]{:S(2)}, u32[]{:S(2)}) collective-permute-start(f32[32,256]{1,0:T(8,128)S(1)} %folded.2.refs_5_), channel_id=1, source_target_pairs={{0,24},{8,0},{16,8},{24,16},{1,25},{9,1},{17,9},{25,17},{2,26},{10... | collective-permute-start | bytes 98312 | tf_op jit(solution)/shard_map/ppermute | solution.py:437
  86.0 1.9 %collective-permute-done.12.refs_6_ = f32[32,256]{1,0:T(8,128)S(1)} collective-permute-done((f32[32,256]{1,0:T(8,128)S(1)}, f32[32,256]{1,0:T(8,128)S(1)}, u32[]{:S(2)}, u32[]{:S(2)}) %collective-permute-start.12) | collective-permute-done | bytes 32800 | tf_op jit(solution)/shard_map/ppermute | solution.py:437
  91.5 4.1 %col_update.1 = (f32[256,256]{1,0:T(8,128)}, f32[256,256]{1,0:T(8,128)}, f32[128,256]{1,0:T(8,128)S(1)}, f32[8,16,256]{2,1,0:T(8,128)}) custom-call(f32[4,4,32,256]{3,2,1,0:T(8,128)S(1)} %get-tuple-element.35.refs_0_, f32[4,4,32,256]{3,2,1,0:T(8,128)S(1)} %collective-permute-done.1.refs_1_, f32[4,4,32,256]{3,2,1,0:T(8,128)} %collective-permute-done.2.refs_2_, ...), custom_call_target="tpu_custom_call" | custom-call | flops 1500000000 | bytes 5000000 | tf_op jit(solution)/shard_map/col_update/pallas_call | solution.py:398
  96.1 5.1 %collective-permute-done.19.refs_1_ = f32[128,256]{1,0:T(8,128)S(1)} collective-permute-done((f32[128,256]{1,0:T(8,128)S(1)}, f32[128,256]{1,0:T(8,128)S(1)}, u32[]{:S(2)}, u32[]{:S(2)}) %collective-permute-start.19) | collective-permute-done | bytes 131104 | tf_op jit(solution)/shard_map/ppermute | solution.py:441
  101.2 1.7 %collective-permute-start.20 = (f32[128,256]{1,0:T(8,128)S(1)}, f32[128,256]{1,0:T(8,128)S(1)}, u32[]{:S(2)}, u32[]{:S(2)}) collective-permute-start(f32[128,256]{1,0:T(8,128)S(1)} %summed.5.refs_0_), channel_id=1, source_target_pairs={{0,3},{1,2},{2,1},{3,0},{4,7},{5,6},{6,5},{7,4},{8,11},{9,10},{10,... | collective-permute-start | bytes 393224 | tf_op jit(solution)/shard_map/ppermute | solution.py:441
  102.9 4.8 %all-to-all-start.2 = ((f32[8,16,256]{2,1,0:T(8,128)}), f32[8,16,256]{2,1,0:T(8,128)S(1)}, u32[]{:S(2)}, u32[]{:S(2)}) async-start(f32[8,16,256]{2,1,0:T(8,128)} %get-tuple-element.51), calls=%async_computation.2 | async-start | bytes 262144 | tf_op jit(solution)/shard_map/all_to_all | solution.py:537
  107.8 8.9 %all-to-all-done.2.block = f32[8,16,256]{2,1,0:T(8,128)S(1)} async-done(((f32[8,16,256]{2,1,0:T(8,128)}), f32[8,16,256]{2,1,0:T(8,128)S(1)}, u32[]{:S(2)}, u32[]{:S(2)}) %all-to-all-start.2) | async-done | bytes 131104 | tf_op jit(solution)/shard_map/all_to_all | solution.py:537
  116.8 2.0 %collective-permute-start.22 = (f32[16,256]{1,0:T(8,128)S(1)}, f32[16,256]{1,0:T(8,128)S(1)}, u32[]{:S(2)}, u32[]{:S(2)}) collective-permute-start(f32[16,256]{1,0:T(8,128)S(1)} %folded.3.refs_0_), channel_id=1, source_target_pairs={{0,1},{1,0},{2,3},{3,2},{4,5},{5,4},{6,7},{7,6},{8,9},{9,8},{10,11... | collective-permute-start | bytes 49160 | tf_op jit(solution)/shard_map/ppermute | solution.py:441
  118.8 1.9 %collective-permute-done.22.refs_1_ = f32[16,256]{1,0:T(8,128)S(1)} collective-permute-done((f32[16,256]{1,0:T(8,128)S(1)}, f32[16,256]{1,0:T(8,128)S(1)}, u32[]{:S(2)}, u32[]{:S(2)}) %collective-permute-start.22) | collective-permute-done | bytes 16416 | tf_op jit(solution)/shard_map/ppermute | solution.py:441
  121.1 3.7 %shard_map.103.inv = f32[280,256]{1,0:T(8,128)S(1)} custom-call(f32[128,256]{1,0:T(8,128)S(1)} %copy-done.1, f32[16,256]{1,0:T(8,128)S(1)} %get-tuple-element.34.weights, f32[128,256]{1,0:T(8,128)S(1)} %summed.6.mine, f32[128,256]{1,0:T(8,128)S(1)} %collective-permute-done.21.other), custom_call_target="tpu_custom_call" | custom-call | flops 3000000000 | bytes 1000000 | tf_op jit(solution)/shard_map/pallas_call | solution.py:322
  (64 shorter events, 14.8 us)
Async XLA Ops:
  2.0 17.6 %all-to-all-start = ((f32[8,16,256]{2,1,0:T(8,128)}), f32[8,16,256]{2,1,0:T(8,128)S(1)}, u32[]{:S(2)}, u32[]{:S(2)}) async-start(f32[8,16,256]{2,1,0:T(8,128)} %spread.2), calls=%async_computation | async-start | bytes 262144 | tf_op jit(solution)/shard_map/all_to_all | solution.py:483
  19.6 5.7 %collective-permute-start = (f32[2,4,128,256]{3,2,1,0:T(8,128)}, f32[2,4,128,256]{3,2,1,0:T(8,128)S(1)}, u32[]{:S(2)}, u32[]{:S(2)}) collective-permute-start(f32[2,4,128,256]{3,2,1,0:T(8,128)} %get-tuple-element.33), channel_id=1, source_target_pairs={{0,4},{4,0},{1,5},{5,1},{2,6},{6,2},{3,7},{7,3},{8,12},{12,8},{9,1... | collective-permute-start | bytes 3145736 | tf_op jit(solution)/shard_map/ppermute | solution.py:437
  19.6 7.7 %collective-permute-start.4 = (f32[8,16,256]{2,1,0:T(8,128)S(1)}, f32[8,16,256]{2,1,0:T(8,128)S(1)}, u32[]{:S(2)}, u32[]{:S(2)}) collective-permute-start(f32[8,16,256]{2,1,0:T(8,128)S(1)} %all-to-all-done.refs_0_), channel_id=1, source_target_pairs={{0,8},{8,16},{16,24},{24,0},{1,9},{9,17},{17,25},{25,1},{2,10},{10... | collective-permute-start | bytes 393224 | tf_op jit(solution)/shard_map/ppermute | solution.py:437
  21.2 9.3 %collective-permute-start.5 = (f32[8,16,256]{2,1,0:T(8,128)S(1)}, f32[8,16,256]{2,1,0:T(8,128)S(1)}, u32[]{:S(2)}, u32[]{:S(2)}) collective-permute-start(f32[8,16,256]{2,1,0:T(8,128)S(1)} %all-to-all-done.refs_0_), channel_id=1, source_target_pairs={{0,16},{8,24},{16,0},{24,8},{1,17},{9,25},{17,1},{25,9},{2,18},{10... | collective-permute-start | bytes 393224 | tf_op jit(solution)/shard_map/ppermute | solution.py:437
  23.9 6.6 %collective-permute-start.6 = (f32[8,16,256]{2,1,0:T(8,128)S(1)}, f32[8,16,256]{2,1,0:T(8,128)S(1)}, u32[]{:S(2)}, u32[]{:S(2)}) collective-permute-start(f32[8,16,256]{2,1,0:T(8,128)S(1)} %all-to-all-done.refs_0_), channel_id=1, source_target_pairs={{0,24},{8,0},{16,8},{24,16},{1,25},{9,1},{17,9},{25,17},{2,26},{10... | collective-permute-start | bytes 393224 | tf_op jit(solution)/shard_map/ppermute | solution.py:437
  32.4 2.1 %collective-permute-start.7 = (f32[4,32,256]{2,1,0:T(8,128)S(1)}, f32[4,32,256]{2,1,0:T(8,128)S(1)}, u32[]{:S(2)}, u32[]{:S(2)}) collective-permute-start(f32[4,32,256]{2,1,0:T(8,128)S(1)} %get-tuple-element.43), channel_id=1, source_target_pairs={{0,4},{4,0},{1,5},{5,1},{2,6},{6,2},{3,7},{7,3},{8,12},{12,8},{9,1... | collective-permute-start | bytes 393224 | tf_op jit(solution)/shard_map/ppermute | solution.py:437
  34.0 38.2 %collective-permute-start.11 = (f32[256,256]{1,0:T(8,128)}, f32[256,256]{1,0:T(8,128)}, u32[]{:S(2)}, u32[]{:S(2)}) collective-permute-start(f32[256,256]{1,0:T(8,128)} %row_gram.1.mine), channel_id=1, source_target_pairs={{0,4},{4,0},{1,5},{5,1},{2,6},{6,2},{3,7},{7,3},{8,12},{12,8},{9,1... | collective-permute-start | bytes 786440 | tf_op jit(solution)/shard_map/ppermute | solution.py:437
  34.5 7.0 %collective-permute-start.10 = (f32[32,256]{1,0:T(8,128)S(1)}, f32[32,256]{1,0:T(8,128)S(1)}, u32[]{:S(2)}, u32[]{:S(2)}) collective-permute-start(f32[32,256]{1,0:T(8,128)S(1)} %get-tuple-element.47), channel_id=1, source_target_pairs={{0,24},{8,0},{16,8},{24,16},{1,25},{9,1},{17,9},{25,17},{2,26},{10... | collective-permute-start | bytes 98312 | tf_op jit(solution)/shard_map/ppermute | solution.py:437
  36.8 47.0 %collective-permute-start.1 = (f32[4,4,32,256]{3,2,1,0:T(8,128)S(1)}, f32[4,4,32,256]{3,2,1,0:T(8,128)S(1)}, u32[]{:S(2)}, u32[]{:S(2)}) collective-permute-start(f32[4,4,32,256]{3,2,1,0:T(8,128)S(1)} %get-tuple-element.36), channel_id=1, source_target_pairs={{0,8},{8,16},{16,24},{24,0},{1,9},{9,17},{17,25},{25,1},{2,10},{10... | collective-permute-start | bytes 1572872 | tf_op jit(solution)/shard_map/ppermute | solution.py:437
  36.8 27.4 %collective-permute-start.8 = (f32[32,256]{1,0:T(8,128)S(1)}, f32[32,256]{1,0:T(8,128)S(1)}, u32[]{:S(2)}, u32[]{:S(2)}) collective-permute-start(f32[32,256]{1,0:T(8,128)S(1)} %get-tuple-element.45), channel_id=1, source_target_pairs={{0,8},{8,16},{16,24},{24,0},{1,9},{9,17},{17,25},{25,1},{2,10},{10... | collective-permute-start | bytes 98312 | tf_op jit(solution)/shard_map/ppermute | solution.py:437
  37.9 26.3 %collective-permute-start.9 = (f32[32,256]{1,0:T(8,128)S(1)}, f32[32,256]{1,0:T(8,128)S(1)}, u32[]{:S(2)}, u32[]{:S(2)}) collective-permute-start(f32[32,256]{1,0:T(8,128)S(1)} %get-tuple-element.46), channel_id=1, source_target_pairs={{0,16},{8,24},{16,0},{24,8},{1,17},{9,25},{17,1},{25,9},{2,18},{10... | collective-permute-start | bytes 98312 | tf_op jit(solution)/shard_map/ppermute | solution.py:437
  41.5 44.5 %collective-permute-start.2 = (f32[4,4,32,256]{3,2,1,0:T(8,128)S(1)}, f32[4,4,32,256]{3,2,1,0:T(8,128)}, u32[]{:S(2)}, u32[]{:S(2)}) collective-permute-start(f32[4,4,32,256]{3,2,1,0:T(8,128)S(1)} %get-tuple-element.37), channel_id=1, source_target_pairs={{0,16},{8,24},{16,0},{24,8},{1,17},{9,25},{17,1},{25,9},{2,18},{10... | collective-permute-start | bytes 1572872 | tf_op jit(solution)/shard_map/ppermute | solution.py:437
  65.0 17.7 %all-to-all-start.1 = ((f32[8,32,256]{2,1,0:T(8,128)}), f32[8,32,256]{2,1,0:T(8,128)S(1)}, u32[]{:S(2)}, u32[]{:S(2)}) async-start(f32[8,32,256]{2,1,0:T(8,128)} %spread.3), calls=%async_computation.1 | async-start | bytes 524288 | tf_op jit(solution)/shard_map/all_to_all | solution.py:483
  72.2 16.9 %collective-permute-start.3 = (f32[4,4,32,256]{3,2,1,0:T(8,128)S(1)}, f32[4,4,32,256]{3,2,1,0:T(8,128)}, u32[]{:S(2)}, u32[]{:S(2)}) collective-permute-start(f32[4,4,32,256]{3,2,1,0:T(8,128)S(1)} %get-tuple-element.38), channel_id=1, source_target_pairs={{0,24},{8,0},{16,8},{24,16},{1,25},{9,1},{17,9},{25,17},{2,26},{10... | collective-permute-start | bytes 1572872 | tf_op jit(solution)/shard_map/ppermute | solution.py:437
  82.7 5.2 %collective-permute-start.12 = (f32[32,256]{1,0:T(8,128)S(1)}, f32[32,256]{1,0:T(8,128)S(1)}, u32[]{:S(2)}, u32[]{:S(2)}) collective-permute-start(f32[32,256]{1,0:T(8,128)S(1)} %folded.2.refs_5_), channel_id=1, source_target_pairs={{0,8},{8,16},{16,24},{24,0},{1,9},{9,17},{17,25},{25,1},{2,10},{10... | collective-permute-start | bytes 98312 | tf_op jit(solution)/shard_map/ppermute | solution.py:437
  82.8 5.5 %collective-permute-start.13 = (f32[32,256]{1,0:T(8,128)S(1)}, f32[32,256]{1,0:T(8,128)S(1)}, u32[]{:S(2)}, u32[]{:S(2)}) collective-permute-start(f32[32,256]{1,0:T(8,128)S(1)} %folded.2.refs_5_), channel_id=1, source_target_pairs={{0,16},{8,24},{16,0},{24,8},{1,17},{9,25},{17,1},{25,9},{2,18},{10... | collective-permute-start | bytes 98312 | tf_op jit(solution)/shard_map/ppermute | solution.py:437
  83.8 5.3 %collective-permute-start.14 = (f32[32,256]{1,0:T(8,128)S(1)}, f32[32,256]{1,0:T(8,128)S(1)}, u32[]{:S(2)}, u32[]{:S(2)}) collective-permute-start(f32[32,256]{1,0:T(8,128)S(1)} %folded.2.refs_5_), channel_id=1, source_target_pairs={{0,24},{8,0},{16,8},{24,16},{1,25},{9,1},{17,9},{25,17},{2,26},{10... | collective-permute-start | bytes 98312 | tf_op jit(solution)/shard_map/ppermute | solution.py:437
  86.0 3.1 %collective-permute-start.15 = (f32[32,256]{1,0:T(8,128)S(1)}, f32[32,256]{1,0:T(8,128)S(1)}, u32[]{:S(2)}, u32[]{:S(2)}) collective-permute-start(f32[32,256]{1,0:T(8,128)S(1)} %folded.2.refs_5_), channel_id=1, source_target_pairs={{0,4},{4,0},{1,5},{5,1},{2,6},{6,2},{3,7},{7,3},{8,12},{12,8},{9,1... | collective-permute-start | bytes 98312 | tf_op jit(solution)/shard_map/ppermute | solution.py:437
  95.5 5.7 %collective-permute-start.19 = (f32[128,256]{1,0:T(8,128)S(1)}, f32[128,256]{1,0:T(8,128)S(1)}, u32[]{:S(2)}, u32[]{:S(2)}) collective-permute-start(f32[128,256]{1,0:T(8,128)S(1)} %get-tuple-element.50.refs_0_), channel_id=1, source_target_pairs={{0,1},{1,0},{2,3},{3,2},{4,5},{5,4},{6,7},{7,6},{8,9},{9,8},{10,11... | collective-permute-start | bytes 393224 | tf_op jit(solution)/shard_map/ppermute | solution.py:441
  101.2 6.5 %collective-permute-start.20 = (f32[128,256]{1,0:T(8,128)S(1)}, f32[128,256]{1,0:T(8,128)S(1)}, u32[]{:S(2)}, u32[]{:S(2)}) collective-permute-start(f32[128,256]{1,0:T(8,128)S(1)} %summed.5.refs_0_), channel_id=1, source_target_pairs={{0,3},{1,2},{2,1},{3,0},{4,7},{5,6},{6,5},{7,4},{8,11},{9,10},{10,... | collective-permute-start | bytes 393224 | tf_op jit(solution)/shard_map/ppermute | solution.py:441
  102.9 13.9 %all-to-all-start.2 = ((f32[8,16,256]{2,1,0:T(8,128)}), f32[8,16,256]{2,1,0:T(8,128)S(1)}, u32[]{:S(2)}, u32[]{:S(2)}) async-start(f32[8,16,256]{2,1,0:T(8,128)} %get-tuple-element.51), calls=%async_computation.2 | async-start | bytes 262144 | tf_op jit(solution)/shard_map/all_to_all | solution.py:537
  107.7 13.4 %collective-permute-start.21 = (f32[128,256]{1,0:T(8,128)S(1)}, f32[128,256]{1,0:T(8,128)S(1)}, u32[]{:S(2)}, u32[]{:S(2)}) collective-permute-start(f32[128,256]{1,0:T(8,128)S(1)} %summed.6.mine), channel_id=1, source_target_pairs={{0,4},{4,0},{1,5},{5,1},{2,6},{6,2},{3,7},{7,3},{8,12},{12,8},{9,1... | collective-permute-start | bytes 393224 | tf_op jit(solution)/shard_map/ppermute | solution.py:437
  116.8 3.8 %collective-permute-start.22 = (f32[16,256]{1,0:T(8,128)S(1)}, f32[16,256]{1,0:T(8,128)S(1)}, u32[]{:S(2)}, u32[]{:S(2)}) collective-permute-start(f32[16,256]{1,0:T(8,128)S(1)} %folded.3.refs_0_), channel_id=1, source_target_pairs={{0,1},{1,0},{2,3},{3,2},{4,5},{5,4},{6,7},{7,6},{8,9},{9,8},{10,11... | collective-permute-start | bytes 49160 | tf_op jit(solution)/shard_map/ppermute | solution.py:441
  120.6 4.2 %collective-permute-start.23 = (f32[16,256]{1,0:T(8,128)S(1)}, f32[16,256]{1,0:T(8,128)S(1)}, u32[]{:S(2)}, u32[]{:S(2)}) collective-permute-start(f32[16,256]{1,0:T(8,128)S(1)} %summed.7.mine), channel_id=1, source_target_pairs={{0,3},{1,2},{2,1},{3,0},{4,7},{5,6},{6,5},{7,4},{8,11},{9,10},{10,... | collective-permute-start | bytes 49160 | tf_op jit(solution)/shard_map/ppermute | solution.py:441
  (12 other events, 151.9 us)

commit v7 on v6

--- a/solution.py
+++ b/solution.py
@@ -182,11 +182,13 @@
     weights[...] = jnp.concatenate(sum(lines, []), axis=0)
     for s in range(4):
         source = own if s < 2 else other
-        for k in range(4):
-            place = slice(HALF * k, HALF * (k + 1))
-            high_t[s, :, place], low_t[s, :, place] = split(source[s % 2, k].T)
-            for shift, block in enumerate(blocks):
-                start = pl.multiple_of(lax.rem(x + shift, NX) * 32, 32)
+        for at in range(NX):
+            rows = [source[s % 2, k, 32 * at : 32 * at + 32, :] for k in range(4)]
+            place = slice(HALF * at, HALF * at + HALF)
+            high_t[s, :, place], low_t[s, :, place] = split(jnp.concatenate(rows, axis=0).T)
+        for shift, block in enumerate(blocks):
+            start = pl.multiple_of(lax.rem(x + shift, NX) * 32, 32)
+            for k in range(4):
                 block[s, k] = source[s % 2, k, pl.ds(start, 32), :]
 
 
@@ -214,18 +216,33 @@
                 rows[half, pl.ds(start, 16), :] = pieces[shift][z, :, 128 * half : 128 * half + 128]
 
 
-def totals_kernel(high_t, low_t, weights, *refs):
-    pieces, (keep, send), (rows, total) = refs[:4], refs[4:6], refs[6:]
-    _, x, core, _ = place_of_own()
-    place_rows(x, pieces, rows)
-    sums = [0.0] * 4
-    for k in range(4):
-        line = [rows[half, pl.ds(k, HALF, stride=4), :] for half in range(2)]
-        lines = split(jnp.concatenate(line, axis=1))
-        place = slice(HALF * k, HALF * (k + 1))
-        for s in range(4):
-            sums[s] += dot3((high_t[s, :, place], low_t[s, :, place]), lines)
-    total[...] = sum(part * weights[s : s + 1, :] for s, part in enumerate(sums))
+def piece_sums(high_t, low_t, weights, x, shift, piece, rows):
+    for z in range(NZ):
+        for half in range(2):
+            rows[half, 16 * z : 16 * z + 16, :] = piece[z, :, 128 * half : 128 * half + 128]
+    lines = [
+        jnp.concatenate([rows[half, pl.ds(k, 32, stride=4), :] for half in range(2)], axis=1)
+        for k in range(4)
+    ]
+    lines = split(jnp.concatenate(lines, axis=0))
+    start = pl.multiple_of(lax.rem(x - shift + NX, NX) * HALF, HALF)
+    total = 0.0
+    for s in range(4):
+        part = high_t[s, :, pl.ds(start, HALF)], low_t[s, :, pl.ds(start, HALF)]
+        total += dot3(part, lines) * weights[s : s + 1, :]
+    return total
+
+
+def early_kernel(high_t, low_t, weights, first, second, third, total, rows):
+    x = lax.axis_index("x")
+    total[...] = piece_sums(high_t, low_t, weights, x, 0, first, rows)
+    total[...] += piece_sums(high_t, low_t, weights, x, 1, second, rows)
+    total[...] += piece_sums(high_t, low_t, weights, x, 3, third, rows)
+
+
+def totals_kernel(high_t, low_t, weights, piece, early, keep, send, rows, total):
+    x, core = lax.axis_index("x"), lax.axis_index("c")
+    total[...] = early[...] + piece_sums(high_t, low_t, weights, x, 2, piece, rows)
     for shift in range(NX):
         target = lax.rem(x + shift, NX)
         for ref, owner in ((keep, core), (send, 1 - core)):
@@ -234,17 +251,29 @@
 
 
 def totals(high_t, low_t, weights, pieces):
+    rows, total = pltpu.VMEM((2, 128, 128), F32), pltpu.VMEM((COLS, RANK), F32)
+    cost = pl.CostEstimate(flops=400_000_000, bytes_accessed=2_000_000, transcendentals=0)
+    early = pl.pallas_call(
+        early_kernel,
+        in_specs=[VMEM] * 6,
+        out_specs=VMEM,
+        out_shape=jax.ShapeDtypeStruct((COLS, RANK), F32),
+        scratch_shapes=[rows],
+        compiler_params=room(12),
+        cost_estimate=cost,
+        name="early_totals",
+    )(high_t, low_t, weights, pieces[0], pieces[1], pieces[3])
     part = jax.ShapeDtypeStruct((NX, 32, RANK), F32)
     return pl.pallas_call(
         totals_kernel,
-        in_specs=[VMEM] * 7,
+        in_specs=[VMEM] * 5,
         out_specs=[VMEM] * 2,
         out_shape=[part] * 2,
-        scratch_shapes=[pltpu.VMEM((2, KEEP // 2, 128), F32), pltpu.VMEM((COLS, RANK), F32)],
+        scratch_shapes=[rows, total],
         compiler_params=room(12),
-        cost_estimate=pl.CostEstimate(flops=800_000_000, bytes_accessed=4_000_000, transcendentals=0),
+        cost_estimate=cost,
         name="totals",
-    )(high_t, low_t, weights, *pieces)
+    )(high_t, low_t, weights, pieces[2], early)
 
 
 def row_gram_kernel(*refs):
@@ -518,7 +547,8 @@
     other = shifted(gram, "c", NC, 1)
     args = snap_factor, weights, gram, other
     inv = system(col_system_kernel, DUAL + COLS, *args, col_factor, col_dual)
-    parts = list(summed([keep, shifted(send, "c", NC, 1)], (32, RANK), NX))
+    send = shifted(send, "c", NC, 1)
+    parts = list(summed([keep, send], (32, RANK), NX))
     parts = [parts[0], *around(parts, "x")]
     chunk = copied_along(parts, "z", NZ)
     coefficients = [blocks[0], *around(list(blocks), "x")]

time: 128 us -> 129 us (level)
  waiting for transfers between devices: 49.8 us -> 48.5 us
  transfers between devices with their start and end apart: 27 -> 27, of which waited for: 11 -> 12; matrix products, arithmetic and copies ran while one was open for 0% -> 0% of each run, Pallas kernels for 16% -> 17%
where the time goes in v7:
time: 129 us; the launch traced here: 127 us
  waiting for transfers between devices  48.5 us (38%)
  starting transfers between devices  43 us (33%)
  Pallas kernels  28.6 us (22%)
  local copies, waits for them, and re-layouts  5.88 us (5%)
    ppermute x20, waiting for transfers between devices, shifted(): lax.ppermute(array, axis, [(i, (i + by) % size) for i in range(size)])  29.3 us
    ppermute x20, starting transfers between devices, shifted(): lax.ppermute(array, axis, [(i, (i + by) % size) for i in range(size)])  17.4 us
    all_to_all x2, starting transfers between devices, copied_along(): return lax.all_to_all(whole, axes, 0, 0, tiled=True)  15.7 us
    pallas_call x1, Pallas kernels, dct(): pl.pallas_call(dct_kernel, grid=(steps,), in_specs=[pl.BlockSpec(block, l...  9.11 us
    all_to_all x1, waiting for transfers between devices, update(): block = lax.all_to_all(block, 'z', 0, 0, tiled=True)  8.95 us
    pallas_call x2, Pallas kernels, system(): pl.pallas_call(kernel, in_specs=[VMEM] * len(args), out_specs=VMEM, out_s...  8.47 us
    ppermute x4, waiting for transfers between devices, swapped(): return lax.ppermute(array, axis, [(i, i ^ flip) for i in range(4)])  6.99 us
    unnamed x18, local copies, waits for them, and re-layouts  5.88 us
  transfers between devices with their start and end apart: 27, of which 12 were waited for; matrix products, arithmetic and copies ran while one was open for 0% of the time, Pallas kernels for 17%

profile of v7, /device:TPU:8, one launch (start us, length us, event | category | flops | bytes accessed | tf_op | source)
XLA Modules:
  0.0 126.9 jit_solution(15084493937079354918)
XLA Ops:
  2.0 8.5 %all-to-all-start = ((f32[8,16,256]{2,1,0:T(8,128)}), f32[8,16,256]{2,1,0:T(8,128)S(1)}, u32[]{:S(2)}, u32[]{:S(2)}) async-start(f32[8,16,256]{2,1,0:T(8,128)} %spread.2), calls=%async_computation | async-start | bytes 262144 | tf_op jit(solution)/shard_map/all_to_all | solution.py:512
  10.5 9.1 %dct.1 = (f32[2,4,128,256]{3,2,1,0:T(8,128)}, f32[2,4,128,256]{3,2,1,0:T(8,128)}) custom-call(f32[2,4096,256]{2,1,0:T(8,128)} %x3.1, f32[2,4096,256]{2,1,0:T(8,128)} %x3.1, f32[2,4096,256]{2,1,0:T(8,128)} %x3.1, f32[2,4096,256]{2,1,0:T(8,128)} %x3.1, f32[4,280,256]{2,1,0:T(8,128)} %constant.2.clone.table), custom_call_target="tpu_custom_call" | custom-call | flops 7000000000 | bytes 12000000 | tf_op jit(solution)/shard_map/dct/pallas_call | solution.py:145
  19.6 1.6 %collective-permute-start.5 = (f32[8,16,256]{2,1,0:T(8,128)S(1)}, f32[8,16,256]{2,1,0:T(8,128)S(1)}, u32[]{:S(2)}, u32[]{:S(2)}) collective-permute-start(f32[8,16,256]{2,1,0:T(8,128)S(1)} %all-to-all-done.first.refs_0_), channel_id=1, source_target_pairs={{0,8},{8,16},{16,24},{24,0},{1,9},{9,17},{17,25},{25,1},{2,10},{10... | collective-permute-start | bytes 393224 | tf_op jit(solution)/shard_map/ppermute | solution.py:466
  21.2 1.7 %collective-permute-start.6 = (f32[8,16,256]{2,1,0:T(8,128)S(1)}, f32[8,16,256]{2,1,0:T(8,128)S(1)}, u32[]{:S(2)}, u32[]{:S(2)}) collective-permute-start(f32[8,16,256]{2,1,0:T(8,128)S(1)} %all-to-all-done.first.refs_0_), channel_id=1, source_target_pairs={{0,24},{8,0},{16,8},{24,16},{1,25},{9,1},{17,9},{25,17},{2,26},{10... | collective-permute-start | bytes 393224 | tf_op jit(solution)/shard_map/ppermute | solution.py:466
  22.9 1.8 %collective-permute-start.4 = (f32[8,16,256]{2,1,0:T(8,128)S(1)}, f32[8,16,256]{2,1,0:T(8,128)S(1)}, u32[]{:S(2)}, u32[]{:S(2)}) collective-permute-start(f32[8,16,256]{2,1,0:T(8,128)S(1)} %all-to-all-done.first.refs_0_), channel_id=1, source_target_pairs={{0,16},{8,24},{16,0},{24,8},{1,17},{9,25},{17,1},{25,9},{2,18},{10... | collective-permute-start | bytes 393224 | tf_op jit(solution)/shard_map/ppermute | solution.py:466
  26.7 2.1 %collective-permute-done.6.third.refs_3_ = f32[8,16,256]{2,1,0:T(8,128)S(1)} collective-permute-done((f32[8,16,256]{2,1,0:T(8,128)S(1)}, f32[8,16,256]{2,1,0:T(8,128)S(1)}, u32[]{:S(2)}, u32[]{:S(2)}) %collective-permute-start.6) | collective-permute-done | bytes 131104 | tf_op jit(solution)/shard_map/ppermute | solution.py:466
  28.8 1.4 %early_totals.1.early = f32[256,256]{1,0:T(8,128)S(1)} custom-call(bf16[4,256,512]{2,1,0:T(8,128)(2,1)S(1)} %get-tuple-element.39.high_t, bf16[4,256,512]{2,1,0:T(8,128)(2,1)S(1)} %get-tuple-element.40.low_t, f32[16,256]{1,0:T(8,128)S(1)} %get-tuple-element.34.weights, f32[8,16,256]{2,1,0:T(8,128)S(1)} %all-to-all-done.first.refs_0_, ...), custom_call_target="tpu_custom_call" | custom-call | flops 400000000 | bytes 2000000 | tf_op jit(solution)/shard_map/early_totals/pallas_call | solution.py:256
  31.2 1.5 %row_gram.1.mine = f32[256,256]{1,0:T(8,128)} custom-call(f32[8,16,256]{2,1,0:T(8,128)S(1)} %all-to-all-done.first.refs_0_, f32[8,16,256]{2,1,0:T(8,128)S(1)} %collective-permute-done.5.second.refs_1_, f32[8,16,256]{2,1,0:T(8,128)S(1)} %collective-permute-done.4.piece.refs_2_, f32[8,16,256]{2,1,0:T(8,128)S(1)} %collective-permute-done.6.third.refs_3_), custom_call_target="tpu_custom_call" | custom-call | flops 400000000 | bytes 800000 | tf_op jit(solution)/shard_map/row_gram/pallas_call | solution.py:287
  33.2 3.5 %collective-permute-start.10 = (f32[32,256]{1,0:T(8,128)S(1)}, f32[32,256]{1,0:T(8,128)S(1)}, u32[]{:S(2)}, u32[]{:S(2)}) collective-permute-start(f32[32,256]{1,0:T(8,128)S(1)} %get-tuple-element.47), channel_id=1, source_target_pairs={{0,24},{8,0},{16,8},{24,16},{1,25},{9,1},{17,9},{25,17},{2,26},{10... | collective-permute-start | bytes 98312 | tf_op jit(solution)/shard_map/ppermute | solution.py:466
  36.7 4.7 %collective-permute-start.9 = (f32[32,256]{1,0:T(8,128)S(1)}, f32[32,256]{1,0:T(8,128)S(1)}, u32[]{:S(2)}, u32[]{:S(2)}) collective-permute-start(f32[32,256]{1,0:T(8,128)S(1)} %get-tuple-element.46), channel_id=1, source_target_pairs={{0,16},{8,24},{16,0},{24,8},{1,17},{9,25},{17,1},{25,9},{2,18},{10... | collective-permute-start | bytes 98312 | tf_op jit(solution)/shard_map/ppermute | solution.py:466
  41.4 22.7 %collective-permute-done.8.refs_1_ = f32[32,256]{1,0:T(8,128)S(1)} collective-permute-done((f32[32,256]{1,0:T(8,128)S(1)}, f32[32,256]{1,0:T(8,128)S(1)}, u32[]{:S(2)}, u32[]{:S(2)}) %collective-permute-start.8) | collective-permute-done | bytes 32800 | tf_op jit(solution)/shard_map/ppermute | solution.py:466
  64.8 7.2 %all-to-all-start.1 = ((f32[8,32,256]{2,1,0:T(8,128)}), f32[8,32,256]{2,1,0:T(8,128)S(1)}, u32[]{:S(2)}, u32[]{:S(2)}) async-start(f32[8,32,256]{2,1,0:T(8,128)} %spread.3), calls=%async_computation.1 | async-start | bytes 524288 | tf_op jit(solution)/shard_map/all_to_all | solution.py:512
  73.9 4.8 %shard_map.102.refs_4_ = f32[792,256]{1,0:T(8,128)S(1)} custom-call(f32[128,256]{1,0:T(8,128)S(1)} %copy-done.1, f32[16,256]{1,0:T(8,128)S(1)} %get-tuple-element.34.weights, f32[256,256]{1,0:T(8,128)} %row_gram.1.mine, f32[256,256]{1,0:T(8,128)} %collective-permute-done.11.other, f32[256,256]{1,0:T(8,128)S(1)} %copy-done.5, f32[256,256]{1,0:T(8,128)S(1)} %copy-done.6), custom_call_target="tpu_custom_call" | custom-call | flops 3000000000 | bytes 1000000 | tf_op jit(solution)/shard_map/pallas_call | solution.py:351
  79.6 3.3 %all-to-all-done.1.block = f32[8,32,256]{2,1,0:T(8,128)S(1)} async-done(((f32[8,32,256]{2,1,0:T(8,128)}), f32[8,32,256]{2,1,0:T(8,128)S(1)}, u32[]{:S(2)}, u32[]{:S(2)}) %all-to-all-start.1) | async-done | bytes 262176 | tf_op jit(solution)/shard_map/all_to_all | solution.py:512
  83.6 2.7 %collective-permute-start.14 = (f32[32,256]{1,0:T(8,128)S(1)}, f32[32,256]{1,0:T(8,128)S(1)}, u32[]{:S(2)}, u32[]{:S(2)}) collective-permute-start(f32[32,256]{1,0:T(8,128)S(1)} %folded.2.refs_5_), channel_id=1, source_target_pairs={{0,24},{8,0},{16,8},{24,16},{1,25},{9,1},{17,9},{25,17},{2,26},{10... | collective-permute-start | bytes 98312 | tf_op jit(solution)/shard_map/ppermute | solution.py:466
  86.3 1.9 %collective-permute-done.12.refs_6_ = f32[32,256]{1,0:T(8,128)S(1)} collective-permute-done((f32[32,256]{1,0:T(8,128)S(1)}, f32[32,256]{1,0:T(8,128)S(1)}, u32[]{:S(2)}, u32[]{:S(2)}) %collective-permute-start.12) | collective-permute-done | bytes 32800 | tf_op jit(solution)/shard_map/ppermute | solution.py:466
  91.7 4.1 %col_update.1 = (f32[256,256]{1,0:T(8,128)}, f32[256,256]{1,0:T(8,128)}, f32[128,256]{1,0:T(8,128)S(1)}, f32[8,16,256]{2,1,0:T(8,128)}) custom-call(f32[4,4,32,256]{3,2,1,0:T(8,128)S(1)} %get-tuple-element.35.refs_0_, f32[4,4,32,256]{3,2,1,0:T(8,128)S(1)} %collective-permute-done.1.refs_1_, f32[4,4,32,256]{3,2,1,0:T(8,128)} %collective-permute-done.2.refs_2_, ...), custom_call_target="tpu_custom_call" | custom-call | flops 1500000000 | bytes 5000000 | tf_op jit(solution)/shard_map/col_update/pallas_call | solution.py:427
  96.3 5.1 %collective-permute-done.19.refs_1_ = f32[128,256]{1,0:T(8,128)S(1)} collective-permute-done((f32[128,256]{1,0:T(8,128)S(1)}, f32[128,256]{1,0:T(8,128)S(1)}, u32[]{:S(2)}, u32[]{:S(2)}) %collective-permute-start.19) | collective-permute-done | bytes 131104 | tf_op jit(solution)/shard_map/ppermute | solution.py:470
  101.5 1.7 %collective-permute-start.20 = (f32[128,256]{1,0:T(8,128)S(1)}, f32[128,256]{1,0:T(8,128)S(1)}, u32[]{:S(2)}, u32[]{:S(2)}) collective-permute-start(f32[128,256]{1,0:T(8,128)S(1)} %summed.5.refs_0_), channel_id=1, source_target_pairs={{0,3},{1,2},{2,1},{3,0},{4,7},{5,6},{6,5},{7,4},{8,11},{9,10},{10,... | collective-permute-start | bytes 393224 | tf_op jit(solution)/shard_map/ppermute | solution.py:470
  103.1 5.3 %all-to-all-start.2 = ((f32[8,16,256]{2,1,0:T(8,128)}), f32[8,16,256]{2,1,0:T(8,128)S(1)}, u32[]{:S(2)}, u32[]{:S(2)}) async-start(f32[8,16,256]{2,1,0:T(8,128)} %get-tuple-element.51), calls=%async_computation.2 | async-start | bytes 262144 | tf_op jit(solution)/shard_map/all_to_all | solution.py:567
  108.6 8.9 %all-to-all-done.2.block = f32[8,16,256]{2,1,0:T(8,128)S(1)} async-done(((f32[8,16,256]{2,1,0:T(8,128)}), f32[8,16,256]{2,1,0:T(8,128)S(1)}, u32[]{:S(2)}, u32[]{:S(2)}) %all-to-all-start.2) | async-done | bytes 131104 | tf_op jit(solution)/shard_map/all_to_all | solution.py:567
  117.6 2.0 %collective-permute-start.22 = (f32[16,256]{1,0:T(8,128)S(1)}, f32[16,256]{1,0:T(8,128)S(1)}, u32[]{:S(2)}, u32[]{:S(2)}) collective-permute-start(f32[16,256]{1,0:T(8,128)S(1)} %folded.3.refs_0_), channel_id=1, source_target_pairs={{0,1},{1,0},{2,3},{3,2},{4,5},{5,4},{6,7},{7,6},{8,9},{9,8},{10,11... | collective-permute-start | bytes 49160 | tf_op jit(solution)/shard_map/ppermute | solution.py:470
  119.5 1.9 %collective-permute-done.22.refs_1_ = f32[16,256]{1,0:T(8,128)S(1)} collective-permute-done((f32[16,256]{1,0:T(8,128)S(1)}, f32[16,256]{1,0:T(8,128)S(1)}, u32[]{:S(2)}, u32[]{:S(2)}) %collective-permute-start.22) | collective-permute-done | bytes 16416 | tf_op jit(solution)/shard_map/ppermute | solution.py:470
  121.9 3.7 %shard_map.103.inv = f32[280,256]{1,0:T(8,128)S(1)} custom-call(f32[128,256]{1,0:T(8,128)S(1)} %copy-done.1, f32[16,256]{1,0:T(8,128)S(1)} %get-tuple-element.34.weights, f32[128,256]{1,0:T(8,128)S(1)} %summed.6.mine, f32[128,256]{1,0:T(8,128)S(1)} %collective-permute-done.21.other), custom_call_target="tpu_custom_call" | custom-call | flops 3000000000 | bytes 1000000 | tf_op jit(solution)/shard_map/pallas_call | solution.py:351
  (65 shorter events, 15.1 us)
Async XLA Ops:
  2.0 17.6 %all-to-all-start = ((f32[8,16,256]{2,1,0:T(8,128)}), f32[8,16,256]{2,1,0:T(8,128)S(1)}, u32[]{:S(2)}, u32[]{:S(2)}) async-start(f32[8,16,256]{2,1,0:T(8,128)} %spread.2), calls=%async_computation | async-start | bytes 262144 | tf_op jit(solution)/shard_map/all_to_all | solution.py:512
  19.6 5.1 %collective-permute-start = (f32[2,4,128,256]{3,2,1,0:T(8,128)}, f32[2,4,128,256]{3,2,1,0:T(8,128)S(1)}, u32[]{:S(2)}, u32[]{:S(2)}) collective-permute-start(f32[2,4,128,256]{3,2,1,0:T(8,128)} %get-tuple-element.33), channel_id=1, source_target_pairs={{0,4},{4,0},{1,5},{5,1},{2,6},{6,2},{3,7},{7,3},{8,12},{12,8},{9,1... | collective-permute-start | bytes 3145736 | tf_op jit(solution)/shard_map/ppermute | solution.py:466
  19.6 7.1 %collective-permute-start.5 = (f32[8,16,256]{2,1,0:T(8,128)S(1)}, f32[8,16,256]{2,1,0:T(8,128)S(1)}, u32[]{:S(2)}, u32[]{:S(2)}) collective-permute-start(f32[8,16,256]{2,1,0:T(8,128)S(1)} %all-to-all-done.first.refs_0_), channel_id=1, source_target_pairs={{0,8},{8,16},{16,24},{24,0},{1,9},{9,17},{17,25},{25,1},{2,10},{10... | collective-permute-start | bytes 393224 | tf_op jit(solution)/shard_map/ppermute | solution.py:466
  21.2 7.7 %collective-permute-start.6 = (f32[8,16,256]{2,1,0:T(8,128)S(1)}, f32[8,16,256]{2,1,0:T(8,128)S(1)}, u32[]{:S(2)}, u32[]{:S(2)}) collective-permute-start(f32[8,16,256]{2,1,0:T(8,128)S(1)} %all-to-all-done.first.refs_0_), channel_id=1, source_target_pairs={{0,24},{8,0},{16,8},{24,16},{1,25},{9,1},{17,9},{25,17},{2,26},{10... | collective-permute-start | bytes 393224 | tf_op jit(solution)/shard_map/ppermute | solution.py:466
  22.9 7.6 %collective-permute-start.4 = (f32[8,16,256]{2,1,0:T(8,128)S(1)}, f32[8,16,256]{2,1,0:T(8,128)S(1)}, u32[]{:S(2)}, u32[]{:S(2)}) collective-permute-start(f32[8,16,256]{2,1,0:T(8,128)S(1)} %all-to-all-done.first.refs_0_), channel_id=1, source_target_pairs={{0,16},{8,24},{16,0},{24,8},{1,17},{9,25},{17,1},{25,9},{2,18},{10... | collective-permute-start | bytes 393224 | tf_op jit(solution)/shard_map/ppermute | solution.py:466
  31.1 2.1 %collective-permute-start.7 = (f32[4,32,256]{2,1,0:T(8,128)S(1)}, f32[4,32,256]{2,1,0:T(8,128)S(1)}, u32[]{:S(2)}, u32[]{:S(2)}) collective-permute-start(f32[4,32,256]{2,1,0:T(8,128)S(1)} %get-tuple-element.43), channel_id=1, source_target_pairs={{0,4},{4,0},{1,5},{5,1},{2,6},{6,2},{3,7},{7,3},{8,12},{12,8},{9,1... | collective-permute-start | bytes 393224 | tf_op jit(solution)/shard_map/ppermute | solution.py:466
  32.7 39.3 %collective-permute-start.11 = (f32[256,256]{1,0:T(8,128)}, f32[256,256]{1,0:T(8,128)}, u32[]{:S(2)}, u32[]{:S(2)}) collective-permute-start(f32[256,256]{1,0:T(8,128)} %row_gram.1.mine), channel_id=1, source_target_pairs={{0,4},{4,0},{1,5},{5,1},{2,6},{6,2},{3,7},{7,3},{8,12},{12,8},{9,1... | collective-permute-start | bytes 786440 | tf_op jit(solution)/shard_map/ppermute | solution.py:466
  33.2 8.2 %collective-permute-start.10 = (f32[32,256]{1,0:T(8,128)S(1)}, f32[32,256]{1,0:T(8,128)S(1)}, u32[]{:S(2)}, u32[]{:S(2)}) collective-permute-start(f32[32,256]{1,0:T(8,128)S(1)} %get-tuple-element.47), channel_id=1, source_target_pairs={{0,24},{8,0},{16,8},{24,16},{1,25},{9,1},{17,9},{25,17},{2,26},{10... | collective-permute-start | bytes 98312 | tf_op jit(solution)/shard_map/ppermute | solution.py:466
  36.7 46.9 %collective-permute-start.1 = (f32[4,4,32,256]{3,2,1,0:T(8,128)S(1)}, f32[4,4,32,256]{3,2,1,0:T(8,128)S(1)}, u32[]{:S(2)}, u32[]{:S(2)}) collective-permute-start(f32[4,4,32,256]{3,2,1,0:T(8,128)S(1)} %get-tuple-element.36), channel_id=1, source_target_pairs={{0,8},{8,16},{16,24},{24,0},{1,9},{9,17},{17,25},{25,1},{2,10},{10... | collective-permute-start | bytes 1572872 | tf_op jit(solution)/shard_map/ppermute | solution.py:466
  36.7 27.4 %collective-permute-start.8 = (f32[32,256]{1,0:T(8,128)S(1)}, f32[32,256]{1,0:T(8,128)S(1)}, u32[]{:S(2)}, u32[]{:S(2)}) collective-permute-start(f32[32,256]{1,0:T(8,128)S(1)} %get-tuple-element.45), channel_id=1, source_target_pairs={{0,8},{8,16},{16,24},{24,0},{1,9},{9,17},{17,25},{25,1},{2,10},{10... | collective-permute-start | bytes 98312 | tf_op jit(solution)/shard_map/ppermute | solution.py:466
  36.7 27.4 %collective-permute-start.9 = (f32[32,256]{1,0:T(8,128)S(1)}, f32[32,256]{1,0:T(8,128)S(1)}, u32[]{:S(2)}, u32[]{:S(2)}) collective-permute-start(f32[32,256]{1,0:T(8,128)S(1)} %get-tuple-element.46), channel_id=1, source_target_pairs={{0,16},{8,24},{16,0},{24,8},{1,17},{9,25},{17,1},{25,9},{2,18},{10... | collective-permute-start | bytes 98312 | tf_op jit(solution)/shard_map/ppermute | solution.py:466
  41.4 44.9 %collective-permute-start.2 = (f32[4,4,32,256]{3,2,1,0:T(8,128)S(1)}, f32[4,4,32,256]{3,2,1,0:T(8,128)}, u32[]{:S(2)}, u32[]{:S(2)}) collective-permute-start(f32[4,4,32,256]{3,2,1,0:T(8,128)S(1)} %get-tuple-element.37), channel_id=1, source_target_pairs={{0,16},{8,24},{16,0},{24,8},{1,17},{9,25},{17,1},{25,9},{2,18},{10... | collective-permute-start | bytes 1572872 | tf_op jit(solution)/shard_map/ppermute | solution.py:466
  64.8 18.1 %all-to-all-start.1 = ((f32[8,32,256]{2,1,0:T(8,128)}), f32[8,32,256]{2,1,0:T(8,128)S(1)}, u32[]{:S(2)}, u32[]{:S(2)}) async-start(f32[8,32,256]{2,1,0:T(8,128)} %spread.3), calls=%async_computation.1 | async-start | bytes 524288 | tf_op jit(solution)/shard_map/all_to_all | solution.py:512
  72.0 17.4 %collective-permute-start.3 = (f32[4,4,32,256]{3,2,1,0:T(8,128)S(1)}, f32[4,4,32,256]{3,2,1,0:T(8,128)}, u32[]{:S(2)}, u32[]{:S(2)}) collective-permute-start(f32[4,4,32,256]{3,2,1,0:T(8,128)S(1)} %get-tuple-element.38), channel_id=1, source_target_pairs={{0,24},{8,0},{16,8},{24,16},{1,25},{9,1},{17,9},{25,17},{2,26},{10... | collective-permute-start | bytes 1572872 | tf_op jit(solution)/shard_map/ppermute | solution.py:466
  83.0 5.2 %collective-permute-start.12 = (f32[32,256]{1,0:T(8,128)S(1)}, f32[32,256]{1,0:T(8,128)S(1)}, u32[]{:S(2)}, u32[]{:S(2)}) collective-permute-start(f32[32,256]{1,0:T(8,128)S(1)} %folded.2.refs_5_), channel_id=1, source_target_pairs={{0,8},{8,16},{16,24},{24,0},{1,9},{9,17},{17,25},{25,1},{2,10},{10... | collective-permute-start | bytes 98312 | tf_op jit(solution)/shard_map/ppermute | solution.py:466
  83.0 5.5 %collective-permute-start.13 = (f32[32,256]{1,0:T(8,128)S(1)}, f32[32,256]{1,0:T(8,128)S(1)}, u32[]{:S(2)}, u32[]{:S(2)}) collective-permute-start(f32[32,256]{1,0:T(8,128)S(1)} %folded.2.refs_5_), channel_id=1, source_target_pairs={{0,16},{8,24},{16,0},{24,8},{1,17},{9,25},{17,1},{25,9},{2,18},{10... | collective-permute-start | bytes 98312 | tf_op jit(solution)/shard_map/ppermute | solution.py:466
  83.6 5.8 %collective-permute-start.14 = (f32[32,256]{1,0:T(8,128)S(1)}, f32[32,256]{1,0:T(8,128)S(1)}, u32[]{:S(2)}, u32[]{:S(2)}) collective-permute-start(f32[32,256]{1,0:T(8,128)S(1)} %folded.2.refs_5_), channel_id=1, source_target_pairs={{0,24},{8,0},{16,8},{24,16},{1,25},{9,1},{17,9},{25,17},{2,26},{10... | collective-permute-start | bytes 98312 | tf_op jit(solution)/shard_map/ppermute | solution.py:466
  86.3 3.1 %collective-permute-start.15 = (f32[32,256]{1,0:T(8,128)S(1)}, f32[32,256]{1,0:T(8,128)S(1)}, u32[]{:S(2)}, u32[]{:S(2)}) collective-permute-start(f32[32,256]{1,0:T(8,128)S(1)} %folded.2.refs_5_), channel_id=1, source_target_pairs={{0,4},{4,0},{1,5},{5,1},{2,6},{6,2},{3,7},{7,3},{8,12},{12,8},{9,1... | collective-permute-start | bytes 98312 | tf_op jit(solution)/shard_map/ppermute | solution.py:466
  95.8 5.7 %collective-permute-start.19 = (f32[128,256]{1,0:T(8,128)S(1)}, f32[128,256]{1,0:T(8,128)S(1)}, u32[]{:S(2)}, u32[]{:S(2)}) collective-permute-start(f32[128,256]{1,0:T(8,128)S(1)} %get-tuple-element.50.refs_0_), channel_id=1, source_target_pairs={{0,1},{1,0},{2,3},{3,2},{4,5},{5,4},{6,7},{7,6},{8,9},{9,8},{10,11... | collective-permute-start | bytes 393224 | tf_op jit(solution)/shard_map/ppermute | solution.py:470
  101.5 7.0 %collective-permute-start.20 = (f32[128,256]{1,0:T(8,128)S(1)}, f32[128,256]{1,0:T(8,128)S(1)}, u32[]{:S(2)}, u32[]{:S(2)}) collective-permute-start(f32[128,256]{1,0:T(8,128)S(1)} %summed.5.refs_0_), channel_id=1, source_target_pairs={{0,3},{1,2},{2,1},{3,0},{4,7},{5,6},{6,5},{7,4},{8,11},{9,10},{10,... | collective-permute-start | bytes 393224 | tf_op jit(solution)/shard_map/ppermute | solution.py:470
  103.1 14.4 %all-to-all-start.2 = ((f32[8,16,256]{2,1,0:T(8,128)}), f32[8,16,256]{2,1,0:T(8,128)S(1)}, u32[]{:S(2)}, u32[]{:S(2)}) async-start(f32[8,16,256]{2,1,0:T(8,128)} %get-tuple-element.51), calls=%async_computation.2 | async-start | bytes 262144 | tf_op jit(solution)/shard_map/all_to_all | solution.py:567
  108.5 13.3 %collective-permute-start.21 = (f32[128,256]{1,0:T(8,128)S(1)}, f32[128,256]{1,0:T(8,128)S(1)}, u32[]{:S(2)}, u32[]{:S(2)}) collective-permute-start(f32[128,256]{1,0:T(8,128)S(1)} %summed.6.mine), channel_id=1, source_target_pairs={{0,4},{4,0},{1,5},{5,1},{2,6},{6,2},{3,7},{7,3},{8,12},{12,8},{9,1... | collective-permute-start | bytes 393224 | tf_op jit(solution)/shard_map/ppermute | solution.py:466
  117.6 3.8 %collective-permute-start.22 = (f32[16,256]{1,0:T(8,128)S(1)}, f32[16,256]{1,0:T(8,128)S(1)}, u32[]{:S(2)}, u32[]{:S(2)}) collective-permute-start(f32[16,256]{1,0:T(8,128)S(1)} %folded.3.refs_0_), channel_id=1, source_target_pairs={{0,1},{1,0},{2,3},{3,2},{4,5},{5,4},{6,7},{7,6},{8,9},{9,8},{10,11... | collective-permute-start | bytes 49160 | tf_op jit(solution)/shard_map/ppermute | solution.py:470
  121.4 4.2 %collective-permute-start.23 = (f32[16,256]{1,0:T(8,128)S(1)}, f32[16,256]{1,0:T(8,128)S(1)}, u32[]{:S(2)}, u32[]{:S(2)}) collective-permute-start(f32[16,256]{1,0:T(8,128)S(1)} %summed.7.mine), channel_id=1, source_target_pairs={{0,3},{1,2},{2,1},{3,0},{4,7},{5,6},{6,5},{7,4},{8,11},{9,10},{10,... | collective-permute-start | bytes 49160 | tf_op jit(solution)/shard_map/ppermute | solution.py:470
  (12 other events, 91.5 us)
